TPU v7x, 32 devices: a whole 2x2x4 slice. The times are simulated.
32 devices in a mesh: dp: 16 (over z, y, x), fsdp: 2 (over core).
Axes of the slice: x: 2, y: 2, z: 4, core: 2. Of those that a mesh axis runs over, the one named last changes fastest.
Arguments:
- inputs: float32 [64, 28, 28, 1024], P('dp', 'fsdp'), may hold values from -6 to 6
- cotangent: float32 [64, 28, 28, 1024], P('dp', 'fsdp'), may hold values from -6 to 6
- clip_index: int32 [64], replicated, may hold values from 0 to 9, never falling along the last dimension, each value on 1 to 8 neighbouring positions
- reduce_weight: float32 [2, 1024, 256], P(None, ('dp', 'fsdp')), may hold values from -0.1875 to 0.1875
- mixing_weight: float32 [2, 256, 256], P(None, ('dp', 'fsdp')), may hold values from -0.375 to 0.375
- depthwise: float32 [2, 256, 27], P(None, ('dp', 'fsdp')), may hold values from -1.25 to 1.25
- expand_weight: float32 [2, 256, 1024], P(None, ('dp', 'fsdp')), may hold values from -0.375 to 0.375
- gain_narrow: float32 [2, 256], P(None, ('dp', 'fsdp')), may hold values from 0.1 to 1.9
- bias_narrow: float32 [2, 256], P(None, ('dp', 'fsdp')), may hold values from -3 to 3
- gain_depth: float32 [2, 256], P(None, ('dp', 'fsdp')), may hold values from 0.1 to 1.9
- bias_depth: float32 [2, 256], P(None, ('dp', 'fsdp')), may hold values from -3 to 3
- gain_wide: float32 [2, 1024], P(None, ('dp', 'fsdp')), may hold values from 0.1 to 1.9
- bias_wide: float32 [2, 1024], P(None, ('dp', 'fsdp')), may hold values from -3 to 3
- momentum_reduce_weight: float32 [2, 1024, 256], P(None, ('dp', 'fsdp')), may hold values from -2048 to 2048
- momentum_mixing_weight: float32 [2, 256, 256], P(None, ('dp', 'fsdp')), may hold values from -2048 to 2048
- momentum_depthwise: float32 [2, 256, 27], P(None, ('dp', 'fsdp')), may hold values from -2048 to 2048
- momentum_expand_weight: float32 [2, 256, 1024], P(None, ('dp', 'fsdp')), may hold values from -2048 to 2048
- momentum_gain_narrow: float32 [2, 256], P(None, ('dp', 'fsdp')), may hold values from -2048 to 2048
- momentum_bias_narrow: float32 [2, 256], P(None, ('dp', 'fsdp')), may hold values from -2048 to 2048
- momentum_gain_depth: float32 [2, 256], P(None, ('dp', 'fsdp')), may hold values from -2048 to 2048
- momentum_bias_depth: float32 [2, 256], P(None, ('dp', 'fsdp')), may hold values from -2048 to 2048
- momentum_gain_wide: float32 [2, 1024], P(None, ('dp', 'fsdp')), may hold values from -2048 to 2048
- momentum_bias_wide: float32 [2, 1024], P(None, ('dp', 'fsdp')), may hold values from -2048 to 2048
Outputs:
- block_out: float32 [64, 28, 28, 1024], P('dp', 'fsdp')
- pooled: float32 [10, 1024], replicated
- gradient_inputs: float32 [64, 28, 28, 1024], P('dp', 'fsdp')
- gradient_reduce_weight: float32 [2, 1024, 256], P(None, ('dp', 'fsdp'))
- gradient_mixing_weight: float32 [2, 256, 256], P(None, ('dp', 'fsdp'))
- gradient_depthwise: float32 [2, 256, 27], P(None, ('dp', 'fsdp'))
- gradient_expand_weight: float32 [2, 256, 1024], P(None, ('dp', 'fsdp'))
- gradient_gain_narrow: float32 [2, 256], P(None, ('dp', 'fsdp'))
- gradient_bias_narrow: float32 [2, 256], P(None, ('dp', 'fsdp'))
- gradient_gain_depth: float32 [2, 256], P(None, ('dp', 'fsdp'))
- gradient_bias_depth: float32 [2, 256], P(None, ('dp', 'fsdp'))
- gradient_gain_wide: float32 [2, 1024], P(None, ('dp', 'fsdp'))
- gradient_bias_wide: float32 [2, 1024], P(None, ('dp', 'fsdp'))
- velocity_reduce_weight: float32 [2, 1024, 256], P(None, ('dp', 'fsdp'))
- velocity_mixing_weight: float32 [2, 256, 256], P(None, ('dp', 'fsdp'))
- velocity_depthwise: float32 [2, 256, 27], P(None, ('dp', 'fsdp'))
- velocity_expand_weight: float32 [2, 256, 1024], P(None, ('dp', 'fsdp'))
- velocity_gain_narrow: float32 [2, 256], P(None, ('dp', 'fsdp'))
- velocity_bias_narrow: float32 [2, 256], P(None, ('dp', 'fsdp'))
- velocity_gain_depth: float32 [2, 256], P(None, ('dp', 'fsdp'))
- velocity_bias_depth: float32 [2, 256], P(None, ('dp', 'fsdp'))
- velocity_gain_wide: float32 [2, 1024], P(None, ('dp', 'fsdp'))
- velocity_bias_wide: float32 [2, 1024], P(None, ('dp', 'fsdp'))
- updated_reduce_weight: float32 [2, 1024, 256], P(None, ('dp', 'fsdp'))
- updated_mixing_weight: float32 [2, 256, 256], P(None, ('dp', 'fsdp'))
- updated_depthwise: float32 [2, 256, 27], P(None, ('dp', 'fsdp'))
- updated_expand_weight: float32 [2, 256, 1024], P(None, ('dp', 'fsdp'))
- updated_gain_narrow: float32 [2, 256], P(None, ('dp', 'fsdp'))
- updated_bias_narrow: float32 [2, 256], P(None, ('dp', 'fsdp'))
- updated_gain_depth: float32 [2, 256], P(None, ('dp', 'fsdp'))
- updated_bias_depth: float32 [2, 256], P(None, ('dp', 'fsdp'))
- updated_gain_wide: float32 [2, 1024], P(None, ('dp', 'fsdp'))
- updated_bias_wide: float32 [2, 1024], P(None, ('dp', 'fsdp'))
Inputs may be any that keep to these rules, and one draw needn't show every extreme that they name: `clip_index`: clip numbers never fall along the frames; each of the 10 clips holds 1 to 8 frames, and one holds exactly 8.
All inputs are finite; a program needn't handle non-finite values.
Results may differ from a plain program's by a relative error of at most 0.0085.
Values sent between devices are 32-bit elements; how exact they have to be, the bound alone decides.
No kernel may reach another device: no remote copies, remote signals or barrier semaphores. Data moves between devices by JAX's collectives and lax.ppermute only.
A program may use at most 192 MiB of HBM per device.

v0:
```python
import jax
import jax.numpy as jnp
from jax import lax
from jax.sharding import PartitionSpec as P

EPSILON = 1e-05
MOMENTUM = 0.9
LEARN_RATE = 0.0001
HIGHEST = lax.Precision.HIGHEST


def with_halo(cells, sides, width):
    for axis, dim in sides:
        count = lax.axis_size(axis)
        ends = count - 1
        head = lax.slice_in_dim(cells, 0, width, axis=dim)
        tail = lax.slice_in_dim(cells, cells.shape[dim] - width, cells.shape[dim], axis=dim)
        cells = jnp.concatenate(
            [
                lax.ppermute(tail, axis, [(i, (i + 1) % count) for i in range(ends)]),
                cells,
                lax.ppermute(head, axis, [((i + 1) % count, i) for i in range(ends)]),
            ],
            axis=dim,
        )
    return cells


def matmul(left, right):
    return jnp.dot(left, right, precision=HIGHEST, preferred_element_type=jnp.float32)


def matmul_left_turned(left, right):
    return lax.dot_general(
        left, right, (((0,), (0,)), ((), ())), precision=HIGHEST, preferred_element_type=jnp.float32
    )


def matmul_right_turned(left, right):
    return lax.dot_general(
        left, right, (((1,), (1,)), ((), ())), precision=HIGHEST, preferred_element_type=jnp.float32
    )


def frame_keep(clip_index, first_frame, frames):
    edge = jnp.full((1,), -1, jnp.int32)
    padded = jnp.concatenate([edge, clip_index, edge])
    window = lax.dynamic_slice_in_dim(padded, first_frame, frames + 2)
    centre = window[1:-1]
    before = (window[:-2] == centre).astype(jnp.float32)
    after = (window[2:] == centre).astype(jnp.float32)
    return (jnp.stack([before, jnp.ones(centre.shape, jnp.float32), after]), centre)


def stencil(padded, kernel, keep_mask):
    frames = keep_mask.shape[1]
    rows = padded.shape[1] - 2
    columns = padded.shape[2] - 2
    result = jnp.zeros((frames, rows, columns, padded.shape[3]), jnp.float32)
    for offset_time in range(3):
        partial_sum = jnp.zeros_like(result)
        for offset_row in range(3):
            for offset_col in range(3):
                tap_weight = kernel[:, offset_time * 9 + offset_row * 3 + offset_col]
                partial_sum = (
                    partial_sum
                    + padded[
                        offset_time : offset_time + frames,
                        offset_row : offset_row + rows,
                        offset_col : offset_col + columns,
                        :,
                    ]
                    * tap_weight
                )
        result = result + keep_mask[offset_time][:, None, None, None] * partial_sum
    return result


def kernel_gradient(padded, upstream, keep_mask):
    frames, rows, columns = (upstream.shape[0], upstream.shape[1], upstream.shape[2])
    pieces = []
    for offset_time in range(3):
        weighted = upstream * keep_mask[offset_time][:, None, None, None]
        for offset_row in range(3):
            for offset_col in range(3):
                window = padded[
                    offset_time : offset_time + frames,
                    offset_row : offset_row + rows,
                    offset_col : offset_col + columns,
                    :,
                ]
                pieces.append(jnp.sum(window * weighted, axis=(0, 1, 2)))
    return jnp.stack(pieces, axis=1)


def grow_forward(field):
    grown = with_halo(field, (("dp", 0), ("fsdp", 1)), 1)
    return jnp.pad(grown, ((0, 0), (0, 0), (1, 1), (0, 0)))


def grow_backward(field):
    grown = with_halo(field, (("dp", 0), ("fsdp", 1)), 1)
    return jnp.pad(grown, ((0, 0), (0, 0), (1, 1), (0, 0)))


def gather_forward(
    reduce_part,
    mixing_part,
    depth_part,
    expand_part,
    gain_narrow,
    bias_narrow,
    gain_depth,
    bias_depth,
    gain_wide,
    bias_wide,
):
    return (
        lax.all_gather(reduce_part, ("dp", "fsdp"), axis=0, tiled=True),
        lax.all_gather(mixing_part, ("dp", "fsdp"), axis=0, tiled=True),
        lax.all_gather(depth_part, ("dp", "fsdp"), axis=0, tiled=True),
        lax.all_gather(expand_part, ("dp", "fsdp"), axis=0, tiled=True),
        lax.all_gather(gain_narrow, ("dp", "fsdp"), axis=0, tiled=True),
        lax.all_gather(bias_narrow, ("dp", "fsdp"), axis=0, tiled=True),
        lax.all_gather(gain_depth, ("dp", "fsdp"), axis=0, tiled=True),
        lax.all_gather(bias_depth, ("dp", "fsdp"), axis=0, tiled=True),
        lax.all_gather(gain_wide, ("dp", "fsdp"), axis=0, tiled=True),
        lax.all_gather(bias_wide, ("dp", "fsdp"), axis=0, tiled=True),
    )


def gather_backward(
    reduce_part, mixing_part, depth_part, expand_part, gain_narrow, gain_depth, gain_wide
):
    return (
        lax.all_gather(reduce_part, ("dp", "fsdp"), axis=0, tiled=True),
        lax.all_gather(mixing_part, ("dp", "fsdp"), axis=0, tiled=True),
        lax.all_gather(depth_part, ("dp", "fsdp"), axis=0, tiled=True),
        lax.all_gather(expand_part, ("dp", "fsdp"), axis=0, tiled=True),
        lax.all_gather(gain_narrow, ("dp", "fsdp"), axis=0, tiled=True),
        lax.all_gather(gain_depth, ("dp", "fsdp"), axis=0, tiled=True),
        lax.all_gather(gain_wide, ("dp", "fsdp"), axis=0, tiled=True),
    )


def scatter_gradients(reduce_delta, mixing_delta, depth_delta, expand_delta):
    return (
        lax.psum_scatter(reduce_delta, ("dp", "fsdp"), scatter_dimension=0, tiled=True),
        lax.psum_scatter(mixing_delta, ("dp", "fsdp"), scatter_dimension=0, tiled=True),
        lax.psum_scatter(depth_delta, ("dp", "fsdp"), scatter_dimension=0, tiled=True),
        lax.psum_scatter(expand_delta, ("dp", "fsdp"), scatter_dimension=0, tiled=True),
    )


def batch_moments(values, voxel_count):
    totals = lax.psum(jnp.sum(values, axis=0), ("dp", "fsdp"))
    average = totals / voxel_count
    centred = values - average
    variance = lax.psum(jnp.sum(centred * centred, axis=0), ("dp", "fsdp")) / voxel_count
    inverse = lax.rsqrt(variance + EPSILON)
    return ((values - average) * inverse, inverse)


def norm_backward(upstream, normed, gain_full, inverse, voxel_count):
    gain_delta, bias_delta = lax.psum(
        (jnp.sum(upstream * normed, axis=0), jnp.sum(upstream, axis=0)), ("dp", "fsdp")
    )
    delta = (
        gain_full
        * inverse
        * (upstream - bias_delta / voxel_count - normed * gain_delta / voxel_count)
    )
    return (delta, gain_delta, bias_delta)


def forward_block(flat_in, weights, keep_mask, grid_shape, voxel_count):
    (
        reduce_full,
        mixing_full,
        depth_full,
        expand_full,
        gain_narrow,
        bias_narrow,
        gain_depth,
        bias_depth,
        gain_wide,
        bias_wide,
    ) = weights
    frames, rows, columns = grid_shape
    narrow_act = matmul(flat_in, reduce_full)
    normed_first, inverse_first = batch_moments(narrow_act, voxel_count)
    before_first = gain_narrow * normed_first + bias_narrow
    relu_first = jnp.maximum(before_first, 0.0)
    mixed = matmul(relu_first, mixing_full)
    padded_mixed = grow_forward(mixed.reshape(frames, rows, columns, mixed.shape[1]))
    depth_act = stencil(padded_mixed, depth_full, keep_mask).reshape(mixed.shape)
    normed_second, inverse_second = batch_moments(depth_act, voxel_count)
    before_second = gain_depth * normed_second + bias_depth
    relu_second = jnp.maximum(before_second, 0.0)
    expanded = matmul(relu_second, expand_full)
    normed_third, inverse_third = batch_moments(expanded, voxel_count)
    summed = gain_wide * normed_third + bias_wide + flat_in
    output = jnp.maximum(summed, 0.0)
    stored = (
        flat_in,
        normed_first,
        inverse_first,
        before_first,
        relu_first,
        padded_mixed,
        normed_second,
        inverse_second,
        before_second,
        relu_second,
        normed_third,
        inverse_third,
        summed,
    )
    return (output, stored)


def backward_block(upstream, weights, stored, keep_mask, voxel_count):
    reduce_full, mixing_full, depth_full, expand_full, gain_narrow, gain_depth, gain_wide = weights
    (
        flat_in,
        normed_first,
        inverse_first,
        before_first,
        relu_first,
        padded_mixed,
        normed_second,
        inverse_second,
        before_second,
        relu_second,
        normed_third,
        inverse_third,
        summed,
    ) = stored
    frames = keep_mask.shape[1]
    rows = padded_mixed.shape[1] - 2
    columns = padded_mixed.shape[2] - 2
    delta_summed = jnp.where(summed > 0.0, upstream, 0.0)
    delta_expanded, gain_wide_delta, bias_wide_delta = norm_backward(
        delta_summed, normed_third, gain_wide, inverse_third, voxel_count
    )
    expand_delta = matmul_left_turned(relu_second, delta_expanded)
    delta_second = jnp.where(
        before_second > 0.0, matmul_right_turned(delta_expanded, expand_full), 0.0
    )
    delta_depth, gain_depth_delta, bias_depth_delta = norm_backward(
        delta_second, normed_second, gain_depth, inverse_second, voxel_count
    )
    grid_delta = delta_depth.reshape(frames, rows, columns, delta_depth.shape[1])
    padded_delta = grow_backward(grid_delta)
    delta_mixed = stencil(padded_delta, depth_full[:, ::-1], keep_mask).reshape(delta_depth.shape)
    depth_delta = kernel_gradient(padded_mixed, grid_delta, keep_mask)
    mixing_delta = matmul_left_turned(relu_first, delta_mixed)
    delta_first = jnp.where(before_first > 0.0, matmul_right_turned(delta_mixed, mixing_full), 0.0)
    delta_narrow, gain_narrow_delta, bias_narrow_delta = norm_backward(
        delta_first, normed_first, gain_narrow, inverse_first, voxel_count
    )
    reduce_delta = matmul_left_turned(flat_in, delta_narrow)
    delta_input = matmul_right_turned(delta_narrow, reduce_full) + delta_summed
    owned = scatter_gradients(reduce_delta, mixing_delta, depth_delta, expand_delta)
    norm_deltas = (
        gain_narrow_delta,
        bias_narrow_delta,
        gain_depth_delta,
        bias_depth_delta,
        gain_wide_delta,
        bias_wide_delta,
    )
    return (delta_input, owned, norm_deltas)


def owned_slice(full, devices, position):
    share = full.shape[0] // devices
    return lax.dynamic_slice_in_dim(full, position * share, share)


def body(
    inputs,
    cotangent,
    clip_index,
    reduce_weight,
    mixing_weight,
    depthwise,
    expand_weight,
    gain_narrow,
    bias_narrow,
    gain_depth,
    bias_depth,
    gain_wide,
    bias_wide,
    momentum_reduce_weight,
    momentum_mixing_weight,
    momentum_depthwise,
    momentum_expand_weight,
    momentum_gain_narrow,
    momentum_bias_narrow,
    momentum_gain_depth,
    momentum_bias_depth,
    momentum_gain_wide,
    momentum_bias_wide,
):
    frames, rows, columns, channels = inputs.shape
    voxels = frames * rows * columns
    devices = lax.axis_size(("dp", "fsdp"))
    rank = lax.axis_index(("dp", "fsdp"))
    voxel_count = float(voxels * lax.axis_size("dp") * lax.axis_size("fsdp"))
    keep_mask, centre = frame_keep(clip_index, lax.axis_index("dp") * frames, frames)
    params = (
        reduce_weight,
        mixing_weight,
        depthwise,
        expand_weight,
        gain_narrow,
        bias_narrow,
        gain_depth,
        bias_depth,
        gain_wide,
        bias_wide,
    )
    momenta = (
        momentum_reduce_weight,
        momentum_mixing_weight,
        momentum_depthwise,
        momentum_expand_weight,
        momentum_gain_narrow,
        momentum_bias_narrow,
        momentum_gain_depth,
        momentum_bias_depth,
        momentum_gain_wide,
        momentum_bias_wide,
    )
    current = inputs.reshape(voxels, channels)
    saved = []
    gathered = []
    for position in range(2):
        weights = gather_forward(
            reduce_weight[position],
            mixing_weight[position],
            depthwise[position],
            expand_weight[position],
            gain_narrow[position],
            bias_narrow[position],
            gain_depth[position],
            bias_depth[position],
            gain_wide[position],
            bias_wide[position],
        )
        current, stored = forward_block(
            current, weights, keep_mask, (frames, rows, columns), voxel_count
        )
        saved.append(stored)
        gathered.append(weights)
    output_grid = current.reshape(frames, rows, columns, channels)
    clips = clip_index.shape[0] // 6
    labels = jnp.arange(clips, dtype=jnp.int32)
    frame_sums = jnp.sum(output_grid, axis=(1, 2))
    local_hot = (centre[None, :] == labels[:, None]).astype(jnp.float32)
    pooled_sums = lax.psum(matmul(local_hot, frame_sums), ("dp", "fsdp"))
    counts = jnp.sum((clip_index[None, :] == labels[:, None]).astype(jnp.float32), axis=1) * float(
        rows * lax.axis_size("fsdp") * columns
    )
    pooled = pooled_sums / counts[:, None]
    upstream = cotangent.reshape(voxels, channels)
    owned_blocks = [None, None]
    norm_blocks = [None, None]
    for position in (1, 0):
        weights = gather_backward(
            reduce_weight[position],
            mixing_weight[position],
            depthwise[position],
            expand_weight[position],
            gain_narrow[position],
            gain_depth[position],
            gain_wide[position],
        )
        upstream, owned, norm_deltas = backward_block(
            upstream, weights, saved[position], keep_mask, voxel_count
        )
        owned_blocks[position] = owned
        norm_blocks[position] = tuple((owned_slice(item, devices, rank) for item in norm_deltas))
    gradient_inputs = upstream.reshape(frames, rows, columns, channels)
    deltas = []
    for index in range(4):
        deltas.append(jnp.stack([owned_blocks[0][index], owned_blocks[1][index]]))
    for index in range(6):
        deltas.append(jnp.stack([norm_blocks[0][index], norm_blocks[1][index]]))
    velocity = [MOMENTUM * momenta[index] + deltas[index] for index in range(10)]
    updated = [
        params[index] - LEARN_RATE * (deltas[index] + MOMENTUM * velocity[index])
        for index in range(10)
    ]
    return (
        output_grid,
        pooled,
        gradient_inputs,
        deltas[0],
        deltas[1],
        deltas[2],
        deltas[3],
        deltas[4],
        deltas[5],
        deltas[6],
        deltas[7],
        deltas[8],
        deltas[9],
        velocity[0],
        velocity[1],
        velocity[2],
        velocity[3],
        velocity[4],
        velocity[5],
        velocity[6],
        velocity[7],
        velocity[8],
        velocity[9],
        updated[0],
        updated[1],
        updated[2],
        updated[3],
        updated[4],
        updated[5],
        updated[6],
        updated[7],
        updated[8],
        updated[9],
    )


def solution(mesh):
    placed = (
        P("dp", "fsdp", None, None),
        P("dp", "fsdp", None, None),
        P(),
        P(None, ("dp", "fsdp"), None),
        P(None, ("dp", "fsdp"), None),
        P(None, ("dp", "fsdp"), None),
        P(None, ("dp", "fsdp"), None),
        P(None, ("dp", "fsdp")),
        P(None, ("dp", "fsdp")),
        P(None, ("dp", "fsdp")),
        P(None, ("dp", "fsdp")),
        P(None, ("dp", "fsdp")),
        P(None, ("dp", "fsdp")),
        P(None, ("dp", "fsdp"), None),
        P(None, ("dp", "fsdp"), None),
        P(None, ("dp", "fsdp"), None),
        P(None, ("dp", "fsdp"), None),
        P(None, ("dp", "fsdp")),
        P(None, ("dp", "fsdp")),
        P(None, ("dp", "fsdp")),
        P(None, ("dp", "fsdp")),
        P(None, ("dp", "fsdp")),
        P(None, ("dp", "fsdp")),
    )
    return jax.shard_map(
        body,
        mesh=mesh,
        in_specs=placed,
        out_specs=(
            P("dp", "fsdp", None, None),
            P(),
            P("dp", "fsdp", None, None),
            P(None, ("dp", "fsdp"), None),
            P(None, ("dp", "fsdp"), None),
            P(None, ("dp", "fsdp"), None),
            P(None, ("dp", "fsdp"), None),
            P(None, ("dp", "fsdp")),
            P(None, ("dp", "fsdp")),
            P(None, ("dp", "fsdp")),
            P(None, ("dp", "fsdp")),
            P(None, ("dp", "fsdp")),
            P(None, ("dp", "fsdp")),
            P(None, ("dp", "fsdp"), None),
            P(None, ("dp", "fsdp"), None),
            P(None, ("dp", "fsdp"), None),
            P(None, ("dp", "fsdp"), None),
            P(None, ("dp", "fsdp")),
            P(None, ("dp", "fsdp")),
            P(None, ("dp", "fsdp")),
            P(None, ("dp", "fsdp")),
            P(None, ("dp", "fsdp")),
            P(None, ("dp", "fsdp")),
            P(None, ("dp", "fsdp"), None),
            P(None, ("dp", "fsdp"), None),
            P(None, ("dp", "fsdp"), None),
            P(None, ("dp", "fsdp"), None),
            P(None, ("dp", "fsdp")),
            P(None, ("dp", "fsdp")),
            P(None, ("dp", "fsdp")),
            P(None, ("dp", "fsdp")),
            P(None, ("dp", "fsdp")),
            P(None, ("dp", "fsdp")),
        ),
        check_vma=False,
    )
```

profile of v0, /device:TPU:0, one launch (start us, length us, event | category | flops | bytes accessed | tf_op | source)
XLA Modules:
  0.0 2198.7 jit_solution(8986479500426817963)
XLA Ops:
  20.6 44.1 %all-gather.8 = f32[1,256,256]{2,1,0:T(8,128)S(1)} all-gather(f32[1,8,256]{2,1,0:T(8,128)S(1)} %get-tuple-element.401), channel_id=10, replica_groups=mesh['dp'=16,'fsdp'=2] {'dp','fsdp'}, dimensions={1}, use_global_device_ids=true | all-gather | bytes 270336 | tf_op jit(solution)/shard_map/all_gather | solution.py:120
  64.7 9.6 copy.90
  89.3 37.0 %psum.175 = f32[256]{0:T(256)S(1)} all-reduce(f32[256]{0:T(256)S(1)} %get-tuple-element.418), channel_id=1, replica_groups=mesh['dp'=16,'fsdp'=2] {'dp','fsdp'}, use_global_device_ids=true, to_apply=%region_1.0 | all-reduce | flops 256 | bytes 2048 | tf_op jit(solution)/shard_map/psum | solution.py:156
  126.6 41.5 %all-reduce.29 = (f32[256]{0:T(256)S(1)}, f32[256]{0:T(256)S(1)}, f32[256]{0:T(256)S(1)}) all-reduce(f32[256]{0:T(256)S(1)} %bitcast_dynamic-update-slice_fusion.5, f32[256]{0:T(256)S(1)} %bitcast_dynamic-update-slice_fusion.6, f32[256]{0:T(256)S(1)} %multiply_reduce_fusion.65), channel_id=9, replica_groups=mesh['dp'=16,'fsdp'=2] {'dp','fsdp'}, use_global_device_ids=true, to_apply=%add.10 | all-reduce | flops 768 | bytes 6144
  175.8 41.2 %all-gather.9 = f32[1,256,27]{2,1,0:T(8,128)S(1)} all-gather(f32[1,8,27]{2,1,0:T(8,128)S(1)} %get-tuple-element.403), channel_id=11, replica_groups=mesh['dp'=16,'fsdp'=2] {'dp','fsdp'}, dimensions={1}, use_global_device_ids=true | all-gather | bytes 28512 | tf_op jit(solution)/shard_map/all_gather | solution.py:121
  223.9 11.4 collective-permute-done.1
  238.3 38.4 %all-gather.15 = f32[1,256,256]{2,1,0:T(8,128)S(1)} all-gather(f32[1,8,256]{2,1,0:T(8,128)S(1)} %get-tuple-element.400), channel_id=17, replica_groups=mesh['dp'=16,'fsdp'=2] {'dp','fsdp'}, dimensions={1}, use_global_device_ids=true | all-gather | bytes 270336 | tf_op jit(solution)/shard_map/all_gather | solution.py:120
  276.7 37.2 %all-gather.16 = f32[1,256,27]{2,1,0:T(8,128)S(1)} all-gather(f32[1,8,27]{2,1,0:T(8,128)S(1)} %copy-done.90), channel_id=18, replica_groups=mesh['dp'=16,'fsdp'=2] {'dp','fsdp'}, dimensions={1}, use_global_device_ids=true | all-gather | bytes 28512 | tf_op jit(solution)/shard_map/all_gather | solution.py:121
  325.9 37.1 %psum.177 = f32[256]{0:T(256)S(1)} all-reduce(f32[256]{0:T(256)} %get-tuple-element.377), channel_id=1, replica_groups=mesh['dp'=16,'fsdp'=2] {'dp','fsdp'}, use_global_device_ids=true, to_apply=%region_5.6 | all-reduce | flops 256 | bytes 2048 | tf_op jit(solution)/shard_map/psum | solution.py:156
  367.4 42.8 %all-reduce.28 = (f32[256]{0:T(256)}, f32[256]{0:T(256)S(1)}, f32[256]{0:T(256)}) all-reduce(f32[256]{0:T(256)} %copy-done.238, f32[256]{0:T(256)} %copy-done.241, f32[256]{0:T(256)S(1)} %multiply_reduce_fusion.57), channel_id=12, replica_groups=mesh['dp'=16,'fsdp'=2] {'dp','fsdp'}, use_global_device_ids=true, to_apply=%add.11 | all-reduce | flops 768 | bytes 6144
  411.5 9.4 fusion.211
  420.9 39.0 %psum.179 = f32[1024]{0:T(1024)S(1)} all-reduce(f32[1024]{0:T(1024)} %get-tuple-element.420), channel_id=1, replica_groups=mesh['dp'=16,'fsdp'=2] {'dp','fsdp'}, use_global_device_ids=true, to_apply=%region_9.10 | all-reduce | flops 1024 | bytes 8192 | tf_op jit(solution)/shard_map/psum | solution.py:156
  463.5 41.9 %all-reduce.27 = (f32[1024]{0:T(1024)}, f32[1024]{0:T(1024)}, f32[1024]{0:T(1024)}) all-reduce(f32[1024]{0:T(1024)} %copy-done.89, f32[1024]{0:T(1024)S(1)} %copy-done.88, f32[1024]{0:T(1024)S(1)} %multiply_reduce_fusion.3), channel_id=14, replica_groups=mesh['dp'=16,'fsdp'=2] {'dp','fsdp'}, use_global_device_ids=true, to_apply=%add.12 | all-reduce | flops 3072 | bytes 24576
  506.7 9.0 add_add_fusion.1
  524.2 38.9 %psum.181 = f32[256]{0:T(256)} all-reduce(f32[256]{0:T(256)S(1)} %get-tuple-element.422), channel_id=1, replica_groups=mesh['dp'=16,'fsdp'=2] {'dp','fsdp'}, use_global_device_ids=true, to_apply=%region_13.14 | all-reduce | flops 256 | bytes 2048 | tf_op jit(solution)/shard_map/psum | solution.py:156
  565.9 42.5 %all-reduce.26 = (f32[256]{0:T(256)}, f32[256]{0:T(256)}, f32[256]{0:T(256)}) all-reduce(f32[256]{0:T(256)} %copy-done.240, f32[256]{0:T(256)} %copy-done.239, f32[256]{0:T(256)} %multiply_reduce_fusion.64), channel_id=16, replica_groups=mesh['dp'=16,'fsdp'=2] {'dp','fsdp'}, use_global_device_ids=true, to_apply=%add.13 | all-reduce | flops 768 | bytes 6144
  650.6 9.5 copy.91
  672.3 9.5 fusion.196
  684.4 39.9 %psum.183 = f32[256]{0:T(256)S(1)} all-reduce(f32[256]{0:T(256)S(1)} %get-tuple-element.375), channel_id=1, replica_groups=mesh['dp'=16,'fsdp'=2] {'dp','fsdp'}, use_global_device_ids=true, to_apply=%region_17.18 | all-reduce | flops 256 | bytes 2048 | tf_op jit(solution)/shard_map/psum | solution.py:156
  726.0 40.5 %all-reduce.25 = (f32[256]{0:T(256)S(1)}, f32[256]{0:T(256)S(1)}, f32[256]{0:T(256)S(1)}) all-reduce(f32[256]{0:T(256)S(1)} %copy-done.237, f32[256]{0:T(256)S(1)} %copy-done.235, f32[256]{0:T(256)S(1)} %multiply_reduce_fusion.56), channel_id=19, replica_groups=mesh['dp'=16,'fsdp'=2] {'dp','fsdp'}, use_global_device_ids=true, to_apply=%add.14 | all-reduce | flops 768 | bytes 6144
  775.4 39.7 %psum.185 = f32[1024]{0:T(1024)S(1)} all-reduce(f32[1024]{0:T(1024)S(1)} %get-tuple-element.424), channel_id=1, replica_groups=mesh['dp'=16,'fsdp'=2] {'dp','fsdp'}, use_global_device_ids=true, to_apply=%region_21.22 | all-reduce | flops 1024 | bytes 8192 | tf_op jit(solution)/shard_map/psum | solution.py:156
  818.6 40.8 %all-reduce.24 = (f32[1024]{0:T(1024)S(1)}, f32[1024]{0:T(1024)S(1)}, f32[1024]{0:T(1024)S(1)}) all-reduce(f32[1024]{0:T(1024)} %bitcast_dynamic-update-slice_fusion, f32[1024]{0:T(1024)S(1)} %multiply_reduce_fusion.2, f32[1024]{0:T(1024)} %bitcast_dynamic-update-slice_fusion.11), channel_id=21, replica_groups=mesh['dp'=16,'fsdp'=2] {'dp','fsdp'}, use_global_device_ids=true, to_apply=%add.15 | all-reduce | flops 3072 | bytes 24576
  859.4 11.4 fusion.191
  870.7 39.7 %all-reduce.23 = (f32[1024]{0:T(1024)S(1)}, f32[1024]{0:T(1024)S(1)}) all-reduce(f32[1024]{0:T(1024)S(1)} %get-tuple-element.168, f32[1024]{0:T(1024)S(1)} %get-tuple-element.167), channel_id=1, replica_groups=mesh['dp'=16,'fsdp'=2] {'dp','fsdp'}, use_global_device_ids=true, to_apply=%region_30.31 | all-reduce | flops 2048 | bytes 16384 | tf_op jit(solution)/shard_map/psum | solution.py:165
  910.5 12.9 fusion.195
  923.4 40.6 %all-reduce.22 = (f32[256]{0:T(256)S(1)}, f32[256]{0:T(256)S(1)}) all-reduce(f32[256]{0:T(256)S(1)} %get-tuple-element.246, f32[256]{0:T(256)S(1)} %get-tuple-element.245), channel_id=1, replica_groups=mesh['dp'=16,'fsdp'=2] {'dp','fsdp'}, use_global_device_ids=true, to_apply=%region_34.35 | all-reduce | flops 512 | bytes 4096 | tf_op jit(solution)/shard_map/psum | solution.py:165
  974.1 11.8 multiply_reduce_fusion.4
  1022.4 9.1 fusion.39
  1038.9 40.6 %all-reduce.21 = (f32[256]{0:T(256)S(1)}, f32[256]{0:T(256)S(1)}) all-reduce(f32[256]{0:T(256)S(1)} %get-tuple-element.244, f32[256]{0:T(256)S(1)} %get-tuple-element.243), channel_id=1, replica_groups=mesh['dp'=16,'fsdp'=2] {'dp','fsdp'}, use_global_device_ids=true, to_apply=%region_38.39 | all-reduce | flops 512 | bytes 4096 | tf_op jit(solution)/shard_map/psum | solution.py:165
  1080.1 14.7 fusion.190
  1094.9 40.4 %all-reduce.20 = (f32[1024]{0:T(1024)S(1)}, f32[1024]{0:T(1024)S(1)}) all-reduce(f32[1024]{0:T(1024)S(1)} %get-tuple-element.166, f32[1024]{0:T(1024)S(1)} %get-tuple-element.165), channel_id=1, replica_groups=mesh['dp'=16,'fsdp'=2] {'dp','fsdp'}, use_global_device_ids=true, to_apply=%region_42.43 | all-reduce | flops 2048 | bytes 16384 | tf_op jit(solution)/shard_map/psum | solution.py:165
  1135.3 12.9 fusion.193
  1148.2 39.9 %all-reduce.19 = (f32[256]{0:T(256)S(1)}, f32[256]{0:T(256)S(1)}) all-reduce(f32[256]{0:T(256)S(1)} %get-tuple-element.242, f32[256]{0:T(256)S(1)} %get-tuple-element.241), channel_id=1, replica_groups=mesh['dp'=16,'fsdp'=2] {'dp','fsdp'}, use_global_device_ids=true, to_apply=%region_46.47 | all-reduce | flops 512 | bytes 4096 | tf_op jit(solution)/shard_map/psum | solution.py:165
  1217.6 12.0 collective-permute-done.12
  1276.6 14.7 fusion
  1291.5 12.6 fusion.95
  1304.6 10.2 copy.97
  1315.8 12.3 fusion.103
  1331.4 56.7 %all-reduce.32.cloned.1.call-done = (f32[10,1024]{1,0:T(8,128)}, f32[256]{0:T(256)}, f32[256]{0:T(256)}, f32[256,27]{0,1:T(8,128)}, f32[256,27]{0,1:T(8,128)}) async-done(((f32[10,1024]{1,0:T(8,128)}, f32[256]{0:T(256)}, f32[256]{0:T(256)}, f32[256,27]{0,1:T(8,128)}, f32[256,27]{0,1:T(8,128)}), (f32[10,1024]{1,0:T(8,128)}, f32[256]{0:T(256)}, f32[256]{0:T(256)}, f32[256,27]{0,1:T(8,128)}, ...) | async-done | bytes 98320 | tf_op jit(solution)/shard_map/psum | solution.py:362
  1388.8 10.0 convolution_bitcast_fusion
  1401.8 9.6 convolution_add_fusion
  1418.8 10.2 copy.98
  1431.6 95.0 %reduce-scatter.15.cloned.1.call-done = f32[8,256]{1,0:T(8,128)} async-done(((f32[256,256]{1,0:T(8,128)}), f32[8,256]{1,0:T(8,128)}) %reduce-scatter.15.cloned.1.call-update) | async-done | bytes 8208 | tf_op jit(solution)/shard_map/reduce_scatter | solution.py:149
  1526.5 131.7 %reduce-scatter.13.cloned.1.call-done = f32[8,256]{1,0:T(8,128)} async-done(((f32[256,256]{1,0:T(8,128)}), f32[8,256]{1,0:T(8,128)}) %reduce-scatter.13.cloned.1.call-update) | async-done | bytes 8208 | tf_op jit(solution)/shard_map/reduce_scatter | solution.py:149
  1659.6 131.7 %reduce-scatter.23.cloned.1.call-done = f32[32,256]{1,0:T(8,128)} async-done(((f32[1024,256]{1,0:T(8,128)}), f32[32,256]{1,0:T(8,128)}) %reduce-scatter.23.cloned.1.call-update) | async-done | bytes 32784
  1792.2 132.1 %reduce-scatter.19.cloned.1.call-done = f32[8,1024]{1,0:T(8,128)} async-done(((f32[256,1024]{1,0:T(8,128)}), f32[8,1024]{1,0:T(8,128)}) %reduce-scatter.19.cloned.1.call-update) | async-done | bytes 32784 | tf_op jit(solution)/shard_map/reduce_scatter | solution.py:151
  1924.3 132.9 %reduce-scatter.17.cloned.1.call-done = f32[8,1024]{1,0:T(8,128)} async-done(((f32[256,1024]{1,0:T(8,128)}), f32[8,1024]{1,0:T(8,128)}) %reduce-scatter.17.cloned.1.call-update) | async-done | bytes 32784 | tf_op jit(solution)/shard_map/reduce_scatter | solution.py:151
  2058.7 131.7 %reduce-scatter.21.cloned.1.call-done = f32[32,256]{1,0:T(8,128)} async-done(((f32[1024,256]{1,0:T(8,128)}), f32[32,256]{1,0:T(8,128)}) %reduce-scatter.21.cloned.1.call-update) | async-done | bytes 32784
  (724 shorter events, 303.2 us)
Async XLA Ops:
  7.2 74.5 %all-gather.25.cloned.1.call-start = ((), (), s32[]{:S(2)}) async-start(), calls=%async_computation.10 | async-start | bytes 1081344 | tf_op jit(solution)/shard_map/all_gather | solution.py:119
  8.7 402.8 %all-gather.27.cloned.1.call-start = ((), (), s32[]{:S(2)}) async-start(), calls=%async_computation.11 | async-start | bytes 1081344 | tf_op jit(solution)/shard_map/all_gather | solution.py:122
  10.2 505.5 %all-gather.29.cloned.1.call-start = ((), (), s32[]{:S(2)}) async-start(), calls=%async_computation.12 | async-start | bytes 1081344 | tf_op jit(solution)/shard_map/all_gather | solution.py:119
  10.9 755.7 %all-gather.31.cloned.1.call-start = ((), (), s32[]{:S(2)}) async-start(), calls=%async_computation.13 | async-start | bytes 1081344 | tf_op jit(solution)/shard_map/all_gather | solution.py:122
  11.5 1376.7 %all-reduce.32.cloned.1.call-start = ((), (), s32[]{:S(2)}) async-start(), calls=%async_computation.16 | async-start | bytes 266240 | tf_op jit(solution)/shard_map/psum | solution.py:362
  12.4 303.8 %copy-start.65 = (f32[4]{0:T(128)}, f32[4]{0:T(128)S(1)}, u32[]{:S(2)}) copy-start(f32[4]{0:T(128)S(1)} %get-tuple-element.416) | copy-start | bytes 52
  12.4 659.2 %copy-start.51 = (f32[4]{0:T(128)}, f32[4]{0:T(128)S(1)}, u32[]{:S(2)}) copy-start(f32[4]{0:T(128)S(1)} %get-tuple-element.417) | copy-start | bytes 52
  16.3 58.1 %copy-start.240 = (f32[256]{0:T(256)}, f32[256]{0:T(256)S(1)}, u32[]{:S(2)}) copy-start(f32[256]{0:T(256)S(1)} %bitcast_dynamic-update-slice_fusion.2) | copy-start | bytes 3076
  64.7 103.9 %copy-start.27 = (f32[1,256,256]{2,1,0:T(8,128)}, f32[1,256,256]{2,1,0:T(8,128)S(1)}, u32[]{:S(2)}) copy-start(f32[1,256,256]{2,1,0:T(8,128)S(1)} %all-gather.8) | copy-start | bytes 786436
  89.3 80.9 %copy-start.1 = (f32[1568,256]{1,0:T(8,128)}, f32[1568,256]{1,0:T(8,128)S(1)}, u32[]{:S(2)}) copy-start(f32[1568,256]{1,0:T(8,128)S(1)} %get-tuple-element.419) | copy-start | bytes 4816900
  171.5 51.0 %collective-permute-start = (f32[1,14,28,256]{3,2,1,0:T(8,128)S(1)}, f32[1,14,28,256]{3,2,1,0:T(8,128)S(1)}, u32[]{:S(2)}, u32[]{:S(2)}) collective-permute-start(f32[1,14,28,256]{3,2,1,0:T(8,128)S(1)} %slice.887), channel_id=1, source_target_pairs={{0,2},{2,4},{4,6},{6,8},{8,10},{10,12},{12,14},{14,16},{16,18},{18... | collective-permute-start | bytes 1204232 | tf_op jit(solution)/shard_map/ppermute | solution.py:20
  218.5 16.8 collective-permute-start.1
  235.3 80.0 %copy-start.24 = (f32[1,14,28,256]{3,2,1,0:T(8,128)}, f32[1,14,28,256]{3,2,1,0:T(8,128)S(1)}, u32[]{:S(2)}) copy-start(f32[1,14,28,256]{3,2,1,0:T(8,128)S(1)} %collective-permute-done.1) | copy-start | bytes 1204228
  235.4 80.9 %copy-start.8 = (f32[6,14,28,256]{3,2,1,0:T(8,128)}, f32[6,14,28,256]{3,2,1,0:T(8,128)S(1)}, u32[]{:S(2)}) copy-start(f32[6,14,28,256]{3,2,1,0:T(8,128)S(1)} %constant_dynamic-update-slice_fusion) | copy-start | bytes 7225348
  235.4 80.2 %collective-permute-start.2 = (f32[6,1,28,256]{3,2,1,0:T(8,128)S(1)}, f32[6,1,28,256]{3,2,1,0:T(8,128)S(1)}, u32[]{:S(2)}, u32[]{:S(2)}) collective-permute-start(f32[6,1,28,256]{3,2,1,0:T(8,128)S(1)} %get-tuple-element.386), channel_id=1, source_target_pairs={{0,1},{2,3},{4,5},{6,7},{8,9},{10,11},{12,13},{14,15},{16,17},{18,... | collective-permute-start | bytes 516104 | tf_op jit(solution)/shard_map/ppermute | solution.py:20
  237.0 78.7 %collective-permute-start.3 = (f32[6,1,28,256]{3,2,1,0:T(8,128)S(1)}, f32[6,1,28,256]{3,2,1,0:T(8,128)S(1)}, u32[]{:S(2)}, u32[]{:S(2)}) collective-permute-start(f32[6,1,28,256]{3,2,1,0:T(8,128)S(1)} %get-tuple-element.387), channel_id=1, source_target_pairs={{1,0},{3,2},{5,4},{7,6},{9,8},{11,10},{13,12},{15,14},{17,16},{19,... | collective-permute-start | bytes 516104 | tf_op jit(solution)/shard_map/ppermute | solution.py:22
  506.7 628.6 %copy-start.45 = (f32[1024]{0:T(1024)}, f32[1024]{0:T(1024)S(1)}, u32[]{:S(2)}) copy-start(f32[1024]{0:T(1024)S(1)} %get-tuple-element.405) | copy-start | bytes 12292
  563.7 516.3 %copy-start.47 = (f32[256]{0:T(256)}, f32[256]{0:T(256)S(1)}, u32[]{:S(2)}) copy-start(f32[256]{0:T(256)S(1)} %broadcast_multiply_fusion.9) | copy-start | bytes 3076
  616.6 22.7 %collective-permute-start.4 = (f32[1,14,28,256]{3,2,1,0:T(8,128)}, f32[1,14,28,256]{3,2,1,0:T(8,128)}, u32[]{:S(2)}, u32[]{:S(2)}) collective-permute-start(f32[1,14,28,256]{3,2,1,0:T(8,128)} %slice.954), channel_id=1, source_target_pairs={{0,2},{2,4},{4,6},{6,8},{8,10},{10,12},{12,14},{14,16},{16,18},{18... | collective-permute-start | bytes 1204232 | tf_op jit(solution)/shard_map/ppermute | solution.py:20
  625.3 16.7 collective-permute-start.5
  645.4 23.6 %collective-permute-start.6 = (f32[6,1,28,256]{3,2,1,0:T(8,128)}, f32[6,1,28,256]{3,2,1,0:T(8,128)}, u32[]{:S(2)}, u32[]{:S(2)}) collective-permute-start(f32[6,1,28,256]{3,2,1,0:T(8,128)} %get-tuple-element.384), channel_id=1, source_target_pairs={{0,1},{2,3},{4,5},{6,7},{8,9},{10,11},{12,13},{14,15},{16,17},{18,... | collective-permute-start | bytes 516104 | tf_op jit(solution)/shard_map/ppermute | solution.py:20
  647.4 21.7 collective-permute-start.7
  724.3 239.8 %copy-start.57 = (f32[256]{0:T(256)}, f32[256]{0:T(256)S(1)}, u32[]{:S(2)}) copy-start(f32[256]{0:T(256)S(1)} %broadcast_multiply_fusion.8) | copy-start | bytes 3076
  766.6 143.9 %copy-start.77 = (f32[256]{0:T(256)}, f32[256]{0:T(256)S(1)}, u32[]{:S(2)}) copy-start(f32[256]{0:T(256)S(1)} %get-tuple-element.326) | copy-start | bytes 3076
  766.6 143.9 %copy-start.199 = (f32[256]{0:T(256)}, f32[256]{0:T(256)S(1)}, u32[]{:S(2)}) copy-start(f32[256]{0:T(256)S(1)} %get-tuple-element.325) | copy-start | bytes 3076
  766.6 197.5 %copy-start.71 = (f32[256]{0:T(256)}, f32[256]{0:T(256)S(1)}, u32[]{:S(2)}) copy-start(f32[256]{0:T(256)S(1)} %get-tuple-element.415) | copy-start | bytes 3076
  987.7 25.3 %collective-permute-start.8 = (f32[1,14,28,256]{3,2,1,0:T(8,128)}, f32[1,14,28,256]{3,2,1,0:T(8,128)}, u32[]{:S(2)}, u32[]{:S(2)}) collective-permute-start(f32[1,14,28,256]{3,2,1,0:T(8,128)} %slice.1017), channel_id=1, source_target_pairs={{0,2},{2,4},{4,6},{6,8},{8,10},{10,12},{12,14},{14,16},{16,18},{18... | collective-permute-start | bytes 1204232 | tf_op jit(solution)/shard_map/ppermute | solution.py:20
  992.7 23.0 %collective-permute-start.9 = (f32[1,14,28,256]{3,2,1,0:T(8,128)}, f32[1,14,28,256]{3,2,1,0:T(8,128)}, u32[]{:S(2)}, u32[]{:S(2)}) collective-permute-start(f32[1,14,28,256]{3,2,1,0:T(8,128)} %slice.1019), channel_id=1, source_target_pairs={{2,0},{4,2},{6,4},{8,6},{10,8},{12,10},{14,12},{16,14},{18,16},{20... | collective-permute-start | bytes 1204232 | tf_op jit(solution)/shard_map/ppermute | solution.py:22
  1016.8 3.6 collective-permute-start.10
  1018.1 3.3 collective-permute-start.11
  1207.2 22.4 %collective-permute-start.12 = (f32[1,14,28,256]{3,2,1,0:T(8,128)}, f32[1,14,28,256]{3,2,1,0:T(8,128)S(1)}, u32[]{:S(2)}, u32[]{:S(2)}) collective-permute-start(f32[1,14,28,256]{3,2,1,0:T(8,128)} %slice.1049), channel_id=1, source_target_pairs={{0,2},{2,4},{4,6},{6,8},{8,10},{10,12},{12,14},{14,16},{16,18},{18... | collective-permute-start | bytes 1204232 | tf_op jit(solution)/shard_map/ppermute | solution.py:20
  1211.4 20.0 collective-permute-start.13
  1231.5 16.5 collective-permute-start.14
  1233.0 15.0 collective-permute-start.15
  1265.6 261.0 %reduce-scatter.15.cloned.1.call-start = ((), (), s32[]{:S(2)}) async-start(), calls=%async_computation.7 | async-start | bytes 270336 | tf_op jit(solution)/shard_map/reduce_scatter | solution.py:149
  1271.2 387.0 %reduce-scatter.13.cloned.1.call-start = ((), (), s32[]{:S(2)}) async-start(), calls=%async_computation.6 | async-start | bytes 270336 | tf_op jit(solution)/shard_map/reduce_scatter | solution.py:149
  1276.6 514.7 %reduce-scatter.23.cloned.1.call-start = ((), (), s32[]{:S(2)}) async-start(), calls=%async_computation.15 | async-start | bytes 1081344
  1291.4 632.9 %reduce-scatter.19.cloned.1.call-start = ((), (), s32[]{:S(2)}) async-start(), calls=%async_computation.9 | async-start | bytes 1081344 | tf_op jit(solution)/shard_map/reduce_scatter | solution.py:151
  1304.1 753.1 %reduce-scatter.17.cloned.1.call-start = ((), (), s32[]{:S(2)}) async-start(), calls=%async_computation.8 | async-start | bytes 1081344 | tf_op jit(solution)/shard_map/reduce_scatter | solution.py:151
  1315.8 73.0 %copy-start.18 = (f32[1568,256]{1,0:T(8,128)S(1)}, f32[1568,256]{1,0:T(8,128)}, u32[]{:S(2)}) copy-start(f32[1568,256]{1,0:T(8,128)} %get-tuple-element.430) | copy-start | bytes 4816900
  1315.8 73.0 %copy-start.73 = (f32[256]{0:T(256)S(1)}, f32[256]{0:T(256)}, u32[]{:S(2)}) copy-start(f32[256]{0:T(256)} %get-tuple-element.408) | copy-start | bytes 3076
  1328.1 862.2 %reduce-scatter.21.cloned.1.call-start = ((), (), s32[]{:S(2)}) async-start(), calls=%async_computation.14 | async-start | bytes 1081344
  1418.8 239.5 %copy-start.40 = (f32[2,8,256]{2,1,0:T(8,128)S(1)}, f32[2,8,256]{2,1,0:T(8,128)}, u32[]{:S(2)}) copy-start(f32[2,8,256]{2,1,0:T(8,128)} %param.27) | copy-start | bytes 49156
  1418.8 239.5 %copy-start.91 = (f32[2,8,256]{2,1,0:T(8,128)S(1)}, f32[2,8,256]{2,1,0:T(8,128)}, u32[]{:S(2)}) copy-start(f32[2,8,256]{2,1,0:T(8,128)} %param.37) | copy-start | bytes 49156
  1418.8 638.4 %copy-start.37 = (f32[2,8,1024]{2,1,0:T(8,128)S(1)}, f32[2,8,1024]{2,1,0:T(8,128)}, u32[]{:S(2)}) copy-start(f32[2,8,1024]{2,1,0:T(8,128)} %param.29) | copy-start | bytes 196612
  1418.8 638.4 %copy-start.41 = (f32[2,8,1024]{2,1,0:T(8,128)S(1)}, f32[2,8,1024]{2,1,0:T(8,128)}, u32[]{:S(2)}) copy-start(f32[2,8,1024]{2,1,0:T(8,128)} %param.39) | copy-start | bytes 196612
  1418.8 772.4 %copy-start.38 = (f32[2,32,256]{2,1,0:T(8,128)S(1)}, f32[2,32,256]{2,1,0:T(8,128)}, u32[]{:S(2)}) copy-start(f32[2,32,256]{2,1,0:T(8,128)} %param.26) | copy-start | bytes 196612
  1418.8 772.4 %copy-start.42 = (f32[2,32,256]{2,1,0:T(8,128)S(1)}, f32[2,32,256]{2,1,0:T(8,128)}, u32[]{:S(2)}) copy-start(f32[2,32,256]{2,1,0:T(8,128)} %param.36) | copy-start | bytes 196612
  (237 other events, 1933.1 us)
Sparse Core Ops, SparseCore 0:
  11.5 56.5 all-gather.24
  71.5 52.5 all-gather.26
  127.6 52.6 all-gather.28
  183.6 53.6 all-gather.30
  1265.7 122.4 all-reduce.31
  1390.2 136.2 reduce-scatter.14
  1528.9 129.3 reduce-scatter.12
  1660.5 130.7 reduce-scatter.22
  1793.6 130.6 reduce-scatter.18
  1926.4 130.7 reduce-scatter.16
  2059.5 130.7 reduce-scatter.20
where the time goes:
time: 2210 us; the launch traced here: 2200 us
  waiting for transfers between devices  847 us (38%)
  blocking collectives  844 us (38%)
  local copies, waits for them, and re-layouts  161 us (7%)
  matrix products  159 us (7%)
  other arithmetic  134 us (6%)
  starting transfers between devices  35.9 us (2%)
    reduce_scatter x2, waiting for transfers between devices, scatter_gradients(): lax.psum_scatter(expand_delta, ('dp', 'fsdp'), scatter_dimension=0, tiled...  265 us
    unnamed x13, waiting for transfers between devices  265 us
    unnamed x6, blocking collectives  250 us
    psum x6, blocking collectives, batch_moments(): totals = lax.psum(jnp.sum(values, axis=0), ('dp', 'fsdp'))  231 us
    reduce_scatter x2, waiting for transfers between devices, scatter_gradients(): lax.psum_scatter(mixing_delta, ('dp', 'fsdp'), scatter_dimension=0, tiled...  227 us
    psum x5, blocking collectives, norm_backward(): lax.psum((jnp.sum(upstream * normed, axis=0), jnp.sum(upstream, axis=0)),...  201 us
    all_gather x2, blocking collectives, gather_forward(): lax.all_gather(mixing_part, ('dp', 'fsdp'), axis=0, tiled=True)  82.5 us
    all_gather x2, blocking collectives, gather_forward(): lax.all_gather(depth_part, ('dp', 'fsdp'), axis=0, tiled=True)  78.4 us
  transfers between devices with their start and end apart: 27, of which 12 were waited for; matrix products, arithmetic and copies ran while one was open for 14% of the time, Pallas kernels for 0%

commit v1 on v0

v1 whole, which is shorter than its diff:
```python
import functools

import jax
import jax.numpy as jnp
from jax import lax
from jax.experimental import pallas as pl
from jax.experimental.pallas import tpu as pltpu
from jax.sharding import PartitionSpec as P

EPSILON = 1e-05
MOMENTUM = 0.9
LEARN_RATE = 0.0001
HIGHEST = lax.Precision.HIGHEST
AX = ("dp", "fsdp")
F32 = jnp.float32
BF16 = jnp.bfloat16
MIB = 1 << 20

VM = pl.BlockSpec(memory_space=pltpu.VMEM)
SM = pl.BlockSpec(memory_space=pltpu.SMEM)


def params(mib):
    return pltpu.CompilerParams(vmem_limit_bytes=mib * MIB)


def dot6(left, right):
    return jnp.dot(left, right, precision=HIGHEST, preferred_element_type=F32)


def dot6_rt(left, right):
    return lax.dot_general(
        left, right, (((1,), (1,)), ((), ())), precision=HIGHEST, preferred_element_type=F32
    )


def split2(value):
    high = value.astype(BF16)
    return high, (value - high.astype(F32)).astype(BF16)


def dot3(left, right):
    lh, ll = left
    rh, rl = right
    mm = functools.partial(jnp.dot, preferred_element_type=F32)
    return mm(lh, rh) + (mm(lh, rl) + mm(ll, rh))


def columns_of(shape, width):
    col = lax.broadcasted_iota(jnp.int32, shape, len(shape) - 2)
    return col < width


def put_rows(st_ref, first, vec):
    for i in range(vec.shape[1] // 128):
        piece = vec[:, i * 128 : (i + 1) * 128]
        st_ref[:, first + i, :] = jnp.broadcast_to(piece, (st_ref.shape[0], 128))


def take_rows(st_ref, first, channels):
    return jnp.concatenate(
        [st_ref[:, first + i, :] for i in range(channels // 128)], axis=1
    )


def narrow_moments(st_ref, channels, local, total):
    k = channels // 128
    sums = take_rows(st_ref, 0, channels)
    squares = take_rows(st_ref, k, channels)
    mean = jnp.sum(sums, axis=0, keepdims=True) / total
    off = sums / local - mean
    var = (
        jnp.sum(squares, axis=0, keepdims=True)
        + local * jnp.sum(off * off, axis=0, keepdims=True)
    ) / total
    return mean, lax.rsqrt(var + EPSILON)


def sum_frames(frames, piece, channels):
    def step(f, acc):
        return acc + jnp.sum(piece(f), axis=0, keepdims=True)

    return lax.fori_loop(0, frames, step, jnp.zeros((1, channels), F32))


def local_moments(field_ref, width, local):
    frames, rows, padded, channels = field_ref.shape
    size = rows * padded
    total = sum_frames(frames, lambda f: field_ref[f].reshape(size, channels), channels)
    mean = total / local

    def squares(f):
        value = field_ref[f]
        value = jnp.where(columns_of(value.shape, width), value - mean, 0.0)
        return (value * value).reshape(size, channels)

    return total, sum_frames(frames, squares, channels)


def pad_columns(value, padded):
    rows, width, channels = value.shape
    if padded == width:
        return value
    return jnp.concatenate([value, jnp.zeros((rows, padded - width, channels), F32)], axis=1)


STAGES = ((3, 4), (1, 2), (0,))


def slot_mask(slot):
    mask = 0
    for bits in STAGES:
        mask |= (slot & ((1 << len(bits)) - 1)) << bits[0]
        slot >>= len(bits)
    return mask


def order_rows(slots_ref, out_ref, me, lanes=slice(None)):
    count, rows, _ = slots_ref.shape
    for s in range(count):
        where = pl.multiple_of(jnp.bitwise_xor(me, slot_mask(s)) * rows, rows)
        out_ref[pl.ds(where, rows), :] = slots_ref[s, :, lanes]


def k_first(width, me_ref, x_ref, w_ref, a_ref, st_ref, w_scr):
    f = pl.program_id(0)
    frames, rows, padded, narrow = a_ref.shape
    slotted = len(w_ref.shape) == 3

    @pl.when(f == 0)
    def _():
        if slotted:
            order_rows(w_ref, w_scr, me_ref[0])
        else:
            w_scr[...] = w_ref[...]

    x = pad_columns(x_ref[0], padded)
    a = dot6(x.reshape(rows * padded, x.shape[2]), w_scr[...])
    a_ref[f] = a.reshape(rows, padded, narrow)

    @pl.when(f == frames - 1)
    def _():
        total, squares = local_moments(a_ref, width, float(frames * rows * width))
        put_rows(st_ref, 0, total)
        put_rows(st_ref, narrow // 128, squares)


def frame_taps(k_ref, keep_ref, f, frames, lanes, flipped):
    taps = []
    for o in range(3):
        keep = keep_ref[o * frames + f]
        rows = []
        for p in range(3):
            cols = []
            for q in range(3):
                tap = 9 * o + 3 * p + q
                if flipped:
                    tap = 26 - tap
                cols.append(k_ref[tap : tap + 1, lanes] * keep)
            rows.append(cols)
        taps.append(rows)
    return taps


def shifted(value, padded):
    return pltpu.roll(value, 1, 0), value, pltpu.roll(value, padded - 1, 0)


def stencil_into(mp_ref, k_ref, keep_ref, store, frames, rows, padded, flipped):
    for half in range(mp_ref.shape[3] // 128):
        lanes = slice(half * 128, half * 128 + 128)

        def frame(f, carry):
            taps = frame_taps(k_ref, keep_ref, f, frames, lanes, flipped)

            def row(j, older, old):
                new = jnp.zeros((padded, 128), F32)
                for o in range(3):
                    views = shifted(mp_ref[f + o, j, :, lanes], padded)
                    for q in range(3):
                        older = older + views[q] * taps[o][2][q]
                        old = old + views[q] * taps[o][1][q]
                        new = new + views[q] * taps[o][0][q]
                return older, old, new

            zero = jnp.zeros((padded, 128), F32)
            _, _, new = row(0, zero, zero)
            _, old, new = row(1, zero, new)

            def step(j, accs):
                done, old, new = row(j, accs[0], accs[1])
                store(f, j - 2, lanes, done)
                return old, new

            lax.fori_loop(2, rows + 2, step, (old, new))
            return carry

        lax.fori_loop(0, frames, frame, 0)


def k_mix(width, total, keep_ref, a_ref, hp_ref, hn_ref, up_ref, dn_ref, cu_ref, cd_ref, st_in,
          w_ref, k_ref, vec_ref, c_ref, m_ref, mom_ref, st_ref, w_scr, mp_ref, *, slot_lanes):
    frames, rows, padded, narrow = a_ref.shape
    local = float(frames * rows * width)
    size = rows * padded
    top = keep_ref[3 * frames]
    bottom = keep_ref[3 * frames + 1]
    if slot_lanes:
        order_rows(w_ref, w_scr, keep_ref[3 * frames + 2].astype(jnp.int32), slice(0, narrow))
    else:
        w_scr[...] = w_ref[...]
    mean, inverse = narrow_moments(st_in, narrow, local, total)
    mom_ref[0:1, :] = mean
    mom_ref[1:2, :] = inverse
    scale = vec_ref[0:1, :] * inverse
    shift = vec_ref[1:2, :]

    def mixed(value):
        r = jnp.maximum((value - mean) * scale + shift, 0.0)
        r = jnp.where(columns_of(r.shape, width), r, 0.0)
        m = dot6(r.reshape(-1, narrow), w_scr[...])
        return m.reshape(value.shape)

    def own(f, carry):
        m = mixed(a_ref[f])
        m_ref[f] = m
        mp_ref[f + 1, 1 : rows + 1] = m
        return carry

    lax.fori_loop(0, frames, own, 0)
    mp_ref[0, 1 : rows + 1] = mixed(hp_ref[0])
    mp_ref[frames + 1, 1 : rows + 1] = mixed(hn_ref[0])
    mp_ref[1 : frames + 1, 0] = mixed(up_ref[:, 0]) * top
    mp_ref[1 : frames + 1, rows + 1] = mixed(dn_ref[:, 0]) * bottom
    cu = mixed(cu_ref[:, 0]) * top
    cd = mixed(cd_ref[:, 0]) * bottom
    mp_ref[0, 0] = cu[0]
    mp_ref[frames + 1, 0] = cu[1]
    mp_ref[0, rows + 1] = cd[0]
    mp_ref[frames + 1, rows + 1] = cd[1]

    def store(f, r, lanes, value):
        c_ref[f, r, :, lanes] = jnp.where(columns_of(value.shape, width), value, 0.0)

    stencil_into(mp_ref, k_ref, keep_ref, store, frames, rows, padded, False)
    total_c, squares = local_moments(c_ref, width, local)
    put_rows(st_ref, 0, total_c)
    put_rows(st_ref, narrow // 128, squares)


def second_act(c, mom, vec):
    return (c - mom[0:1, :]) * (vec[2:3, :] * mom[1:2, :]) + vec[3:4, :]


def k_expand(width, total, me_ref, c_ref, st_in, w_ref, vec_ref, e_ref, mom_ref, off_ref, st_ref,
             w_out, s_ref, sums_scr, *, slot_lanes):
    f = pl.program_id(0)
    frames, rows, padded, narrow = c_ref.shape
    wide = e_ref.shape[3]
    local = float(frames * rows * width)
    size = rows * padded

    @pl.when(f == 0)
    def _():
        if slot_lanes:
            order_rows(w_ref, w_out, me_ref[0], slice(narrow, narrow + wide))
        else:
            w_out[...] = w_ref[...]
        mean, inverse = narrow_moments(st_in, narrow, local, total)
        mom_ref[0:1, :] = mean
        mom_ref[1:2, :] = inverse
        mom = mom_ref[...]

        def act(g, acc):
            s = jnp.maximum(second_act(c_ref[g], mom, vec_ref), 0.0)
            s = jnp.where(columns_of(s.shape, width), s, 0.0)
            s_ref[g] = s
            return acc + jnp.sum(s.reshape(size, narrow), axis=0, keepdims=True)

        sums = lax.fori_loop(0, frames, act, jnp.zeros((1, narrow), F32))
        sums_scr[0:1, :] = sums / local
        put_rows(st_ref, 0, sums)
        off_ref[...] = dot6(jnp.broadcast_to(sums / local, (8, narrow)), w_out[...])
        sums_scr[1:2, :] = jnp.zeros((1, narrow), F32)

    s = s_ref[f]
    s = jnp.where(columns_of(s.shape, width), s - sums_scr[0:1, :], 0.0)
    e = dot6(s.reshape(size, narrow), w_out[...])
    e_ref[0] = e.reshape(rows, padded, wide)
    part = jnp.sum(e * e, axis=0, keepdims=True)
    k = narrow // 128

    @pl.when(f == 0)
    def _():
        put_rows(st_ref, k, part)

    @pl.when(f > 0)
    def _():
        for i in range(wide // 128):
            st_ref[:, k + i, :] = st_ref[:, k + i, :] + jnp.broadcast_to(
                part[:, i * 128 : (i + 1) * 128], (st_ref.shape[0], 128)
            )


def wide_moments(st_in, w, off, gain, bias, narrow, wide, local, total):
    k = narrow // 128
    s_means = take_rows(st_in, 0, narrow) / local
    squares = take_rows(st_in, k, wide)
    e_means = dot6(s_means, w)
    s_mean = jnp.mean(s_means, axis=0, keepdims=True)
    mean = jnp.mean(e_means, axis=0, keepdims=True)
    away = e_means - mean
    var = (
        jnp.sum(squares, axis=0, keepdims=True)
        + local * jnp.sum(away * away, axis=0, keepdims=True)
    ) / total
    inverse = lax.rsqrt(var + EPSILON)
    scale = gain * inverse
    return scale, (off - mean) * scale + bias, inverse, s_mean


def k_join(width, total, e_ref, x_ref, st_in, off_ref, w_ref, vecw_ref, wr_ref, x_out, a_ref,
           momw_ref, smean_ref, st_ref):
    f = pl.program_id(0)
    frames, rows, padded, narrow = a_ref.shape
    wide = e_ref.shape[3]
    local = float(frames * rows * width)
    size = rows * padded

    @pl.when(f == 0)
    def _():
        scale, shift, inverse, s_mean = wide_moments(
            st_in, w_ref[...], off_ref[0:1, :], vecw_ref[0:1, :], vecw_ref[1:2, :], narrow, wide,
            local, total,
        )
        momw_ref[0:1, :] = scale
        momw_ref[1:2, :] = shift
        momw_ref[2:3, :] = inverse
        smean_ref[0:1, :] = s_mean

    x = pad_columns(x_ref[0], padded)
    z = e_ref[0] * momw_ref[0:1, :] + momw_ref[1:2, :] + x
    z = jnp.where(columns_of(z.shape, width), jnp.maximum(z, 0.0), 0.0)
    x_out[0] = z
    a = dot6(z.reshape(size, wide), wr_ref[...])
    a_ref[f] = a.reshape(rows, padded, narrow)

    @pl.when(f == frames - 1)
    def _():
        total_a, squares = local_moments(a_ref, width, local)
        put_rows(st_ref, 0, total_a)
        put_rows(st_ref, narrow // 128, squares)


def prepare_wide(width, c_ref, mom_ref, vec_ref, smean_ref, w_ref, alpha, st_h, st_l, wt_h, wt_l):
    frames, rows, padded, narrow = c_ref.shape
    size = rows * padded
    mom = mom_ref[...]
    center = smean_ref[0:1, :]

    def act(g, carry):
        s = jnp.maximum(second_act(c_ref[g], mom, vec_ref), 0.0) - center
        s = jnp.where(columns_of(s.shape, width), s, 0.0)
        high, low = split2(s.reshape(size, narrow).T)
        st_h[g] = high
        st_l[g] = low
        return carry

    lax.fori_loop(0, frames, act, 0)
    high, low = split2((w_ref[...] * alpha).T)
    wt_h[...] = high
    wt_l[...] = low


def wide_step(gz, f, u_ref, p_ref, bias_acc, st_h, st_l, wt_h, wt_l):
    size, wide = gz.shape
    _, rows, padded, narrow = u_ref.shape
    parts = split2(gz)
    u = dot3(parts, (wt_h[...], wt_l[...]))
    u_ref[f] = u.reshape(rows, padded, narrow)
    p = dot3((st_h[f], st_l[f]), parts)
    part = jnp.sum(gz, axis=0, keepdims=True)

    @pl.when(f == 0)
    def _():
        p_ref[...] = p
        bias_acc[0:1, :] = part

    @pl.when(f > 0)
    def _():
        p_ref[...] = p_ref[...] + p
        bias_acc[0:1, :] = bias_acc[0:1, :] + part


def wide_finish(p_ref, w_ref, inverse, bias_acc, st_ref):
    wide = w_ref.shape[1]
    gain_sum = jnp.sum(p_ref[...] * w_ref[...], axis=0, keepdims=True) * inverse
    put_rows(st_ref, 0, bias_acc[0:1, :])
    put_rows(st_ref, wide // 128, gain_sum)


def k_turn(width, total, e_ref, x_ref, cot_ref, st_in, off_ref, w_ref, vecw_ref, c_ref, mom_ref,
           vec_ref, out_ref, gz_ref, u_ref, p_ref, momw_ref, smean_ref, pool_ref, st_ref,
           st_h, st_l, wt_h, wt_l, bias_acc):
    f = pl.program_id(0)
    frames, rows, padded, narrow = c_ref.shape
    wide = e_ref.shape[3]
    local = float(frames * rows * width)
    size = rows * padded

    @pl.when(f == 0)
    def _():
        scale, shift, inverse, s_mean = wide_moments(
            st_in, w_ref[...], off_ref[0:1, :], vecw_ref[0:1, :], vecw_ref[1:2, :], narrow, wide,
            local, total,
        )
        momw_ref[0:1, :] = scale
        momw_ref[1:2, :] = shift
        momw_ref[2:3, :] = inverse
        smean_ref[0:1, :] = s_mean
        prepare_wide(width, c_ref, mom_ref, vec_ref, smean_ref, w_ref, scale, st_h, st_l, wt_h, wt_l)

    z = e_ref[0] * momw_ref[0:1, :] + momw_ref[1:2, :] + x_ref[0]
    out = jnp.maximum(z, 0.0)
    out_ref[0] = out[:, :width, :]
    keep = columns_of(z.shape, width)
    pooled = jnp.where(keep, out, 0.0).reshape(size, wide)
    pool_ref[0] = jnp.broadcast_to(jnp.sum(pooled, axis=0, keepdims=True), (8, wide))
    cot = pad_columns(cot_ref[0], padded)
    gz = jnp.where(jnp.logical_and(z > 0.0, keep), cot, 0.0)
    gz_ref[0] = gz
    wide_step(gz.reshape(size, wide), f, u_ref, p_ref, bias_acc, st_h, st_l, wt_h, wt_l)

    @pl.when(f == frames - 1)
    def _():
        wide_finish(p_ref, w_ref, momw_ref[2:3, :], bias_acc, st_ref)


def k_second(width, total, u_ref, c_ref, st_in, w_ref, momw_ref, smean_ref, mom_ref, vec_ref, n_ref,
             gw_ref, st_ref):
    frames, rows, padded, narrow = u_ref.shape
    wide = w_ref.shape[1]
    size = rows * padded
    k = wide // 128
    bias_sum = jnp.sum(take_rows(st_in, 0, wide), axis=0, keepdims=True)
    gain_sum = jnp.sum(take_rows(st_in, k, wide), axis=0, keepdims=True)
    gw_ref[0:1, :] = gain_sum
    gw_ref[1:2, :] = bias_sum
    alpha = momw_ref[0:1, :]
    w = w_ref[...]
    q = dot6_rt(w * (alpha * momw_ref[2:3, :] * (gain_sum / total)), w)
    d = dot6_rt(jnp.broadcast_to(alpha * (bias_sum / total), (8, wide)), w)[0:1, :]
    mom = mom_ref[...]
    center = smean_ref[0:1, :]

    def step(f, accs):
        c = c_ref[f]
        y = second_act(c, mom, vec_ref)
        keep = columns_of(c.shape, width)
        s = jnp.where(keep, jnp.maximum(y, 0.0) - center, 0.0)
        corr = dot6(s.reshape(size, narrow), q).reshape(rows, padded, narrow)
        n = jnp.where(jnp.logical_and(y > 0.0, keep), u_ref[f] - corr - d, 0.0)
        n_ref[f] = n
        xhat = (c - mom[0:1, :]) * mom[1:2, :]
        return (
            accs[0] + jnp.sum(n.reshape(size, narrow), axis=0, keepdims=True),
            accs[1] + jnp.sum((n * xhat).reshape(size, narrow), axis=0, keepdims=True),
        )

    zero = jnp.zeros((1, narrow), F32)
    bias_acc, gain_acc = lax.fori_loop(0, frames, step, (zero, zero))
    put_rows(st_ref, 0, bias_acc)
    put_rows(st_ref, narrow // 128, gain_acc)


def k_expand_grad(width, total, c_ref, p_ref, w_ref, gw_ref, momw_ref, smean_ref, mom_ref, vec_ref,
                  dw_ref):
    frames, rows, padded, narrow = c_ref.shape
    size = rows * padded
    mom = mom_ref[...]
    center = smean_ref[0:1, :]

    def step(f, accs):
        y = second_act(c_ref[f], mom, vec_ref)
        s = jnp.where(columns_of(y.shape, width), jnp.maximum(y, 0.0) - center, 0.0)
        s = s.reshape(size, narrow)
        turned = s.T
        ones = jnp.broadcast_to(jnp.sum(turned, axis=1, keepdims=True), (narrow, 128))
        return accs[0] + dot3(split2(turned), split2(s)), accs[1] + ones

    gram, sums = lax.fori_loop(
        0, frames, step, (jnp.zeros((narrow, narrow), F32), jnp.zeros((narrow, 128), F32))
    )
    alpha = momw_ref[0:1, :]
    gamma = gw_ref[0:1, :] / total * momw_ref[2:3, :]
    beta = gw_ref[1:2, :] / total
    seen = dot3(split2(gram), split2(w_ref[...]))
    dw_ref[...] = alpha * (p_ref[...] - sums[:, 0:1] * beta - seen * gamma)


def k_first_back(width, total, keep_ref, n_ref, np_ref, nn_ref, nu_ref, nd_ref, ncu_ref, ncd_ref,
                 c_ref, cp_ref, cn_ref, cup_ref, cdn_ref, ccu_ref, ccd_ref, st_in, a_ref, w_ref,
                 k_ref, vec_ref, mom1_ref, mom2_ref, gm_ref, n1_ref, gcp_ref, gd_ref, st_ref,
                 wt_h, wt_l):
    frames, rows, padded, narrow = n_ref.shape
    size = rows * padded
    top = keep_ref[3 * frames]
    bottom = keep_ref[3 * frames + 1]
    k = narrow // 128
    bias_sum = jnp.sum(take_rows(st_in, 0, narrow), axis=0, keepdims=True)
    gain_sum = jnp.sum(take_rows(st_in, k, narrow), axis=0, keepdims=True)
    gd_ref[0:1, :] = gain_sum
    gd_ref[1:2, :] = bias_sum
    mom2 = mom2_ref[...]
    alpha = vec_ref[2:3, :] * mom2[1:2, :]
    beta = bias_sum / total
    gamma = gain_sum / total

    def back(n, c):
        xhat = (c - mom2[0:1, :]) * mom2[1:2, :]
        g = alpha * (n - beta - xhat * gamma)
        return jnp.where(columns_of(g.shape, width), g, 0.0)

    def own(f, carry):
        gcp_ref[f + 1, 1 : rows + 1] = back(n_ref[f], c_ref[f])
        return carry

    lax.fori_loop(0, frames, own, 0)
    gcp_ref[0, 1 : rows + 1] = back(np_ref[0], cp_ref[0])
    gcp_ref[frames + 1, 1 : rows + 1] = back(nn_ref[0], cn_ref[0])
    gcp_ref[1 : frames + 1, 0] = back(nu_ref[:, 0], cup_ref[:, 0]) * top
    gcp_ref[1 : frames + 1, rows + 1] = back(nd_ref[:, 0], cdn_ref[:, 0]) * bottom
    cu = back(ncu_ref[:, 0], ccu_ref[:, 0]) * top
    cd = back(ncd_ref[:, 0], ccd_ref[:, 0]) * bottom
    gcp_ref[0, 0] = cu[0]
    gcp_ref[frames + 1, 0] = cu[1]
    gcp_ref[0, rows + 1] = cd[0]
    gcp_ref[frames + 1, rows + 1] = cd[1]

    def store(f, r, lanes, value):
        gm_ref[f, r, :, lanes] = jnp.where(columns_of(value.shape, width), value, 0.0)

    stencil_into(gcp_ref, k_ref, keep_ref, store, frames, rows, padded, True)
    high, low = split2(w_ref[...].T)
    wt_h[...] = high
    wt_l[...] = low
    mom1 = mom1_ref[...]
    scale1 = vec_ref[0:1, :] * mom1[1:2, :]

    def step(f, accs):
        gr = dot3(split2(gm_ref[f].reshape(size, narrow)), (wt_h[...], wt_l[...]))
        off = a_ref[f] - mom1[0:1, :]
        y = off * scale1 + vec_ref[1:2, :]
        keep = jnp.logical_and(y > 0.0, columns_of(y.shape, width))
        n = jnp.where(keep, gr.reshape(rows, padded, narrow), 0.0)
        n1_ref[f] = n
        return (
            accs[0] + jnp.sum(n.reshape(size, narrow), axis=0, keepdims=True),
            accs[1] + jnp.sum((n * (off * mom1[1:2, :])).reshape(size, narrow), axis=0, keepdims=True),
        )

    zero = jnp.zeros((1, narrow), F32)
    bias_acc, gain_acc = lax.fori_loop(0, frames, step, (zero, zero))
    put_rows(st_ref, 0, bias_acc)
    put_rows(st_ref, k, gain_acc)


def k_mix_grads(width, keep_ref, gcp_ref, m_ref, gm_ref, a_ref, vec_ref, mom1_ref, dk_ref, dm_ref,
                acc_ref):
    frames, rows, padded, narrow = m_ref.shape
    size = rows * padded
    mom1 = mom1_ref[...]
    scale1 = vec_ref[0:1, :] * mom1[1:2, :]

    def mixing(f, acc):
        y = (a_ref[f] - mom1[0:1, :]) * scale1 + vec_ref[1:2, :]
        r = jnp.where(columns_of(y.shape, width), jnp.maximum(y, 0.0), 0.0)
        turned = r.reshape(size, narrow).T
        return acc + dot3(split2(turned), split2(gm_ref[f].reshape(size, narrow)))

    dm_ref[...] = lax.fori_loop(0, frames, mixing, jnp.zeros((narrow, narrow), F32))
    acc_ref[...] = jnp.zeros(acc_ref.shape, F32)
    for half in range(narrow // 128):
        lanes = slice(half * 128, half * 128 + 128)

        def frame(f, carry):
            for o in range(3):
                keep = keep_ref[o * frames + f]

                def row(j, accs):
                    views = shifted(gcp_ref[f + o, j, :, lanes], padded)
                    new = []
                    for p in range(3):
                        r = j - p
                        inside = jnp.logical_and(r >= 0, r < rows).astype(F32)
                        m = m_ref[f, jnp.clip(r, 0, rows - 1), :, lanes] * inside
                        for q in range(3):
                            prod = (m * views[q]).reshape(padded // 8, 8, 128)
                            new.append(accs[3 * p + q] + jnp.sum(prod, axis=0))
                    return tuple(new)

                zero = jnp.zeros((8, 128), F32)
                accs = lax.fori_loop(0, rows + 2, row, (zero,) * 9)
                for i in range(9):
                    tap = 26 - (9 * o + i)
                    acc_ref[tap, :, lanes] = acc_ref[tap, :, lanes] + accs[i] * keep
            return carry

        lax.fori_loop(0, frames, frame, 0)
    for tap in range(27):
        dk_ref[tap : tap + 1, :] = jnp.sum(acc_ref[tap], axis=0, keepdims=True)
    dk_ref[27:32, :] = jnp.zeros((5, narrow), F32)


def first_norm_back(width, total, n1_ref, a_ref, st_in, vec_ref, mom1_ref, gn_ref, ga_ref):
    frames, rows, padded, narrow = n1_ref.shape
    k = narrow // 128
    bias_sum = jnp.sum(take_rows(st_in, 0, narrow), axis=0, keepdims=True)
    gain_sum = jnp.sum(take_rows(st_in, k, narrow), axis=0, keepdims=True)
    gn_ref[0:1, :] = gain_sum
    gn_ref[1:2, :] = bias_sum
    mom1 = mom1_ref[...]
    alpha = vec_ref[0:1, :] * mom1[1:2, :]

    def step(f, carry):
        xhat = (a_ref[f] - mom1[0:1, :]) * mom1[1:2, :]
        g = alpha * (n1_ref[f] - bias_sum / total - xhat * (gain_sum / total))
        ga_ref[f] = jnp.where(columns_of(g.shape, width), g, 0.0)
        return carry

    lax.fori_loop(0, frames, step, 0)


def input_grads(ga, x, f, wt_h, wt_l, dwt):
    turned = split2(ga.T)
    dx = dot3(split2(ga), (wt_h[...], wt_l[...]))
    dw = dot3(turned, split2(x))

    @pl.when(f == 0)
    def _():
        dwt[...] = dw

    @pl.when(f > 0)
    def _():
        dwt[...] = dwt[...] + dw

    return dx


def k_between(width, total, n1_ref, a_ref, st_in, vec_ref, mom1_ref, wr_ref, x_ref, gz_in, c_ref,
              mom2_ref, vec2_ref, w_ref, momw_ref, smean_ref, gz_ref, u_ref, p_ref, dw_ref, gn_ref,
              st_ref, ga_ref, wrt_h, wrt_l, dwt, st_h, st_l, wt_h, wt_l, bias_acc):
    f = pl.program_id(0)
    frames, rows, padded, narrow = n1_ref.shape
    wide = x_ref.shape[3]
    size = rows * padded

    @pl.when(f == 0)
    def _():
        first_norm_back(width, total, n1_ref, a_ref, st_in, vec_ref, mom1_ref, gn_ref, ga_ref)
        high, low = split2(wr_ref[...].T)
        wrt_h[...] = high
        wrt_l[...] = low
        prepare_wide(width, c_ref, mom2_ref, vec2_ref, smean_ref, w_ref, momw_ref[0:1, :], st_h, st_l,
                     wt_h, wt_l)

    x = x_ref[0].reshape(size, wide)
    gy = input_grads(ga_ref[f].reshape(size, narrow), x, f, wrt_h, wrt_l, dwt)
    gy = gy + gz_in[0].reshape(size, wide)
    gz = jnp.where(x > 0.0, gy, 0.0)
    gz_ref[0] = gz.reshape(rows, padded, wide)
    wide_step(gz, f, u_ref, p_ref, bias_acc, st_h, st_l, wt_h, wt_l)

    @pl.when(f == frames - 1)
    def _():
        wide_finish(p_ref, w_ref, momw_ref[2:3, :], bias_acc, st_ref)
        dw_ref[...] = dwt[...].T


def k_last(width, total, n1_ref, a_ref, st_in, vec_ref, mom1_ref, wr_ref, x_ref, gz_in, gx_ref,
           dw_ref, gn_ref, ga_ref, wrt_h, wrt_l, dwt):
    f = pl.program_id(0)
    frames, rows, padded, narrow = n1_ref.shape
    wide = gz_in.shape[3]
    size = rows * padded

    @pl.when(f == 0)
    def _():
        first_norm_back(width, total, n1_ref, a_ref, st_in, vec_ref, mom1_ref, gn_ref, ga_ref)
        high, low = split2(wr_ref[...].T)
        wrt_h[...] = high
        wrt_l[...] = low

    x = pad_columns(x_ref[0], padded).reshape(size, wide)
    gy = input_grads(ga_ref[f].reshape(size, narrow), x, f, wrt_h, wrt_l, dwt)
    gy = gy.reshape(rows, padded, wide) + gz_in[0]
    gx_ref[0] = gy[:, :width, :]

    @pl.when(f == frames - 1)
    def _():
        dw_ref[...] = dwt[...].T


def exchange(rows):
    return lax.all_to_all(rows, AX, 0, 0)


def perm(step, shape):
    dp, fs = shape
    pairs = []
    for i in range(dp):
        for j in range(fs):
            a, b = i + step[0], j + step[1]
            if 0 <= a < dp and 0 <= b < fs:
                pairs.append((i * fs + j, a * fs + b))
    return pairs


def halo(field, shape):
    frames, rows = field.shape[0], field.shape[1]
    first, last = field[0:1], field[frames - 1 :]
    move = lambda value, step: lax.ppermute(value, AX, perm(step, shape))
    before = move(last, (1, 0))
    after = move(first, (-1, 0))
    if shape[1] == 2:
        upper = lax.axis_index("fsdp") == 0
        swap = [(i, i ^ 1) for i in range(shape[0] * 2)]
        edge = jnp.where(upper, field[:, rows - 1 :], field[:, 0:1])
        row = lax.ppermute(edge, AX, swap)
        fwd = [(i, (i + 2) ^ 1) for i in range(shape[0] * 2 - 2)]
        bwd = [(i, (i - 2) ^ 1) for i in range(2, shape[0] * 2)]
        corner = jnp.concatenate(
            [lax.ppermute(edge[frames - 1 :], AX, fwd), lax.ppermute(edge[0:1], AX, bwd)]
        )
        return before, after, row, row, corner, corner
    above = move(field[:, rows - 1 :], (0, 1))
    below = move(field[:, 0:1], (0, -1))
    up = jnp.concatenate(
        [move(last[:, rows - 1 :], (1, 1)), move(first[:, rows - 1 :], (-1, 1))]
    )
    down = jnp.concatenate([move(last[:, 0:1], (1, -1)), move(first[:, 0:1], (-1, -1))])
    return before, after, above, below, up, down


def tree_gather(part, devices):
    stack = part[None]
    for bits in STAGES:
        low = bits[0]
        pieces = [stack]
        for step in range(1, 1 << len(bits)):
            mask = step << low
            pieces.append(lax.ppermute(stack, AX, [(i, i ^ mask) for i in range(devices)]))
        stack = jnp.concatenate(pieces, axis=0)
    return stack


def owner_sums(local, devices):
    parts = local.reshape((devices, local.shape[0] // devices) + local.shape[1:])
    return jnp.sum(lax.all_to_all(parts, AX, 0, 0), axis=0)


def body(inputs, cotangent, clip_index, *args):
    weights, momenta = args[:10], args[10:]
    frames, rows, width, wide = inputs.shape
    narrow = weights[0].shape[2]
    padded = -(-width // 8) * 8
    shape = (lax.axis_size("dp"), lax.axis_size("fsdp"))
    devices = shape[0] * shape[1]
    rank = lax.axis_index(AX)
    total = float(frames * rows * width * devices)
    size = rows * padded
    slotted = devices == 32

    share_n, share_w = weights[1].shape[1], weights[6 + 2].shape[1]
    small = jnp.concatenate(
        [weights[2].reshape(-1)]
        + [weights[i].reshape(-1) for i in (4, 5, 6, 7, 8, 9)]
    )
    length = small.shape[0]
    lanes = -(-length // 128) * 128
    small = jnp.pad(small, (0, lanes - length)).reshape(lanes // 128, 128)
    small = lax.all_to_all(jnp.broadcast_to(small[None], (devices,) + small.shape), AX, 0, 0)
    small = small.reshape(devices, lanes)

    def unpack(first, inner):
        n = 1
        for v in inner:
            n *= v
        return first + n, small[:, first : first + n].reshape((devices,) + inner)

    at, taps = unpack(0, (2, share_n, 27))
    taps = jnp.pad(taps.transpose(1, 3, 0, 2).reshape(2, 27, narrow), ((0, 0), (0, 5), (0, 0)))
    rows_n = []
    for _ in range(4):
        at, vec = unpack(at, (2, share_n))
        rows_n.append(vec.transpose(1, 0, 2).reshape(2, narrow))
    rows_w = []
    for _ in range(2):
        at, vec = unpack(at, (2, share_w))
        rows_w.append(vec.transpose(1, 0, 2).reshape(2, wide))
    vec_n = jnp.pad(jnp.stack(rows_n, axis=1), ((0, 0), (0, 4), (0, 0)))
    vec_w = jnp.pad(jnp.stack(rows_w, axis=1), ((0, 0), (0, 6), (0, 0)))

    edge = jnp.full((1,), -1, jnp.int32)
    window = lax.dynamic_slice_in_dim(
        jnp.concatenate([edge, clip_index, edge]), lax.axis_index("dp") * frames, frames + 2
    )
    centre = window[1:-1]
    flags = jnp.concatenate(
        [
            (window[:-2] == centre).astype(F32),
            jnp.ones((frames,), F32),
            (window[2:] == centre).astype(F32),
            (lax.axis_index("fsdp") > 0).astype(F32)[None],
            (lax.axis_index("fsdp") < shape[1] - 1).astype(F32)[None],
            rank.astype(F32)[None],
        ]
    )
    me = rank.astype(jnp.int32)[None]

    gather = lambda part: lax.all_gather(part, AX, axis=0, tiled=True)
    if slotted:
        wr0 = tree_gather(weights[0][0], devices)
        pair0 = tree_gather(
            jnp.concatenate([weights[1][0], weights[3][0]], axis=1), devices
        )
        mix_w0 = exp_w0 = pair0
    else:
        wr0 = gather(weights[0][0])
        mix_w0, exp_w0 = gather(weights[1][0]), gather(weights[3][0])
    later = jnp.concatenate(
        [
            weights[0][1].reshape(-1),
            weights[1][0].reshape(-1),
            weights[1][1].reshape(-1),
            weights[3][1].reshape(-1),
        ]
    ).reshape(-1, 128)
    later = lax.all_gather(later, AX, axis=0, tiled=False).reshape(devices, -1)

    def unpack_later(first, shp):
        n = shp[0] * shp[1]
        return first + n, later[:, first : first + n].reshape(devices * shp[0], shp[1])

    at, wr1 = unpack_later(0, weights[0].shape[1:])
    at, wm0 = unpack_later(at, weights[1].shape[1:])
    at, wm1 = unpack_later(at, weights[1].shape[1:])
    at, we1 = unpack_later(at, weights[3].shape[1:])

    sds = jax.ShapeDtypeStruct
    field_n = sds((frames, rows, padded, narrow), F32)
    field_w = sds((frames, rows, padded, wide), F32)
    stat_n = sds((devices, 2 * narrow // 128, 128), F32)
    stat_e = sds((devices, (narrow + wide) // 128, 128), F32)
    stat_w = sds((devices, 2 * wide // 128, 128), F32)
    mom_n = sds((8, narrow), F32)
    mom_w = sds((8, wide), F32)
    outer = lambda lead, last: pl.BlockSpec((1, lead, last, wide), lambda f: (f, 0, 0, 0))
    whole = lambda s: pl.BlockSpec(s.shape, lambda f: (0,) * len(s.shape))
    scr = pltpu.VMEM
    cst = functools.partial(pl.CostEstimate, transcendentals=0)
    flop_w = 2 * frames * size * narrow * wide

    def first(x, w):
        return pl.pallas_call(
            functools.partial(k_first, width),
            grid=(frames,),
            in_specs=[SM, outer(rows, width), whole(w)],
            out_specs=(whole(field_n), whole(stat_n)),
            out_shape=(field_n, stat_n),
            scratch_shapes=[scr((wide, narrow), F32)],
            compiler_params=params(30),
            cost_estimate=cst(flops=6 * flop_w, bytes_accessed=4 * x.size),
            name="first",
        )(me, x, w)

    def mix(block, a, halos, st, w):
        return pl.pallas_call(
            functools.partial(k_mix, width, total, slot_lanes=len(w.shape) == 3),
            in_specs=[SM] + [VM] * 11,
            out_specs=(VM,) * 4,
            out_shape=(field_n, field_n, mom_n, stat_n),
            scratch_shapes=[
                scr((narrow, narrow), F32),
                scr((frames + 2, rows + 2, padded, narrow), F32),
            ],
            compiler_params=params(30),
            cost_estimate=cst(flops=6 * flop_w, bytes_accessed=8 * a.size),
            name="mix",
        )(flags, a, *halos, st, w, taps[block], vec_n[block])

    def expand(block, c, st, w):
        return pl.pallas_call(
            functools.partial(k_expand, width, total, slot_lanes=len(w.shape) == 3),
            grid=(frames,),
            in_specs=[SM, whole(c), whole(st), whole(w), whole(mom_n)],
            out_specs=(outer(rows, padded), whole(mom_n), whole(mom_w), whole(stat_e),
                       whole(sds((narrow, wide), F32))),
            out_shape=(field_w, mom_n, mom_w, stat_e, sds((narrow, wide), F32)),
            scratch_shapes=[scr(field_n.shape, F32), scr((8, narrow), F32)],
            compiler_params=params(30),
            cost_estimate=cst(flops=6 * flop_w, bytes_accessed=4 * field_w.size),
            name="expand",
        )(me, c, st, w, vec_n[block])

    def join(block, e, x, st, off, we, wr):
        return pl.pallas_call(
            functools.partial(k_join, width, total),
            grid=(frames,),
            in_specs=[outer(rows, padded), outer(rows, x.shape[2]), whole(st), whole(off), whole(we),
                      whole(mom_w), whole(wr)],
            out_specs=(outer(rows, padded), whole(field_n), whole(mom_w), whole(mom_n),
                       whole(stat_n)),
            out_shape=(field_w, field_n, mom_w, mom_n, stat_n),
            compiler_params=params(40),
            cost_estimate=cst(flops=6 * flop_w, bytes_accessed=12 * field_w.size),
            name="join",
        )(e, x, st, off, we, vec_w[block], wr)

    turned = [
        scr((frames, narrow, size), BF16),
        scr((frames, narrow, size), BF16),
        scr((wide, narrow), BF16),
        scr((wide, narrow), BF16),
    ]

    def turn(e, x, st, off, we, c, mom2):
        pool = sds((frames, 8, wide), F32)
        return pl.pallas_call(
            functools.partial(k_turn, width, total),
            grid=(frames,),
            in_specs=[outer(rows, padded), outer(rows, padded), outer(rows, width), whole(st),
                      whole(off), whole(we), whole(mom_w), whole(c), whole(mom_n), whole(mom_n)],
            out_specs=(outer(rows, width), outer(rows, padded), whole(field_n), whole(we),
                       whole(mom_w), whole(mom_n), pl.BlockSpec((1, 8, wide), lambda f: (f, 0, 0)),
                       whole(stat_w)),
            out_shape=(sds(inputs.shape, F32), field_w, field_n, sds((narrow, wide), F32), mom_w,
                       mom_n, pool, stat_w),
            scratch_shapes=turned + [scr((8, wide), F32)],
            compiler_params=params(48),
            cost_estimate=cst(flops=6 * flop_w, bytes_accessed=20 * field_w.size),
            name="turn",
        )(e, x, cotangent, st, off, we, vec_w[1], c, mom2, vec_n[1])

    def second(block, u, c, st, we, momw, smean, mom2):
        return pl.pallas_call(
            functools.partial(k_second, width, total),
            in_specs=[VM] * 8,
            out_specs=(VM,) * 3,
            out_shape=(field_n, mom_w, stat_n),
            compiler_params=params(24),
            cost_estimate=cst(flops=2 * flop_w, bytes_accessed=12 * c.size),
            name="second",
        )(u, c, st, we, momw, smean, mom2, vec_n[block])

    def expand_grad(block, c, p, we, gw, momw, smean, mom2):
        return pl.pallas_call(
            functools.partial(k_expand_grad, width, total),
            in_specs=[VM] * 8,
            out_specs=VM,
            out_shape=sds((narrow, wide), F32),
            compiler_params=params(24),
            cost_estimate=cst(flops=flop_w, bytes_accessed=8 * c.size),
            name="expand_grad",
        )(c, p, we, gw, momw, smean, mom2, vec_n[block])

    def first_back(block, n, nh, c, ch, st, a, wm, mom1, mom2):
        return pl.pallas_call(
            functools.partial(k_first_back, width, total),
            in_specs=[SM] + [VM] * 21,
            out_specs=(VM,) * 5,
            out_shape=(field_n, field_n, sds((frames + 2, rows + 2, padded, narrow), F32), mom_n,
                       stat_n),
            scratch_shapes=[scr((narrow, narrow), BF16), scr((narrow, narrow), BF16)],
            compiler_params=params(40),
            cost_estimate=cst(flops=6 * flop_w, bytes_accessed=16 * c.size),
            name="first_back",
        )(flags, n, *nh, c, *ch, st, a, wm, taps[block], vec_n[block], mom1, mom2)

    def mix_grads(block, gcp, m, gm, a, mom1):
        return pl.pallas_call(
            functools.partial(k_mix_grads, width),
            in_specs=[SM] + [VM] * 6,
            out_specs=(VM,) * 2,
            out_shape=(sds((32, narrow), F32), sds((narrow, narrow), F32)),
            scratch_shapes=[scr((27, 8, narrow), F32)],
            compiler_params=params(30),
            cost_estimate=cst(flops=6 * flop_w, bytes_accessed=16 * a.size),
            name="mix_grads",
        )(flags, gcp, m, gm, a, vec_n[block], mom1)

    back = [scr(field_n.shape, F32), scr((narrow, wide), BF16), scr((narrow, wide), BF16),
            scr((narrow, wide), F32)]
    full_r = sds((wide, narrow), F32)

    def between(n1, a, st, mom1, wr, x, gz, c, mom2, we, momw, smean):
        return pl.pallas_call(
            functools.partial(k_between, width, total),
            grid=(frames,),
            in_specs=[whole(field_n), whole(field_n), whole(st), whole(mom_n), whole(mom_n),
                      whole(wr), outer(rows, padded), outer(rows, padded), whole(field_n),
                      whole(mom_n), whole(mom_n), whole(we), whole(mom_w), whole(mom_n)],
            out_specs=(outer(rows, padded), whole(field_n), whole(we), whole(full_r), whole(mom_n),
                       whole(stat_w)),
            out_shape=(field_w, field_n, sds((narrow, wide), F32), full_r, mom_n, stat_w),
            scratch_shapes=back + turned + [scr((8, wide), F32)],
            compiler_params=params(56),
            cost_estimate=cst(flops=12 * flop_w, bytes_accessed=12 * field_w.size),
            name="between",
        )(n1, a, st, vec_n[1], mom1, wr, x, gz, c, mom2, vec_n[0], we, momw, smean)

    def last(n1, a, st, mom1, wr, gz):
        return pl.pallas_call(
            functools.partial(k_last, width, total),
            grid=(frames,),
            in_specs=[whole(field_n), whole(field_n), whole(st), whole(mom_n), whole(mom_n),
                      whole(wr), outer(rows, width), outer(rows, padded)],
            out_specs=(outer(rows, width), whole(full_r), whole(mom_n)),
            out_shape=(sds(inputs.shape, F32), full_r, mom_n),
            scratch_shapes=back,
            compiler_params=params(48),
            cost_estimate=cst(flops=6 * flop_w, bytes_accessed=12 * field_w.size),
            name="last",
        )(n1, a, st, vec_n[0], mom1, wr, inputs, gz)

    a0, st = first(inputs, wr0)
    c0, m0, mom10, st = mix(0, a0, halo(a0, shape), exchange(st), mix_w0)
    ch0 = halo(c0, shape)
    e0, mom20, off0, st, we0 = expand(0, c0, exchange(st), exp_w0)
    x1, a1, momw0, smean0, st = join(0, e0, inputs, exchange(st), off0, we0, wr1)
    c1, m1, mom11, st = mix(1, a1, halo(a1, shape), exchange(st), wm1)
    ch1 = halo(c1, shape)
    e1, mom21, off1, st, _ = expand(1, c1, exchange(st), we1)
    out, gz1, u1, p1, momw1, smean1, pool, st = turn(e1, x1, exchange(st), off1, we1, c1, mom21)

    clips = clip_index.shape[0] // 6
    labels = jnp.arange(clips, dtype=jnp.int32)
    hot = (centre[None, :] == labels[:, None]).astype(F32)
    pooled = jnp.dot(hot, pool[:, 0, :], precision=HIGHEST, preferred_element_type=F32)
    if devices <= 64:
        pooled = jnp.sum(lax.all_gather(pooled, AX, axis=0, tiled=False), axis=0)
    else:
        pooled = lax.psum(pooled, AX)
    counts = jnp.sum((clip_index[None, :] == labels[:, None]).astype(F32), axis=1)
    pooled = pooled / (counts * float(rows * shape[1] * width))[:, None]

    n, gw1, st = second(1, u1, c1, exchange(st), we1, momw1, smean1, mom21)
    nh = halo(n, shape)
    st = exchange(st)
    de1 = expand_grad(1, c1, p1, we1, gw1, momw1, smean1, mom21)
    gm, n1, gcp, gd1, st = first_back(1, n, nh, c1, ch1, st, a1, wm1, mom11, mom21)
    st = exchange(st)
    dk1, dm1 = mix_grads(1, gcp, m1, gm, a1, mom11)
    if slotted:
        wr0_full = gather_order(wr0, rank, devices, wide)
    else:
        wr0_full = wr0
    gz0, u0, p0, dr1, gn1, st = between(n1, a1, st, mom11, wr1, x1, gz1, c0, mom20, we0, momw0, smean0)
    n, gw0, st = second(0, u0, c0, exchange(st), we0, momw0, smean0, mom20)
    nh = halo(n, shape)
    st = exchange(st)
    de0 = expand_grad(0, c0, p0, we0, gw0, momw0, smean0, mom20)
    gm, n1, gcp, gd0, st = first_back(0, n, nh, c0, ch0, st, a0, wm0, mom10, mom20)
    st = exchange(st)
    dk0, dm0 = mix_grads(0, gcp, m0, gm, a0, mom10)
    gx, dr0, gn0 = last(n1, a0, st, mom10, wr0_full, gz0)

    own = lambda full: owner_sums(full, devices)
    deltas = [
        jnp.stack([own(dr0), own(dr1)]),
        jnp.stack([own(dm0), own(dm1)]),
        jnp.stack([own(dk0[:27].T), own(dk1[:27].T)]),
        jnp.stack([own(de0), own(de1)]),
    ]

    def mine(vec0, vec1, row):
        share = vec0.shape[1] // devices
        both = jnp.stack([vec0[row], vec1[row]])
        return lax.dynamic_slice_in_dim(both, rank * share, share, axis=1)

    for pair in ((gn0, gn1), (gd0, gd1), (gw0, gw1)):
        deltas.append(mine(pair[0], pair[1], 0))
        deltas.append(mine(pair[0], pair[1], 1))
    velocity = [MOMENTUM * momenta[i] + deltas[i] for i in range(10)]
    updated = [
        weights[i] - LEARN_RATE * (deltas[i] + MOMENTUM * velocity[i]) for i in range(10)
    ]
    return (out, pooled, gx, *deltas, *velocity, *updated)


def k_order(me_ref, slots_ref, out_ref):
    order_rows(slots_ref, out_ref, me_ref[0])


def gather_order(slots, rank, devices, wide):
    return pl.pallas_call(
        k_order,
        in_specs=[SM, VM],
        out_specs=VM,
        out_shape=jax.ShapeDtypeStruct((wide, slots.shape[2]), F32),
        compiler_params=params(12),
        name="order",
    )(rank.astype(jnp.int32)[None], slots)


def solution(mesh):
    field = P("dp", "fsdp", None, None)
    mat = P(None, AX, None)
    vec = P(None, AX)
    group = (mat,) * 4 + (vec,) * 6
    return jax.shard_map(
        body,
        mesh=mesh,
        in_specs=(field, field, P()) + group * 2,
        out_specs=(field, P(), field) + group * 3,
        check_vma=False,
    )
```

time: 2210 us -> 731 us (0.33)
  blocking collectives: 844 us -> 56.8 us
  waiting for transfers between devices: 847 us -> 124 us
  Pallas kernels: 0 us -> 184 us
  matrix products: 159 us -> 0.79 us
  starting transfers between devices: 35.9 us -> 164 us
  other arithmetic: 134 us -> 20.6 us
    reduce_scatter x4 -> x0, waiting for transfers between devices: 492 us -> none  [the longest x2 265 us: scatter_gradients(): lax.psum_scatter(expand_delta, ('dp', 'fsdp'), scatter_dimension=0, tiled...]
    psum x11 -> x0, blocking collectives: 433 us -> none  [the longest x6 231 us: batch_moments(): totals = lax.psum(jnp.sum(values, axis=0), ('dp', 'fsdp'))]
    unnamed x13 -> x2, waiting for transfers between devices: 265 us -> 0.03 us
    unnamed x6 -> x0, blocking collectives: 250 us -> none
    pallas_call x0 -> x18, Pallas kernels: none -> 184 us  [the longest x2 25.6 us: mix_grads(): pl.pallas_call(functools.partial(k_mix_grads, width), in_specs=[SM] + [VM...]
    all_gather x4 -> x0, blocking collectives: 161 us -> none  [the longest x2 82.5 us: gather_forward(): lax.all_gather(mixing_part, ('dp', 'fsdp'), axis=0, tiled=True)]
    dot_general x18 -> x1, matrix products: 145 us -> 0.79 us  [body(): jnp.dot(hot, pool[:, 0, :], precision=HIGHEST, preferred_element_type=F32)]
    reduce_sum x18 -> x10, other arithmetic: 89 us -> 5.7 us  [the longest x8 3.87 us: owner_sums(): return jnp.sum(lax.all_to_all(parts, AX, 0, 0), axis=0)]
  transfers between devices with their start and end apart: 27 -> 64, of which waited for: 12 -> 16; matrix products, arithmetic and copies ran while one was open for 14% -> 15% of each run, Pallas kernels for 0% -> 13%
where the time goes in v1:
time: 731 us; the launch traced here: 719 us
  Pallas kernels  184 us (25%)
  starting transfers between devices  164 us (22%)
  local copies, waits for them, and re-layouts  153 us (21%)
  waiting for transfers between devices  124 us (17%)
  blocking collectives  56.8 us (8%)
  other arithmetic  20.6 us (3%)
  between operations  15.9 us (2%)
    unnamed x257, local copies, waits for them, and re-layouts  120 us
    all_to_all x3, blocking collectives, owner_sums(): return jnp.sum(lax.all_to_all(parts, AX, 0, 0), axis=0)  56.8 us
    all_to_all x12, starting transfers between devices, exchange(): return lax.all_to_all(rows, AX, 0, 0)  50 us
    ppermute x6, waiting for transfers between devices, halo(): lax.ppermute(edge[0:1], AX, bwd)  39.4 us
    all_to_all x12, waiting for transfers between devices, exchange(): return lax.all_to_all(rows, AX, 0, 0)  36.3 us
    ppermute x12, starting transfers between devices, halo(): move = lambda value, step: lax.ppermute(value, AX, perm(step, shape))  32.7 us
    ppermute x6, starting transfers between devices, halo(): lax.ppermute(edge[frames - 1:], AX, fwd)  26.3 us
    pallas_call x2, Pallas kernels, mix_grads(): pl.pallas_call(functools.partial(k_mix_grads, width), in_specs=[SM] + [VM...  25.6 us
  transfers between devices with their start and end apart: 64, of which 16 were waited for; matrix products, arithmetic and copies ran while one was open for 15% of the time, Pallas kernels for 13%

profile of v1, /device:TPU:0, one launch (start us, length us, event | category | flops | bytes accessed | tf_op | source)
XLA Modules:
  0.0 719.3 jit_solution(12001294466535184083)
XLA Ops:
  31.3 9.6 %copy.110.x_ref = f32[4,14,28,1024]{3,2,1,0:T(8,128)} copy(f32[4,14,28,1024]{3,0,2,1:T(4,128)} %param.23) | data formatting | bytes 12845056 | tf_op args[0]
  70.5 8.3 %first.1 = (f32[4,14,32,256]{3,2,1,0:T(8,128)S(1)}, f32[32,4,128]{2,1,0:T(4,128)}) custom-call(s32[1]{0:T(128)} %bitcast.me_ref, f32[4,14,28,1024]{3,2,1,0:T(8,128)S(1)} %copy-done.2, f32[32,32,256]{2,1,0:T(8,128)S(1)} %constant_dynamic-update-slice_fusion.7.w_ref.slots_ref), custom_call_target="tpu_custom_call" | custom-call | flops 5637144576 | bytes 6422528 | tf_op jit(solution)/shard_map/first/pallas_call | solution.py:865
  84.8 4.7 collective-permute-start.10
  89.6 5.3 all-to-all-start
  94.9 10.4 %collective-permute-done.11 = f32[1,1,32,256]{3,2,1,0:T(8,128)S(1)} collective-permute-done((f32[1,1,32,256]{3,2,1,0:T(8,128)S(1)}, f32[1,1,32,256]{3,2,1,0:T(8,128)S(1)}, u32[]{:S(2)}, u32[]{:S(2)}) %collective-permute-start.11) | collective-permute-done | bytes 32800 | tf_op jit(solution)/shard_map/ppermute | solution.py:733
  111.3 11.2 %mix.2 = (f32[4,14,32,256]{3,2,1,0:T(8,128)S(1)}, f32[4,14,32,256]{3,2,1,0:T(8,128)S(1)}, f32[8,256]{1,0:T(8,128)S(1)}, f32[32,4,128]{2,1,0:T(4,128)}) custom-call(f32[15]{0:T(128)S(1)} %concatenate.56.keep_ref, f32[4,14,32,256]{3,2,1,0:T(8,128)S(1)} %copy-done.20, f32[1,14,32,256]{3,2,1,0:T(8,128)S(1)} %collective-permute-done.7.hp_ref, ...), custom_call_target="tpu_custom_call" | custom-call | flops 5637144576 | bytes 3670016 | tf_op jit(solution)/shard_map/mix/pallas_call | solution.py:878
  126.9 7.4 %all-to-all-done.2.st_in = f32[32,4,128]{2,1,0:T(4,128)S(1)} async-done(((f32[32,4,128]{2,1,0:T(4,128)}), f32[32,4,128]{2,1,0:T(4,128)S(1)}, u32[]{:S(2)}, u32[]{:S(2)}) %all-to-all-start.2) | async-done | bytes 65568 | tf_op jit(solution)/shard_map/all_to_all | solution.py:705
  135.6 8.9 %expand.2 = (f32[4,14,32,1024]{3,2,1,0:T(8,128)S(1)}, f32[8,256]{1,0:T(8,128)S(1)}, f32[8,1024]{1,0:T(8,128)S(1)}, f32[32,10,128]{2,1,0:T(8,128)}, f32[256,1024]{1,0:T(8,128)S(1)}) custom-call(s32[1]{0:T(128)} %bitcast.me_ref, f32[4,14,32,256]{3,2,1,0:T(8,128)S(1)} %get-tuple-element.96.c_ref, f32[32,4,128]{2,1,0:T(4,128)S(1)} %all-to-all-done.2.st_in, ...), custom_call_target="tpu_custom_call" | custom-call | flops 5637144576 | bytes 7340032 | tf_op jit(solution)/shard_map/expand/pallas_call | solution.py:893
  161.3 12.1 %join.1 = (f32[4,14,32,1024]{3,2,1,0:T(8,128)S(1)}, f32[4,14,32,256]{3,2,1,0:T(8,128)S(1)}, f32[8,1024]{1,0:T(8,128)S(1)}, f32[8,256]{1,0:T(8,128)S(1)}, f32[32,4,128]{2,1,0:T(4,128)}) custom-call(f32[4,14,32,1024]{3,2,1,0:T(8,128)} %copy-done.67, f32[4,14,28,1024]{3,2,1,0:T(8,128)} %copy.110.x_ref, f32[32,10,128]{2,1,0:T(8,128)S(1)} %all-to-all-done.3.st_in, ...), custom_call_target="tpu_custom_call" | custom-call | flops 5637144576 | bytes 22020096 | tf_op jit(solution)/shard_map/join/pallas_call | solution.py:907
  183.1 4.5 collective-permute-start.22
  187.6 5.4 all-to-all-start.4
  194.8 8.7 %collective-permute-done.23 = f32[1,1,32,256]{3,2,1,0:T(8,128)S(1)} collective-permute-done((f32[1,1,32,256]{3,2,1,0:T(8,128)S(1)}, f32[1,1,32,256]{3,2,1,0:T(8,128)S(1)}, u32[]{:S(2)}, u32[]{:S(2)}) %collective-permute-start.23) | collective-permute-done | bytes 32800 | tf_op jit(solution)/shard_map/ppermute | solution.py:733
  206.3 11.1 %mix.3 = (f32[4,14,32,256]{3,2,1,0:T(8,128)S(1)}, f32[4,14,32,256]{3,2,1,0:T(8,128)S(1)}, f32[8,256]{1,0:T(8,128)S(1)}, f32[32,4,128]{2,1,0:T(4,128)}) custom-call(f32[15]{0:T(128)S(1)} %concatenate.56.keep_ref, f32[4,14,32,256]{3,2,1,0:T(8,128)S(1)} %copy-done.25, f32[1,14,32,256]{3,2,1,0:T(8,128)S(1)} %collective-permute-done.19.hp_ref, ...), custom_call_target="tpu_custom_call" | custom-call | flops 5637144576 | bytes 3670016 | tf_op jit(solution)/shard_map/mix/pallas_call | solution.py:878
  223.2 6.0 all-to-all-done.5.st_in
  229.2 9.2 %expand.3 = (f32[4,14,32,1024]{3,2,1,0:T(8,128)S(1)}, f32[8,256]{1,0:T(8,128)S(1)}, f32[8,1024]{1,0:T(8,128)S(1)}, f32[32,10,128]{2,1,0:T(8,128)S(1)}, f32[256,1024]{1,0:T(8,128)}) custom-call(s32[1]{0:T(128)} %bitcast.me_ref, f32[4,14,32,256]{3,2,1,0:T(8,128)S(1)} %get-tuple-element.104.c_ref, f32[32,4,128]{2,1,0:T(4,128)S(1)} %all-to-all-done.5.st_in, ...), custom_call_target="tpu_custom_call" | custom-call | flops 5637144576 | bytes 7340032 | tf_op jit(solution)/shard_map/expand/pallas_call | solution.py:893
  244.9 9.6 %copy.128.cot_ref = f32[4,14,28,1024]{3,2,1,0:T(8,128)} copy(f32[4,14,28,1024]{3,0,2,1:T(4,128)} %param.24) | data formatting | bytes 12845056 | tf_op args[1]
  255.5 19.8 %turn.1 = (f32[4,14,28,1024]{3,2,1,0:T(8,128)}, f32[4,14,32,1024]{3,2,1,0:T(8,128)}, f32[4,14,32,256]{3,2,1,0:T(8,128)S(1)}, f32[256,1024]{1,0:T(8,128)S(1)}, f3...) custom-call(f32[4,14,32,1024]{3,2,1,0:T(8,128)} %copy-done.4, ...), custom_call_target="tpu_custom_call" | custom-call | flops 5637144576 | bytes 36700160 | tf_op jit(solution)/shard_map/turn/pallas_call | solution.py:929
  278.9 5.0 all-to-all-start.7
  284.9 4.4 collective-permute-start.29
  294.0 5.9 collective-permute-start.32
  301.4 5.2 second.2
  311.4 4.2 collective-permute-start.24
  318.9 17.6 %collective-permute-done.28 = f32[1,1,32,256]{3,2,1,0:T(8,128)S(1)} collective-permute-done((f32[1,1,32,256]{3,2,1,0:T(8,128)S(1)}, f32[1,1,32,256]{3,2,1,0:T(8,128)S(1)}, u32[]{:S(2)}, u32[]{:S(2)}) %collective-permute-start.28) | collective-permute-done | bytes 32800 | tf_op jit(solution)/shard_map/ppermute | solution.py:733
  338.7 7.6 %all-to-all-start.8 = ((f32[32,4,128]{2,1,0:T(4,128)}), f32[32,4,128]{2,1,0:T(4,128)S(1)}, u32[]{:S(2)}, u32[]{:S(2)}) async-start(f32[32,4,128]{2,1,0:T(4,128)} %get-tuple-element.118), calls=%async_computation.8 | async-start | bytes 131072 | tf_op jit(solution)/shard_map/all_to_all | solution.py:705
  348.8 4.9 all-to-all-done.8.st_in
  356.7 10.7 %first_back.2 = (f32[4,14,32,256]{3,2,1,0:T(8,128)S(1)}, f32[4,14,32,256]{3,2,1,0:T(8,128)S(1)}, f32[6,16,32,256]{3,2,1,0:T(8,128)}, f32[8,256]{1,0:T(8,128)S(1)}, f32[32,4,128]{2,1,0:T(4,128)}) custom-call(f32[15]{0:T(128)S(1)} %copy-done.60, f32[4,14,32,256]{3,2,1,0:T(8,128)S(1)} %copy-done.31, f32[1,14,32,256]{3,2,1,0:T(8,128)} %collective-permute-done.24.np_ref, ...), custom_call_target="tpu_custom_call" | custom-call | flops 5637144576 | bytes 7340032 | tf_op jit(solution)/shard_map/first_back/pallas_call | solution.py:968
  374.2 5.8 all-to-all-done.9.st_in
  380.6 25.5 %between.1 = (f32[4,14,32,1024]{3,2,1,0:T(8,128)}, f32[4,14,32,256]{3,2,1,0:T(8,128)}, f32[256,1024]{1,0:T(8,128)}, f32[1024,256]{1,0:T(8,128)}, f32[8,256]{1,0:T(8,128)}, /*index=5*/f32[32,16,128]{2,1,0:T(8,128)}) custom-call(f32[4,14,32,256]{3,2,1,0:T(8,128)} %copy-done.79, f32[4,14,32,256]{3,2,1,0:T(8,128)} %copy-done.24, f32[32,4,128]{2,1,0:T(4,128)} %copy-done.92, ...), custom_call_target="tpu_custom_call" | custom-call | flops 11274289152 | bytes 22020096 | tf_op jit(solution)/shard_map/between/pallas_call | solution.py:997
  410.8 4.3 collective-permute-start.42
  417.4 5.2 collective-permute-start.39
  431.3 5.2 second.3
  440.8 5.9 collective-permute-start.34
  448.1 4.8 collective-permute-start.37
  452.9 13.1 %mix_grads.3 = (f32[32,256]{1,0:T(8,128)S(1)}, f32[256,256]{1,0:T(8,128)}) custom-call(f32[15]{0:T(128)S(1)} %copy-done.61, f32[6,16,32,256]{3,2,1,0:T(8,128)S(1)} %copy-done.69, f32[4,14,32,256]{3,2,1,0:T(8,128)S(1)} %copy-done.74, f32[4,14,32,256]{3,2,1,0:T(8,128)S(1)} %copy-done.76, f32[4,14,32,256]{3,2,1,0:T(8,128)S(1)} %copy-done.27, ...), custom_call_target="tpu_custom_call" | custom-call | flops 5637144576 | bytes 7340032 | tf_op jit(solution)/shard_map/mix_grads/pallas_call | solution.py:981
  466.0 7.2 %all-to-all-start.11 = ((f32[32,4,128]{2,1,0:T(4,128)}), f32[32,4,128]{2,1,0:T(4,128)S(1)}, u32[]{:S(2)}, u32[]{:S(2)}) async-start(f32[32,4,128]{2,1,0:T(4,128)} %get-tuple-element.129), calls=%async_computation.11 | async-start | bytes 131072 | tf_op jit(solution)/shard_map/all_to_all | solution.py:705
  476.8 3.9 all-to-all-done.11.st_in
  488.1 10.7 %first_back.3 = (f32[4,14,32,256]{3,2,1,0:T(8,128)S(1)}, f32[4,14,32,256]{3,2,1,0:T(8,128)S(1)}, f32[6,16,32,256]{3,2,1,0:T(8,128)}, f32[8,256]{1,0:T(8,128)S(1)}, f32[32,4,128]{2,1,0:T(4,128)}) custom-call(f32[15]{0:T(128)S(1)} %copy-done.61, f32[4,14,32,256]{3,2,1,0:T(8,128)S(1)} %copy-done.29, f32[1,14,32,256]{3,2,1,0:T(8,128)} %collective-permute-done.34.np_ref, ...), custom_call_target="tpu_custom_call" | custom-call | flops 5637144576 | bytes 7340032 | tf_op jit(solution)/shard_map/first_back/pallas_call | solution.py:968
  501.3 6.1 all-to-all-start.16
  513.8 12.5 %mix_grads.2 = (f32[32,256]{1,0:T(8,128)S(1)}, f32[256,256]{1,0:T(8,128)S(1)}) custom-call(f32[15]{0:T(128)S(1)} %copy-done.61, f32[6,16,32,256]{3,2,1,0:T(8,128)S(1)} %copy-done.70, f32[4,14,32,256]{3,2,1,0:T(8,128)S(1)} %copy-done.72, f32[4,14,32,256]{3,2,1,0:T(8,128)S(1)} %copy-done.78, f32[4,14,32,256]{3,2,1,0:T(8,128)S(1)} %copy-done.22, ...), custom_call_target="tpu_custom_call" | custom-call | flops 5637144576 | bytes 7340032 | tf_op jit(solution)/shard_map/mix_grads/pallas_call | solution.py:981
  528.1 12.9 %all_to_all.105 = f32[32,1,216]{2,1,0:T(1,128)} all-to-all(f32[32,1,216]{2,1,0:T(1,128)S(1)} %reshape.196), channel_id=1, replica_groups=mesh['dp'=16,'fsdp'=2] {'dp','fsdp'}, dimensions={0} | all-to-all | bytes 55296 | tf_op jit(solution)/shard_map/all_to_all | solution.py:759
  551.0 29.7 %all_to_all.106 = f32[32,8,1024]{2,1,0:T(8,128)} all-to-all(f32[32,8,1024]{2,1,0:T(8,128)} %bitcast.96), channel_id=1, replica_groups=mesh['dp'=16,'fsdp'=2] {'dp','fsdp'}, dimensions={0} | all-to-all | bytes 2097152 | tf_op jit(solution)/shard_map/all_to_all | solution.py:759
  580.8 14.1 %all_to_all.107 = f32[32,8,256]{2,1,0:T(8,128)} all-to-all(f32[32,8,256]{2,1,0:T(8,128)S(1)} %bitcast.97), channel_id=1, replica_groups=mesh['dp'=16,'fsdp'=2] {'dp','fsdp'}, dimensions={0} | all-to-all | bytes 524288 | tf_op jit(solution)/shard_map/all_to_all | solution.py:759
  603.2 21.2 %all-to-all-done.14 = f32[32,32,256]{2,1,0:T(8,128)} async-done(((f32[32,32,256]{2,1,0:T(8,128)}), f32[32,32,256]{2,1,0:T(8,128)}, u32[]{:S(2)}, u32[]{:S(2)}) %all-to-all-start.14) | async-done | bytes 1048608 | tf_op jit(solution)/shard_map/all_to_all | solution.py:759
  629.0 10.2 %copy.132 = f32[4,14,28,1024]{3,0,2,1:T(4,128)} copy(f32[4,14,28,1024]{3,2,1,0:T(8,128)} %get-tuple-element.254) | data formatting | bytes 12845056
  646.3 13.6 %last.1 = (f32[4,14,28,1024]{3,2,1,0:T(8,128)}, f32[1024,256]{1,0:T(8,128)}, f32[8,256]{1,0:T(8,128)S(1)}) custom-call(f32[4,14,32,256]{3,2,1,0:T(8,128)S(1)} %copy-done.66, f32[4,14,32,256]{3,2,1,0:T(8,128)S(1)} %copy-done.23, f32[32,4,128]{2,1,0:T(4,128)S(1)} %all-to-all-done.12.st_in, f32[8,256]{1,0:T(8,128)S(1)} %copy-done.42, f32[8,256]{1,0:T(8,128)S(1)} %copy-done.81, ...), custom_call_target="tpu_custom_call" | custom-call | flops 5637144576 | bytes 22020096 | tf_op jit(solution)/shard_map/last/pallas_call | solution.py:1013
  660.0 5.9 all-to-all-start.13
  668.9 10.1 %copy.133 = f32[4,14,28,1024]{3,0,2,1:T(4,128)} copy(f32[4,14,28,1024]{3,2,1,0:T(8,128)} %get-tuple-element.256) | data formatting | bytes 12845056
  679.7 25.2 %all-gather.7.cloned.1.call-done = f32[32,10,1024]{2,1,0:T(8,128)} async-done(((f32[1,10,1024]{2,1,0:T(8,128)}), f32[32,10,1024]{2,1,0:T(8,128)}) %all-gather.7.cloned.1.call-update) | async-done | bytes 1310736 | tf_op jit(solution)/shard_map/all_gather | solution.py:1041
  (478 shorter events, 232.5 us)
Async XLA Ops:
  8.6 32.4 %collective-permute-start = (f32[1,32,256]{2,1,0:T(8,128)S(1)}, f32[1,32,256]{2,1,0:T(8,128)S(1)}, u32[]{:S(2)}, u32[]{:S(2)}) collective-permute-start(f32[1,32,256]{2,1,0:T(8,128)S(1)} %get-tuple-element.370), channel_id=1, source_target_pairs={{0,8},{1,9},{2,10},{3,11},{4,12},{5,13},{6,14},{7,15},{8,0},{9,1},... | collective-permute-start | bytes 98312 | tf_op jit(solution)/shard_map/ppermute | solution.py:752
  11.6 33.1 %collective-permute-start.1 = (f32[1,32,256]{2,1,0:T(8,128)S(1)}, f32[1,32,256]{2,1,0:T(8,128)S(1)}, u32[]{:S(2)}, u32[]{:S(2)}) collective-permute-start(f32[1,32,256]{2,1,0:T(8,128)S(1)} %get-tuple-element.370), channel_id=1, source_target_pairs={{0,16},{1,17},{2,18},{3,19},{4,20},{5,21},{6,22},{7,23},{8,24},{9,... | collective-permute-start | bytes 98312 | tf_op jit(solution)/shard_map/ppermute | solution.py:752
  14.2 30.5 %collective-permute-start.2 = (f32[1,32,256]{2,1,0:T(8,128)S(1)}, f32[1,32,256]{2,1,0:T(8,128)S(1)}, u32[]{:S(2)}, u32[]{:S(2)}) collective-permute-start(f32[1,32,256]{2,1,0:T(8,128)S(1)} %get-tuple-element.370), channel_id=1, source_target_pairs={{0,24},{1,25},{2,26},{3,27},{4,28},{5,29},{6,30},{7,31},{8,16},{9,... | collective-permute-start | bytes 98312 | tf_op jit(solution)/shard_map/ppermute | solution.py:752
  15.7 34.5 %collective-permute-start.12 = (f32[1,8,1280]{2,1,0:T(8,128)S(1)}, f32[1,8,1280]{2,1,0:T(8,128)S(1)}, u32[]{:S(2)}, u32[]{:S(2)}) collective-permute-start(f32[1,8,1280]{2,1,0:T(8,128)S(1)} %maximum_bitcast_fusion.1), channel_id=1, source_target_pairs={{0,8},{1,9},{2,10},{3,11},{4,12},{5,13},{6,14},{7,15},{8,0},{9,1},... | collective-permute-start | bytes 122888 | tf_op jit(solution)/shard_map/ppermute | solution.py:752
  16.6 34.1 %collective-permute-start.13 = (f32[1,8,1280]{2,1,0:T(8,128)S(1)}, f32[1,8,1280]{2,1,0:T(8,128)S(1)}, u32[]{:S(2)}, u32[]{:S(2)}) collective-permute-start(f32[1,8,1280]{2,1,0:T(8,128)S(1)} %maximum_bitcast_fusion.1), channel_id=1, source_target_pairs={{0,16},{1,17},{2,18},{3,19},{4,20},{5,21},{6,22},{7,23},{8,24},{9,... | collective-permute-start | bytes 122888 | tf_op jit(solution)/shard_map/ppermute | solution.py:752
  26.2 29.4 %all-to-all-start.1 = ((f32[32,5,128]{2,1,0:T(8,128)}), f32[32,5,128]{2,1,0:T(8,128)S(1)}, u32[]{:S(2)}, u32[]{:S(2)}) async-start(f32[32,5,128]{2,1,0:T(8,128)} %broadcast_in_dim.42), calls=%async_computation.1 | async-start | bytes 262144 | tf_op jit(solution)/shard_map/all_to_all | solution.py:782
  29.0 121.7 %all-gather.5.cloned.1.call-start = ((), (), s32[]{:S(2)}) async-start(), calls=%async_computation.21 | async-start | bytes 2703360 | tf_op jit(solution)/shard_map/all_gather | solution.py:839
  46.8 13.0 %collective-permute-start.4 = (f32[4,32,256]{2,1,0:T(8,128)}, f32[4,32,256]{2,1,0:T(8,128)}, u32[]{:S(2)}, u32[]{:S(2)}) collective-permute-start(f32[4,32,256]{2,1,0:T(8,128)} %pad_maximum_fusion.1), channel_id=1, source_target_pairs={{0,4},{1,5},{2,6},{3,7},{4,0},{5,1},{6,2},{7,3},{8,12},{9,13},{10,... | collective-permute-start | bytes 393224 | tf_op jit(solution)/shard_map/ppermute | solution.py:752
  66.9 39.3 %collective-permute-start.18 = (f32[16,8,1280]{2,1,0:T(8,128)}, f32[16,8,1280]{2,1,0:T(8,128)}, u32[]{:S(2)}, u32[]{:S(2)}) collective-permute-start(f32[16,8,1280]{2,1,0:T(8,128)} %get-tuple-element.333), channel_id=1, source_target_pairs={{0,1},{1,0},{2,3},{3,2},{4,5},{5,4},{6,7},{7,6},{8,9},{9,8},{10,11... | collective-permute-start | bytes 1966088 | tf_op jit(solution)/shard_map/ppermute | solution.py:752
  79.7 28.7 %collective-permute-start.7 = (f32[1,14,32,256]{3,2,1,0:T(8,128)}, f32[1,14,32,256]{3,2,1,0:T(8,128)S(1)}, u32[]{:S(2)}, u32[]{:S(2)}) collective-permute-start(f32[1,14,32,256]{3,2,1,0:T(8,128)} %get-tuple-element.332), channel_id=1, source_target_pairs={{0,2},{1,3},{2,4},{3,5},{4,6},{5,7},{6,8},{7,9},{8,10},{9,11},{10,... | collective-permute-start | bytes 1376264 | tf_op jit(solution)/shard_map/ppermute | solution.py:722
  82.2 26.3 %collective-permute-start.8 = (f32[1,14,32,256]{3,2,1,0:T(8,128)S(1)}, f32[1,14,32,256]{3,2,1,0:T(8,128)S(1)}, u32[]{:S(2)}, u32[]{:S(2)}) collective-permute-start(f32[1,14,32,256]{3,2,1,0:T(8,128)S(1)} %get-tuple-element.331), channel_id=1, source_target_pairs={{2,0},{3,1},{4,2},{5,3},{6,4},{7,5},{8,6},{9,7},{10,8},{11,9},{12,... | collective-permute-start | bytes 1376264 | tf_op jit(solution)/shard_map/ppermute | solution.py:722
  83.5 21.8 %collective-permute-start.11 = (f32[1,1,32,256]{3,2,1,0:T(8,128)S(1)}, f32[1,1,32,256]{3,2,1,0:T(8,128)S(1)}, u32[]{:S(2)}, u32[]{:S(2)}) collective-permute-start(f32[1,1,32,256]{3,2,1,0:T(8,128)S(1)} %get-tuple-element.350), channel_id=1, source_target_pairs={{2,1},{3,0},{4,3},{5,2},{6,5},{7,4},{8,7},{9,6},{10,9},{11,8},{12,... | collective-permute-start | bytes 98312 | tf_op jit(solution)/shard_map/ppermute | solution.py:733
  84.8 21.4 %collective-permute-start.10 = (f32[1,1,32,256]{3,2,1,0:T(8,128)S(1)}, f32[1,1,32,256]{3,2,1,0:T(8,128)S(1)}, u32[]{:S(2)}, u32[]{:S(2)}) collective-permute-start(f32[1,1,32,256]{3,2,1,0:T(8,128)S(1)} %get-tuple-element.349), channel_id=1, source_target_pairs={{0,3},{1,2},{2,5},{3,4},{4,7},{5,6},{6,9},{7,8},{8,11},{9,10},{10,... | collective-permute-start | bytes 98312 | tf_op jit(solution)/shard_map/ppermute | solution.py:733
  89.6 18.8 %all-to-all-start = ((f32[32,4,128]{2,1,0:T(4,128)}), f32[32,4,128]{2,1,0:T(4,128)S(1)}, u32[]{:S(2)}, u32[]{:S(2)}) async-start(f32[32,4,128]{2,1,0:T(4,128)} %get-tuple-element.95), calls=%async_computation | async-start | bytes 131072 | tf_op jit(solution)/shard_map/all_to_all | solution.py:705
  148.1 13.2 %all-to-all-start.3 = ((f32[32,10,128]{2,1,0:T(8,128)}), f32[32,10,128]{2,1,0:T(8,128)S(1)}, u32[]{:S(2)}, u32[]{:S(2)}) async-start(f32[32,10,128]{2,1,0:T(8,128)} %get-tuple-element.99), calls=%async_computation.3 | async-start | bytes 524288 | tf_op jit(solution)/shard_map/all_to_all | solution.py:705
  177.7 27.1 %collective-permute-start.21 = (f32[4,1,32,256]{3,2,1,0:T(8,128)S(1)}, f32[4,1,32,256]{3,2,1,0:T(8,128)S(1)}, u32[]{:S(2)}, u32[]{:S(2)}) collective-permute-start(f32[4,1,32,256]{3,2,1,0:T(8,128)S(1)} %slice_select_fusion.4), channel_id=1, source_target_pairs={{0,1},{1,0},{2,3},{3,2},{4,5},{5,4},{6,7},{7,6},{8,9},{9,8},{10,11... | collective-permute-start | bytes 393224 | tf_op jit(solution)/shard_map/ppermute | solution.py:729
  177.8 27.0 %collective-permute-start.19 = (f32[1,14,32,256]{3,2,1,0:T(8,128)S(1)}, f32[1,14,32,256]{3,2,1,0:T(8,128)S(1)}, u32[]{:S(2)}, u32[]{:S(2)}) collective-permute-start(f32[1,14,32,256]{3,2,1,0:T(8,128)S(1)} %get-tuple-element.330), channel_id=1, source_target_pairs={{0,2},{1,3},{2,4},{3,5},{4,6},{5,7},{6,8},{7,9},{8,10},{9,11},{10,... | collective-permute-start | bytes 1376264 | tf_op jit(solution)/shard_map/ppermute | solution.py:722
  180.5 24.3 %collective-permute-start.20 = (f32[1,14,32,256]{3,2,1,0:T(8,128)S(1)}, f32[1,14,32,256]{3,2,1,0:T(8,128)S(1)}, u32[]{:S(2)}, u32[]{:S(2)}) collective-permute-start(f32[1,14,32,256]{3,2,1,0:T(8,128)S(1)} %get-tuple-element.329), channel_id=1, source_target_pairs={{2,0},{3,1},{4,2},{5,3},{6,4},{7,5},{8,6},{9,7},{10,8},{11,9},{12,... | collective-permute-start | bytes 1376264 | tf_op jit(solution)/shard_map/ppermute | solution.py:722
  181.8 21.7 %collective-permute-start.23 = (f32[1,1,32,256]{3,2,1,0:T(8,128)S(1)}, f32[1,1,32,256]{3,2,1,0:T(8,128)S(1)}, u32[]{:S(2)}, u32[]{:S(2)}) collective-permute-start(f32[1,1,32,256]{3,2,1,0:T(8,128)S(1)} %get-tuple-element.348), channel_id=1, source_target_pairs={{2,1},{3,0},{4,3},{5,2},{6,5},{7,4},{8,7},{9,6},{10,9},{11,8},{12,... | collective-permute-start | bytes 98312 | tf_op jit(solution)/shard_map/ppermute | solution.py:733
  183.1 20.4 %collective-permute-start.22 = (f32[1,1,32,256]{3,2,1,0:T(8,128)S(1)}, f32[1,1,32,256]{3,2,1,0:T(8,128)S(1)}, u32[]{:S(2)}, u32[]{:S(2)}) collective-permute-start(f32[1,1,32,256]{3,2,1,0:T(8,128)S(1)} %get-tuple-element.347), channel_id=1, source_target_pairs={{0,3},{1,2},{2,5},{3,4},{4,7},{5,6},{6,9},{7,8},{8,11},{9,10},{10,... | collective-permute-start | bytes 98312 | tf_op jit(solution)/shard_map/ppermute | solution.py:733
  187.6 17.2 %all-to-all-start.4 = ((f32[32,4,128]{2,1,0:T(4,128)}), f32[32,4,128]{2,1,0:T(4,128)S(1)}, u32[]{:S(2)}, u32[]{:S(2)}) async-start(f32[32,4,128]{2,1,0:T(4,128)} %get-tuple-element.103), calls=%async_computation.4 | async-start | bytes 131072 | tf_op jit(solution)/shard_map/all_to_all | solution.py:705
  242.1 13.4 %all-to-all-start.6 = ((f32[32,10,128]{2,1,0:T(8,128)}), f32[32,10,128]{2,1,0:T(8,128)S(1)}, u32[]{:S(2)}, u32[]{:S(2)}) async-start(f32[32,10,128]{2,1,0:T(8,128)} %copy-done.33), calls=%async_computation.6 | async-start | bytes 524288 | tf_op jit(solution)/shard_map/all_to_all | solution.py:705
  278.9 21.0 %all-to-all-start.7 = ((f32[32,16,128]{2,1,0:T(8,128)}), f32[32,16,128]{2,1,0:T(8,128)S(1)}, u32[]{:S(2)}, u32[]{:S(2)}) async-start(f32[32,16,128]{2,1,0:T(8,128)} %copy-done.32), calls=%async_computation.7 | async-start | bytes 524288 | tf_op jit(solution)/shard_map/all_to_all | solution.py:705
  284.9 63.9 %collective-permute-start.29 = (f32[1,14,32,256]{3,2,1,0:T(8,128)}, f32[1,14,32,256]{3,2,1,0:T(8,128)}, u32[]{:S(2)}, u32[]{:S(2)}) collective-permute-start(f32[1,14,32,256]{3,2,1,0:T(8,128)} %get-tuple-element.326), channel_id=1, source_target_pairs={{0,2},{1,3},{2,4},{3,5},{4,6},{5,7},{6,8},{7,9},{8,10},{9,11},{10,... | collective-permute-start | bytes 1376264 | tf_op jit(solution)/shard_map/ppermute | solution.py:722
  289.3 59.5 %collective-permute-start.30 = (f32[1,14,32,256]{3,2,1,0:T(8,128)}, f32[1,14,32,256]{3,2,1,0:T(8,128)}, u32[]{:S(2)}, u32[]{:S(2)}) collective-permute-start(f32[1,14,32,256]{3,2,1,0:T(8,128)} %get-tuple-element.325), channel_id=1, source_target_pairs={{2,0},{3,1},{4,2},{5,3},{6,4},{7,5},{8,6},{9,7},{10,8},{11,9},{12,... | collective-permute-start | bytes 1376264 | tf_op jit(solution)/shard_map/ppermute | solution.py:722
  291.3 26.4 %collective-permute-start.31 = (f32[4,1,32,256]{3,2,1,0:T(8,128)}, f32[4,1,32,256]{3,2,1,0:T(8,128)}, u32[]{:S(2)}, u32[]{:S(2)}) collective-permute-start(f32[4,1,32,256]{3,2,1,0:T(8,128)} %slice_select_fusion.2), channel_id=1, source_target_pairs={{0,1},{1,0},{2,3},{3,2},{4,5},{5,4},{6,7},{7,6},{8,9},{9,8},{10,11... | collective-permute-start | bytes 393224 | tf_op jit(solution)/shard_map/ppermute | solution.py:729
  292.7 18.7 %collective-permute-start.33 = (f32[1,1,32,256]{3,2,1,0:T(8,128)}, f32[1,1,32,256]{3,2,1,0:T(8,128)S(1)}, u32[]{:S(2)}, u32[]{:S(2)}) collective-permute-start(f32[1,1,32,256]{3,2,1,0:T(8,128)} %get-tuple-element.344), channel_id=1, source_target_pairs={{2,1},{3,0},{4,3},{5,2},{6,5},{7,4},{8,7},{9,6},{10,9},{11,8},{12,... | collective-permute-start | bytes 98312 | tf_op jit(solution)/shard_map/ppermute | solution.py:733
  294.0 21.6 %collective-permute-start.32 = (f32[1,1,32,256]{3,2,1,0:T(8,128)}, f32[1,1,32,256]{3,2,1,0:T(8,128)}, u32[]{:S(2)}, u32[]{:S(2)}) collective-permute-start(f32[1,1,32,256]{3,2,1,0:T(8,128)} %get-tuple-element.343), channel_id=1, source_target_pairs={{0,3},{1,2},{2,5},{3,4},{4,7},{5,6},{6,9},{7,8},{8,11},{9,10},{10,... | collective-permute-start | bytes 98312 | tf_op jit(solution)/shard_map/ppermute | solution.py:733
  311.4 42.3 %collective-permute-start.24 = (f32[1,14,32,256]{3,2,1,0:T(8,128)}, f32[1,14,32,256]{3,2,1,0:T(8,128)}, u32[]{:S(2)}, u32[]{:S(2)}) collective-permute-start(f32[1,14,32,256]{3,2,1,0:T(8,128)} %get-tuple-element.328), channel_id=1, source_target_pairs={{0,2},{1,3},{2,4},{3,5},{4,6},{5,7},{6,8},{7,9},{8,10},{9,11},{10,... | collective-permute-start | bytes 1376264 | tf_op jit(solution)/shard_map/ppermute | solution.py:722
  315.6 38.1 %collective-permute-start.25 = (f32[1,14,32,256]{3,2,1,0:T(8,128)}, f32[1,14,32,256]{3,2,1,0:T(8,128)}, u32[]{:S(2)}, u32[]{:S(2)}) collective-permute-start(f32[1,14,32,256]{3,2,1,0:T(8,128)} %get-tuple-element.327), channel_id=1, source_target_pairs={{2,0},{3,1},{4,2},{5,3},{6,4},{7,5},{8,6},{9,7},{10,8},{11,9},{12,... | collective-permute-start | bytes 1376264 | tf_op jit(solution)/shard_map/ppermute | solution.py:722
  317.6 18.9 %collective-permute-start.28 = (f32[1,1,32,256]{3,2,1,0:T(8,128)S(1)}, f32[1,1,32,256]{3,2,1,0:T(8,128)S(1)}, u32[]{:S(2)}, u32[]{:S(2)}) collective-permute-start(f32[1,1,32,256]{3,2,1,0:T(8,128)S(1)} %get-tuple-element.346), channel_id=1, source_target_pairs={{2,1},{3,0},{4,3},{5,2},{6,5},{7,4},{8,7},{9,6},{10,9},{11,8},{12,... | collective-permute-start | bytes 98312 | tf_op jit(solution)/shard_map/ppermute | solution.py:733
  338.7 15.0 %all-to-all-start.8 = ((f32[32,4,128]{2,1,0:T(4,128)}), f32[32,4,128]{2,1,0:T(4,128)S(1)}, u32[]{:S(2)}, u32[]{:S(2)}) async-start(f32[32,4,128]{2,1,0:T(4,128)} %get-tuple-element.118), calls=%async_computation.8 | async-start | bytes 131072 | tf_op jit(solution)/shard_map/all_to_all | solution.py:705
  406.1 18.8 %all-to-all-start.10 = ((f32[32,16,128]{2,1,0:T(8,128)}), f32[32,16,128]{2,1,0:T(8,128)S(1)}, u32[]{:S(2)}, u32[]{:S(2)}) async-start(f32[32,16,128]{2,1,0:T(8,128)} %get-tuple-element.127), calls=%async_computation.10 | async-start | bytes 524288 | tf_op jit(solution)/shard_map/all_to_all | solution.py:705
  409.5 14.4 %collective-permute-start.43 = (f32[1,1,32,256]{3,2,1,0:T(8,128)S(1)}, f32[1,1,32,256]{3,2,1,0:T(8,128)S(1)}, u32[]{:S(2)}, u32[]{:S(2)}) collective-permute-start(f32[1,1,32,256]{3,2,1,0:T(8,128)S(1)} %get-tuple-element.340), channel_id=1, source_target_pairs={{2,1},{3,0},{4,3},{5,2},{6,5},{7,4},{8,7},{9,6},{10,9},{11,8},{12,... | collective-permute-start | bytes 98312 | tf_op jit(solution)/shard_map/ppermute | solution.py:733
  410.8 13.1 %collective-permute-start.42 = (f32[1,1,32,256]{3,2,1,0:T(8,128)S(1)}, f32[1,1,32,256]{3,2,1,0:T(8,128)S(1)}, u32[]{:S(2)}, u32[]{:S(2)}) collective-permute-start(f32[1,1,32,256]{3,2,1,0:T(8,128)S(1)} %get-tuple-element.339), channel_id=1, source_target_pairs={{0,3},{1,2},{2,5},{3,4},{4,7},{5,6},{6,9},{7,8},{8,11},{9,10},{10,... | collective-permute-start | bytes 98312 | tf_op jit(solution)/shard_map/ppermute | solution.py:733
  417.3 29.5 %collective-permute-start.41 = (f32[4,1,32,256]{3,2,1,0:T(8,128)}, f32[4,1,32,256]{3,2,1,0:T(8,128)}, u32[]{:S(2)}, u32[]{:S(2)}) collective-permute-start(f32[4,1,32,256]{3,2,1,0:T(8,128)} %slice_select_fusion), channel_id=1, source_target_pairs={{0,1},{1,0},{2,3},{3,2},{4,5},{5,4},{6,7},{7,6},{8,9},{9,8},{10,11... | collective-permute-start | bytes 393224 | tf_op jit(solution)/shard_map/ppermute | solution.py:729
  417.4 66.2 %collective-permute-start.39 = (f32[1,14,32,256]{3,2,1,0:T(8,128)}, f32[1,14,32,256]{3,2,1,0:T(8,128)}, u32[]{:S(2)}, u32[]{:S(2)}) collective-permute-start(f32[1,14,32,256]{3,2,1,0:T(8,128)} %get-tuple-element.322), channel_id=1, source_target_pairs={{0,2},{1,3},{2,4},{3,5},{4,6},{5,7},{6,8},{7,9},{8,10},{9,11},{10,... | collective-permute-start | bytes 1376264 | tf_op jit(solution)/shard_map/ppermute | solution.py:722
  422.6 60.9 %collective-permute-start.40 = (f32[1,14,32,256]{3,2,1,0:T(8,128)}, f32[1,14,32,256]{3,2,1,0:T(8,128)}, u32[]{:S(2)}, u32[]{:S(2)}) collective-permute-start(f32[1,14,32,256]{3,2,1,0:T(8,128)} %get-tuple-element.321), channel_id=1, source_target_pairs={{2,0},{3,1},{4,2},{5,3},{6,4},{7,5},{8,6},{9,7},{10,8},{11,9},{12,... | collective-permute-start | bytes 1376264 | tf_op jit(solution)/shard_map/ppermute | solution.py:722
  440.8 42.7 %collective-permute-start.34 = (f32[1,14,32,256]{3,2,1,0:T(8,128)}, f32[1,14,32,256]{3,2,1,0:T(8,128)}, u32[]{:S(2)}, u32[]{:S(2)}) collective-permute-start(f32[1,14,32,256]{3,2,1,0:T(8,128)} %get-tuple-element.324), channel_id=1, source_target_pairs={{0,2},{1,3},{2,4},{3,5},{4,6},{5,7},{6,8},{7,9},{8,10},{9,11},{10,... | collective-permute-start | bytes 1376264 | tf_op jit(solution)/shard_map/ppermute | solution.py:722
  446.8 36.8 %collective-permute-start.35 = (f32[1,14,32,256]{3,2,1,0:T(8,128)}, f32[1,14,32,256]{3,2,1,0:T(8,128)}, u32[]{:S(2)}, u32[]{:S(2)}) collective-permute-start(f32[1,14,32,256]{3,2,1,0:T(8,128)} %get-tuple-element.323), channel_id=1, source_target_pairs={{2,0},{3,1},{4,2},{5,3},{6,4},{7,5},{8,6},{9,7},{10,8},{11,9},{12,... | collective-permute-start | bytes 1376264 | tf_op jit(solution)/shard_map/ppermute | solution.py:722
  448.1 25.2 %collective-permute-start.37 = (f32[1,1,32,256]{3,2,1,0:T(8,128)}, f32[1,1,32,256]{3,2,1,0:T(8,128)}, u32[]{:S(2)}, u32[]{:S(2)}) collective-permute-start(f32[1,1,32,256]{3,2,1,0:T(8,128)} %get-tuple-element.341), channel_id=1, source_target_pairs={{0,3},{1,2},{2,5},{3,4},{4,7},{5,6},{6,9},{7,8},{8,11},{9,10},{10,... | collective-permute-start | bytes 98312 | tf_op jit(solution)/shard_map/ppermute | solution.py:733
  466.0 14.7 %all-to-all-start.11 = ((f32[32,4,128]{2,1,0:T(4,128)}), f32[32,4,128]{2,1,0:T(4,128)S(1)}, u32[]{:S(2)}, u32[]{:S(2)}) async-start(f32[32,4,128]{2,1,0:T(4,128)} %get-tuple-element.129), calls=%async_computation.11 | async-start | bytes 131072 | tf_op jit(solution)/shard_map/all_to_all | solution.py:705
  480.7 20.6 %all-to-all-start.18 = ((f32[32,1,216]{2,1,0:T(1,128)}), f32[32,1,216]{2,1,0:T(1,128)S(1)}, u32[]{:S(2)}, u32[]{:S(2)}) async-start(f32[32,1,216]{2,1,0:T(1,128)} %reshape.194), calls=%async_computation.18 | async-start | bytes 65536 | tf_op jit(solution)/shard_map/all_to_all | solution.py:759
  501.3 26.8 %all-to-all-start.16 = ((f32[32,8,256]{2,1,0:T(8,128)}), f32[32,8,256]{2,1,0:T(8,128)}, u32[]{:S(2)}, u32[]{:S(2)}) async-start(f32[32,8,256]{2,1,0:T(8,128)} %bitcast.34), calls=%async_computation.16 | async-start | bytes 524288 | tf_op jit(solution)/shard_map/all_to_all | solution.py:759
  594.9 29.6 %all-to-all-start.14 = ((f32[32,32,256]{2,1,0:T(8,128)}), f32[32,32,256]{2,1,0:T(8,128)}, u32[]{:S(2)}, u32[]{:S(2)}) async-start(f32[32,32,256]{2,1,0:T(8,128)} %bitcast.101), calls=%async_computation.14 | async-start | bytes 2097152 | tf_op jit(solution)/shard_map/all_to_all | solution.py:759
  624.5 35.6 %all-to-all-start.19 = ((f32[32,8,1024]{2,1,0:T(8,128)}), f32[32,8,1024]{2,1,0:T(8,128)}, u32[]{:S(2)}, u32[]{:S(2)}) async-start(f32[32,8,1024]{2,1,0:T(8,128)} %bitcast.42), calls=%async_computation.19 | async-start | bytes 2097152 | tf_op jit(solution)/shard_map/all_to_all | solution.py:759
  628.1 76.8 %all-gather.7.cloned.1.call-start = ((), (), s32[]{:S(2)}) async-start(), calls=%async_computation.22 | async-start | bytes 2162688 | tf_op jit(solution)/shard_map/all_gather | solution.py:1041
  660.0 51.4 %all-to-all-start.13 = ((f32[32,32,256]{2,1,0:T(8,128)}), f32[32,32,256]{2,1,0:T(8,128)S(1)}, u32[]{:S(2)}, u32[]{:S(2)}) async-start(f32[32,32,256]{2,1,0:T(8,128)} %bitcast.28), calls=%async_computation.13 | async-start | bytes 2097152 | tf_op jit(solution)/shard_map/all_to_all | solution.py:759
  (131 other events, 2096.5 us)
Sparse Core Ops, SparseCore 0:
  32.7 61.2 all-gather.4
  641.0 63.9 all-gather.6

commit v2 on v0

v2 whole, which is shorter than its diff:
```python
import functools

import jax
import jax.numpy as jnp
from jax import lax
from jax.experimental import pallas as pl
from jax.experimental.pallas import tpu as pltpu
from jax.sharding import PartitionSpec as P

EPSILON = 1e-05
MOMENTUM = 0.9
LEARN_RATE = 0.0001
HIGHEST = lax.Precision.HIGHEST
AX = ("dp", "fsdp")
F32 = jnp.float32
BF16 = jnp.bfloat16
MIB = 1 << 20


VM = pl.BlockSpec(memory_space=pltpu.VMEM)
SM = pl.BlockSpec(memory_space=pltpu.SMEM)


def params(mib):
    return pltpu.CompilerParams(vmem_limit_bytes=mib * MIB)


def dot6(left, right):
    return jnp.dot(left, right, precision=HIGHEST, preferred_element_type=F32)


def dot6_rt(left, right):
    return lax.dot_general(
        left, right, (((1,), (1,)), ((), ())), precision=HIGHEST, preferred_element_type=F32
    )


def split2(value):
    high = value.astype(BF16)
    return high, (value - high.astype(F32)).astype(BF16)


def dot3(left, right):
    lh, ll = left
    rh, rl = right
    mm = functools.partial(jnp.dot, preferred_element_type=F32)
    return mm(lh, rh) + (mm(lh, rl) + mm(ll, rh))


def keep_split(value, parts_ref):
    rows = value.shape[0]
    for i in range(parts_ref.shape[0] // rows):
        high = value.astype(BF16)
        parts_ref[i * rows : (i + 1) * rows, :] = high
        value = value - high.astype(F32)


def dot_split(left, parts_ref, count):
    rows = parts_ref.shape[0] // count
    right = [parts_ref[i * rows : (i + 1) * rows, :] for i in range(count)]
    pieces = []
    for i in range(count):
        high = left.astype(BF16)
        pieces.append(high)
        left = left - high.astype(F32)
    mm = functools.partial(jnp.dot, preferred_element_type=F32)
    total = mm(pieces[0], right[1]) + mm(pieces[1], right[0])
    if count == 3:
        low = mm(pieces[1], right[1]) + mm(pieces[0], right[2]) + mm(pieces[2], right[0])
        total = total + low
    return mm(pieces[0], right[0]) + total


def total_rows(value):
    return jnp.sum(value, axis=0, keepdims=True)


def get(ref, start, count):
    return jnp.concatenate([ref[h, pl.ds(start, count), :] for h in range(ref.shape[0])], axis=1)


def put(ref, start, value):
    count = value.shape[0]
    for h in range(ref.shape[0]):
        ref[h, pl.ds(start, count), :] = value[:, h * 128 : h * 128 + 128]


def put_rows(st_ref, first, vec):
    for i in range(vec.shape[1] // 128):
        piece = vec[:, i * 128 : (i + 1) * 128]
        st_ref[:, first + i, :] = jnp.broadcast_to(piece, (st_ref.shape[0], 128))


def take_rows(st_ref, first, channels):
    return jnp.concatenate([st_ref[:, first + i, :] for i in range(channels // 128)], axis=1)


def take_sum(st_ref, first, channels):
    return total_rows(take_rows(st_ref, first, channels))


def narrow_moments(st_ref, channels, local, total):
    sums = take_rows(st_ref, 0, channels)
    squares = take_rows(st_ref, channels // 128, channels)
    mean = total_rows(sums) / total
    off = sums / local - mean
    var = (total_rows(squares) + local * total_rows(off * off)) / total
    return mean, lax.rsqrt(var + EPSILON)


def chunk_loop(voxels, chunk, step, carry):
    def one(i, carry):
        return step(pl.multiple_of(i * chunk, chunk), carry)

    return lax.fori_loop(0, voxels // chunk, one, carry)


def local_moments(ref, chunk):
    halves, voxels, _ = ref.shape
    zero = jnp.zeros((1, halves * 128), F32)
    total = chunk_loop(voxels, chunk, lambda i, acc: acc + total_rows(get(ref, i, chunk)), zero)
    mean = total / float(voxels)

    def squares(i, acc):
        value = get(ref, i, chunk) - mean
        return acc + total_rows(value * value)

    return total, chunk_loop(voxels, chunk, squares, zero)


def put_faces(ref, first, last, frames, start=0):
    halves = ref.shape[0]
    count = (ref.shape[1] - 2 * start) // frames
    for face, frame in ((first, 0), (last, frames - 1)):
        for h in range(halves):
            face[h, 0:count, :] = ref[h, pl.ds(start + frame, count, stride=frames), :]


STAGES = ((3, 4), (1, 2), (0,))


def slot_mask(slot):
    mask = 0
    for bits in STAGES:
        mask |= (slot & ((1 << len(bits)) - 1)) << bits[0]
        slot >>= len(bits)
    return mask


def order_rows(stacks, out_ref, me, first, rows, lanes=slice(None)):
    slot = 0
    for stack in stacks:
        for s in range(stack.shape[0]):
            where = pl.multiple_of(jnp.bitwise_xor(me, slot_mask(slot)) * rows, rows)
            out_ref[pl.ds(where, rows), :] = stack[s, first : first + rows, lanes]
            slot += 1


def k_stack(*refs):
    *parts, out = refs
    at = 0
    for part in parts:
        out[at : at + part.shape[0]] = part[...]
        at += part.shape[0]


def as_column(row):
    n = row.shape[1]
    same = lax.broadcasted_iota(jnp.int32, (n, n), 0) == lax.broadcasted_iota(jnp.int32, (n, n), 1)
    return jnp.sum(jnp.where(same, jnp.broadcast_to(row, (n, n)), 0.0), axis=1, keepdims=True)


def k_pack(wr, wm, dw, we, g1, b1, g2, b2, g3, b3, t1, t2):
    share, narrow = wm.shape[1:]
    share_w = wr.shape[1]
    wide = we.shape[2]
    t1[0, 0:share_w, :] = wr[0]
    t1[0, share_w : share_w + share, :] = wm[0]
    lane = lax.broadcasted_iota(jnp.int32, (share, narrow), 1)
    blocks = []
    for b in range(2):
        block = jnp.concatenate([dw[b], jnp.zeros((share, narrow - 27), F32)], axis=1)
        for i, vec in enumerate((g1, b1, g2, b2)):
            block = jnp.where(lane == 27 + i, as_column(vec[b : b + 1, :]), block)
        blocks.append(block)
    t1[0, share_w + share :, :] = jnp.where(lane < 32, blocks[0], pltpu.roll(blocks[1], 32, 1))
    t2[0:share_w, :] = wr[1]
    t2[share_w : share_w + share, :] = wm[1]
    at = share_w + share
    for b in range(2):
        for q in range(wide // narrow):
            t2[at : at + share, :] = we[b, :, q * narrow : (q + 1) * narrow]
            at += share
    lane = lax.broadcasted_iota(jnp.int32, (share_w, narrow), 1)
    block = jnp.zeros((share_w, narrow), F32)
    for i, (vec, b) in enumerate(((g3, 0), (b3, 0), (g3, 1), (b3, 1))):
        block = jnp.where(lane == i, as_column(vec[b : b + 1, :]), block)
    t2[at : at + share_w, :] = block


def k_open_early(me_ref, mine, theirs, wm, tv, scr):
    narrow = wm.shape[0]
    share = scr.shape[0] // (mine.shape[0] * 2)
    share_w = mine.shape[1] - 2 * share
    order_rows((mine, theirs), wm, me_ref[0], share_w, share)
    order_rows((mine, theirs), scr, me_ref[0], share_w + share, share, slice(0, 128))
    turned = scr[...].T
    tv[0] = turned[0:32]
    tv[1] = turned[32:64]


def k_open_later(later, wr, wm, we0, we1, vw):
    wide, narrow = wr.shape
    devices = later.shape[0]
    share, share_w = narrow // devices, wide // devices
    wr[...] = later[:, 0:share_w, :].reshape(wide, narrow)
    wm[...] = later[:, share_w : share_w + share, :].reshape(narrow, narrow)
    at = share_w + share
    for we in (we0, we1):
        for q in range(wide // narrow):
            piece = later[:, at : at + share, :]
            we[:, q * narrow : (q + 1) * narrow] = piece.reshape(narrow, narrow)
            at += share
    turned = later[:, at : at + share_w, 0:128].reshape(wide, 128).T
    vw[0, 0:2, :] = turned[0:2]
    vw[1, 0:2, :] = turned[2:4]


def run_moments(f, value, acc_ref):
    count = float(value.shape[0])
    total = total_rows(value)
    mean = total / count
    apart = value - mean
    squares = total_rows(apart * apart)

    @pl.when(f == 0)
    def _():
        acc_ref[0:1, :] = total
        acc_ref[1:2, :] = squares

    @pl.when(f > 0)
    def _():
        done = f.astype(F32) * count
        seen = acc_ref[0:1, :]
        delta = mean - seen / done
        acc_ref[1:2, :] = acc_ref[1:2, :] + squares + delta * delta * (done * count / (done + count))
        acc_ref[0:1, :] = seen + total


def put_narrow(f, steps, a, a_ref, face_f, face_l, st_ref, acc_ref, frames):
    put(a_ref, 0, a)
    put_faces(a_ref, face_f, face_l, frames)
    run_moments(f, a, acc_ref)

    @pl.when(f == steps - 1)
    def _():
        put_rows(st_ref, 0, acc_ref[0:1, :])
        put_rows(st_ref, a_ref.shape[0], acc_ref[1:2, :])


def k_first(frames, f, steps, me_ref, x_ref, *refs):
    *w_refs, a_ref, face_f, face_l, st_ref, w_out, w_parts, acc_ref = refs
    wide = x_ref.shape[3]
    chunk = a_ref.shape[1]

    @pl.when(f == 0)
    def _():
        if len(w_refs) == 2:
            order_rows(w_refs, w_out, me_ref[0], 0, wide // (2 * w_refs[0].shape[0]))
        else:
            w_out[...] = w_refs[0][...]
        keep_split(w_out[...], w_parts)

    a = dot_split(x_ref[...].reshape(chunk, wide), w_parts, 3)
    put_narrow(f, steps, a, a_ref, face_f, face_l, st_ref, acc_ref, frames)


def finish_narrow(a_ref, st_ref, line):
    total, squares = local_moments(a_ref, line)
    put_rows(st_ref, 0, total)
    put_rows(st_ref, a_ref.shape[0], squares)


def by_frame(keep_ref, o, frames):
    frame = lax.broadcasted_iota(jnp.int32, (8, 128), 0) % frames
    value = jnp.zeros((8, 128), F32)
    for f in range(frames):
        value = jnp.where(frame == f, keep_ref[o * frames + f], value)
    return value


def make_taps(k_ref, keep_ref, wt_ref, frames, flipped):
    for o in range(3):
        keep = by_frame(keep_ref, o, frames)
        for i in range(9):
            tap = 9 * o + i
            source = 26 - tap if flipped else tap
            for h in range(wt_ref.shape[0]):
                row = k_ref[source : source + 1, h * 128 : h * 128 + 128]
                wt_ref[h, tap] = jnp.broadcast_to(row, (8, 128)) * keep


def shift_frames(field, before, after, line, frames, halos):
    halves, voxels, _ = field.shape

    def step(i, carry):
        for h in range(halves):
            value = field[h, pl.ds(i, line), :].reshape(line // 8, 8, 128)
            before[h, pl.ds(i, line), :] = pltpu.roll(value, 1, 1).reshape(line, 128)
            after[h, pl.ds(i, line), :] = pltpu.roll(value, 7, 1).reshape(line, 128)
        return carry

    chunk_loop(voxels, line, step, 0)
    for target, frame, pieces in ((before, 0, halos[0]), (after, frames - 1, halos[1])):
        start = 0
        for piece in pieces:
            count = piece.shape[0]
            for h in range(halves):
                target[h, pl.ds(start * frames + frame, count, stride=frames), :] = piece[
                    :, h * 128 : h * 128 + 128
                ]
            start += count


def column_views(value, first, last):
    n = value.shape[0] - 2
    upper = lax.broadcasted_iota(jnp.int32, (n, 8, 128), 1) < 4
    turned = pltpu.roll(value, 4, 1)
    left = jnp.where(upper, turned[0:n], turned[1 : n + 1])
    right = jnp.where(upper, turned[1 : n + 1], turned[2:])
    return left, value[1 : n + 1], right


def line_views(ref, h, start, line, part, parts):
    n = line // 8 // parts
    zero = jnp.zeros((1, 8, 128), F32)
    pieces = []
    if part == 0:
        pieces.append(zero)
    low = part * n - (part > 0)
    high = (part + 1) * n + (part < parts - 1)
    body = ref[h, pl.ds(start + low * 8, (high - low) * 8), :]
    pieces.append(body.reshape(high - low, 8, 128))
    if part == parts - 1:
        pieces.append(zero)
    value = jnp.concatenate(pieces, axis=0) if len(pieces) > 1 else pieces[0]
    return column_views(value, part == 0, part == parts - 1)


def stencil_into(fields, wt_ref, out_ref, line):
    halves, voxels, _ = out_ref.shape
    rows = voxels // line
    parts = 2 if (line // 8) % 2 == 0 else 1
    n = line // 8 // parts
    for h in range(halves):
        for part in range(parts):

            def row(j, older, old):
                new = jnp.zeros((n, 8, 128), F32)
                start = pl.multiple_of(j * line, line)
                for o in range(3):
                    views = line_views(fields[o], h, start, line, part, parts)
                    for q in range(3):
                        older = older + views[q] * wt_ref[h, 9 * o + 6 + q][None]
                        old = old + views[q] * wt_ref[h, 9 * o + 3 + q][None]
                        new = new + views[q] * wt_ref[h, 9 * o + q][None]
                return older, old, new

            zero = jnp.zeros((n, 8, 128), F32)

            def step(j, accs):
                done, old, new = row(j, accs[0], accs[1])

                @pl.when(j >= 2)
                def _():
                    where = pl.multiple_of((j - 2) * line, line) + part * n * 8
                    out_ref[h, pl.ds(pl.multiple_of(where, 8), n * 8), :] = done.reshape(n * 8, 128)

                return old, new

            lax.fori_loop(0, rows + 2, step, (zero, zero))


def halo_pieces(i, face, up, down, top, bottom, act):
    edge = up.shape[2]
    return (
        act(get(up.at[i], 0, edge)) * top,
        act(get(face, 0, face.shape[1])),
        act(get(down.at[i], 0, edge)) * bottom,
    )


def k_mix(line, frames, total, keep_ref, a_ref, hp_ref, hn_ref, up_ref, dn_ref, cu_ref, cd_ref,
          st_in, w_ref, tv_ref, c_ref, mp_ref, before, after, mom_ref, st_ref, wt_ref, *, flush):
    halves, voxels, _ = a_ref.shape
    narrow = halves * 128
    top = keep_ref[3 * frames]
    bottom = keep_ref[3 * frames + 1]
    mean, inverse = narrow_moments(st_in, narrow, float(voxels), total)
    mom_ref[0:1, :] = mean
    mom_ref[1:2, :] = inverse
    scale = tv_ref[27:28, :] * inverse
    shift = tv_ref[28:29, :]

    def mixed(value):
        return dot6(jnp.maximum((value - mean) * scale + shift, 0.0), w_ref[...])

    chunk = voxels // 2 if (voxels // 2) % line == 0 else voxels

    def own(i, carry):
        put(mp_ref, pl.multiple_of(line + i, 8), mixed(get(a_ref, i, chunk)))
        return carry

    chunk_loop(voxels, chunk, own, 0)
    put(mp_ref, 0, mixed(get(up_ref, 0, line)) * top)
    put(mp_ref, line + voxels, mixed(get(dn_ref, 0, line)) * bottom)
    make_taps(tv_ref, keep_ref, wt_ref, frames, False)
    halos = [
        halo_pieces(i, face, cu_ref, cd_ref, top, bottom, mixed)
        for i, face in enumerate((hp_ref, hn_ref))
    ]
    shift_frames(mp_ref, before, after, line, frames, halos)
    flush(1, 2, 3)
    stencil_into((before, mp_ref, after), wt_ref, c_ref, line)
    finish_narrow(c_ref, st_ref, line)


def second_act(c, mom, tv):
    return (c - mom[0:1, :]) * (tv[29:30, :] * mom[1:2, :]) + tv[30:31, :]


def k_expand(line, total, c_ref, st_in, w_ref, tv_ref, mom_ref, off_ref, sloc_ref, seen_ref, st_ref,
             s_ref):
    halves, voxels, _ = c_ref.shape
    narrow, wide = w_ref.shape
    local = float(voxels)
    mean, inverse = narrow_moments(st_in, narrow, local, total)
    mom_ref[0:1, :] = mean
    mom_ref[1:2, :] = inverse
    mom = mom_ref[...]

    def act(i, acc):
        s = jnp.maximum(second_act(get(c_ref, i, line), mom, tv_ref), 0.0)
        s_ref[pl.ds(i, line), :] = s
        return acc + total_rows(s)

    sums = chunk_loop(voxels, line, act, jnp.zeros((1, narrow), F32))
    center = sums / local
    sloc_ref[...] = jnp.broadcast_to(center, (8, narrow))
    put_rows(st_ref, 0, sums)
    off_ref[...] = dot6(sloc_ref[...], w_ref[...])
    chunk = voxels // 2 if (voxels // 2) % line == 0 else voxels

    def gram(i, acc):
        s = s_ref[pl.ds(i, chunk), :] - center
        return acc + dot6(s.T, s)

    seen = dot6(chunk_loop(voxels, chunk, gram, jnp.zeros((narrow, narrow), F32)), w_ref[...])
    seen_ref[...] = seen
    put_rows(st_ref, halves, total_rows(seen * w_ref[...]))


def k_widen(f, steps, c_ref, mom_ref, tv_ref, sloc_ref, w_ref, e_ref, w_parts):
    @pl.when(f == 0)
    def _():
        keep_split(w_ref[...], w_parts)

    s = jnp.maximum(second_act(get(c_ref, 0, c_ref.shape[1]), mom_ref[...], tv_ref), 0.0)
    e_ref[...] = dot_split(s - sloc_ref[0:1, :], w_parts, 3)


def third_norm(st_in, w_ref, off_ref, vw_ref, momw_ref, smean_ref, local, total):
    narrow, wide = w_ref.shape
    s_means = take_rows(st_in, 0, narrow) / local
    squares = take_rows(st_in, narrow // 128, wide)
    e_means = dot6(s_means, w_ref[...])
    mean = jnp.mean(e_means, axis=0, keepdims=True)
    away = e_means - mean
    var = (total_rows(squares) + local * total_rows(away * away)) / total
    inverse = lax.rsqrt(var + EPSILON)
    scale = vw_ref[0:1, :] * inverse
    momw_ref[0:1, :] = scale
    momw_ref[1:2, :] = (off_ref[0:1, :] - mean) * scale + vw_ref[1:2, :]
    momw_ref[2:3, :] = inverse
    smean_ref[0:1, :] = jnp.mean(s_means, axis=0, keepdims=True)


def k_join(frames, total, local, f, steps, e_ref, x_ref, st_in, off_ref, w_ref, vw_ref, wr_ref, x_out,
           a_ref, face_f, face_l, momw_ref, smean_ref, st_ref, w_parts, acc_ref):

    @pl.when(f == 0)
    def _():
        third_norm(st_in, w_ref, off_ref, vw_ref, momw_ref, smean_ref, local, total)
        keep_split(wr_ref[...], w_parts)

    x = x_ref[...].reshape(x_out.shape)
    x = jnp.maximum(e_ref[...] * momw_ref[0:1, :] + momw_ref[1:2, :] + x, 0.0)
    x_out[...] = x
    a = dot_split(x, w_parts, 3)
    put_narrow(f, steps, a, a_ref, face_f, face_l, st_ref, acc_ref, frames)


def wide_step(gz, s, f, u_ref, p_ref, bias_acc, w_parts):
    put(u_ref, 0, dot_split(gz, w_parts, 2))
    p = dot3(split2(s.T), split2(gz))
    part = total_rows(gz)

    @pl.when(f == 0)
    def _():
        p_ref[...] = p
        bias_acc[0:1, :] = part

    @pl.when(f > 0)
    def _():
        p_ref[...] = p_ref[...] + p
        bias_acc[0:1, :] = bias_acc[0:1, :] + part


def centred_act(c_ref, mom_ref, tv_ref, smean_ref):
    c = get(c_ref, 0, c_ref.shape[1])
    return jnp.maximum(second_act(c, mom_ref[...], tv_ref), 0.0) - smean_ref[0:1, :]


def wide_finish(p_ref, w_ref, inverse, bias_acc, st_ref):
    wide = w_ref.shape[1]
    gain_sum = total_rows(p_ref[...] * w_ref[...]) * inverse
    put_rows(st_ref, 0, bias_acc[0:1, :])
    put_rows(st_ref, wide // 128, gain_sum)


def k_turn(total, local, f, steps, e_ref, x_ref, cot_ref, c_ref, st_in, off_ref, w_ref, vw_ref, mom_ref,
           tv_ref, out_ref, gz_ref, u_ref, p_ref, momw_ref, smean_ref, pool_ref, st_ref, w_parts,
           bias_acc):
    chunk, wide = x_ref.shape

    @pl.when(f == 0)
    def _():
        third_norm(st_in, w_ref, off_ref, vw_ref, momw_ref, smean_ref, local, total)
        keep_split((w_ref[...] * momw_ref[0:1, :]).T, w_parts)

    z = e_ref[...] * momw_ref[0:1, :] + momw_ref[1:2, :] + x_ref[...]
    out = jnp.maximum(z, 0.0)
    out_ref[...] = out.reshape(out_ref.shape)
    pooled = jnp.sum(out.reshape(chunk // 8, 8, wide), axis=0)

    @pl.when(f == 0)
    def _():
        pool_ref[...] = pooled

    @pl.when(f > 0)
    def _():
        pool_ref[...] = pool_ref[...] + pooled

    gz = jnp.where(z > 0.0, cot_ref[...].reshape(chunk, wide), 0.0)
    gz_ref[...] = gz
    s = centred_act(c_ref, mom_ref, tv_ref, smean_ref)
    wide_step(gz, s, f, u_ref, p_ref, bias_acc, w_parts)

    @pl.when(f == steps - 1)
    def _():
        wide_finish(p_ref, w_ref, momw_ref[2:3, :], bias_acc, st_ref)


def k_second(total, f, steps, u_ref, c_ref, st_in, w_ref, momw_ref, smean_ref, mom_ref, tv_ref, *refs):
    *more, n_ref, gw_ref, st_ref, q_parts, acc_ref = refs
    halves, chunk, _ = u_ref.shape
    narrow, wide = w_ref.shape

    @pl.when(f == 0)
    def _():
        bias_sum = take_sum(st_in, 0, wide)
        gain_sum = take_sum(st_in, wide // 128, wide)
        gw_ref[0:1, :] = gain_sum
        gw_ref[1:2, :] = bias_sum
        alpha = momw_ref[0:1, :]
        w = w_ref[...]
        wt = split2(w.T)
        q = dot3(split2(w * (alpha * momw_ref[2:3, :] * (gain_sum / total))), wt)
        keep_split(q, q_parts)
        acc_ref[0:2, :] = jnp.zeros((2, narrow), F32)
        d = dot3(split2(jnp.broadcast_to(alpha * (bias_sum / total), (8, wide))), wt)
        acc_ref[2:3, :] = d[0:1, :]

    mom = mom_ref[...]
    c = get(c_ref, 0, chunk)
    y = second_act(c, mom, tv_ref)
    corr = dot_split(jnp.maximum(y, 0.0) - smean_ref[0:1, :], q_parts, 2)
    n = jnp.where(y > 0.0, get(u_ref, 0, chunk) - corr - acc_ref[2:3, :], 0.0)
    put(n_ref, 0, n)
    xhat = (c - mom[0:1, :]) * mom[1:2, :]
    acc_ref[0:1, :] = acc_ref[0:1, :] + total_rows(n)
    acc_ref[1:2, :] = acc_ref[1:2, :] + total_rows(n * xhat)

    @pl.when(f == steps - 1)
    def _():
        put_rows(st_ref, 0, acc_ref[0:1, :])
        put_rows(st_ref, halves, acc_ref[1:2, :])
        if more:
            st_ref[:, 2 * halves :, :] = more[0][...]


def expand_grad(local, total, p_ref, w_ref, gw_ref, momw_ref, smean_ref, sloc_ref, seen_ref, dw_ref):
    apart = sloc_ref[...] - smean_ref[0:1, :]
    column = apart.T[:, 0:1] * local
    alpha = momw_ref[0:1, :]
    gamma = gw_ref[0:1, :] / total * momw_ref[2:3, :]
    beta = gw_ref[1:2, :] / total
    seen = seen_ref[...] + column * dot6(apart, w_ref[...])[0:1, :]
    dw_ref[...] = alpha * (p_ref[...] - column * beta - seen * gamma)


def norm_sums(f, st_in, out_ref):
    @pl.when(f == 0)
    def _():
        narrow = out_ref.shape[1]
        out_ref[0:1, :] = take_sum(st_in, narrow // 128, narrow)
        out_ref[1:2, :] = take_sum(st_in, 0, narrow)


def norm_back(n, a, gain, mom_ref, sums_ref, total):
    mom = mom_ref[...]
    xhat = (a - mom[0:1, :]) * mom[1:2, :]
    return gain * mom[1:2, :] * (n - sums_ref[1:2, :] / total - xhat * (sums_ref[0:1, :] / total))


def k_center(frames, total, f, steps, n_ref, c_ref, st_in, tv_ref, mom2_ref, gc_ref, face_f, face_l,
             gd_ref, *more):
    norm_sums(f, st_in, gd_ref)
    if more:
        more[0][...] = jnp.sum(st_in[:, 2 * gc_ref.shape[0] :, :], axis=0)
    chunk = n_ref.shape[1]
    n, c = get(n_ref, 0, chunk), get(c_ref, 0, chunk)
    put(gc_ref, 0, norm_back(n, c, tv_ref[29:30, :], mom2_ref, gd_ref, total))
    put_faces(gc_ref, face_f, face_l, frames)


def k_first_back(line, frames, keep_ref, gc_ref, hp_ref, hn_ref, up_ref, dn_ref, cu_ref, cd_ref,
                 a_ref, w_ref, tv_ref, mom1_ref, *refs, flush):
    *more, gm_ref, n1_ref, st_ref, gcp_ref, before, after, wt_ref = refs
    halves, voxels, _ = gc_ref.shape
    narrow = halves * 128
    top = keep_ref[3 * frames]
    bottom = keep_ref[3 * frames + 1]

    def own(i, carry):
        put(gcp_ref, pl.multiple_of(line + i, 8), get(gc_ref, i, line))
        return carry

    chunk_loop(voxels, line, own, 0)
    put(gcp_ref, 0, get(up_ref, 0, line) * top)
    put(gcp_ref, line + voxels, get(dn_ref, 0, line) * bottom)
    make_taps(tv_ref, keep_ref, wt_ref, frames, True)
    halos = [
        halo_pieces(i, face, cu_ref, cd_ref, top, bottom, lambda v: v)
        for i, face in enumerate((hp_ref, hn_ref))
    ]
    shift_frames(gcp_ref, before, after, line, frames, halos)
    stencil_into((before, gcp_ref, after), wt_ref, gm_ref, line)
    flush(0)
    wt = split2(w_ref[...].T)
    mom1 = mom1_ref[...]
    scale1 = tv_ref[27:28, :] * mom1[1:2, :]
    chunk = voxels // 2 if (voxels // 2) % line == 0 else voxels

    def step(i, accs):
        gr = dot3(split2(get(gm_ref, i, chunk)), wt)
        off = get(a_ref, i, chunk) - mom1[0:1, :]
        n = jnp.where(off * scale1 + tv_ref[28:29, :] > 0.0, gr, 0.0)
        put(n1_ref, i, n)
        return accs[0] + total_rows(n), accs[1] + total_rows(n * (off * mom1[1:2, :]))

    zero = jnp.zeros((1, narrow), F32)
    bias_acc, gain_acc = chunk_loop(voxels, chunk, step, (zero, zero))
    put_rows(st_ref, 0, bias_acc)
    put_rows(st_ref, halves, gain_acc)
    if more:
        rest = st_ref.shape[1] - 2 * halves
        st_ref[:, 2 * halves :, :] = jnp.broadcast_to(more[0][...][None], (st_ref.shape[0], rest, 128))


def k_side_grads(line, frames, total, keep_ref, gc_ref, mp_ref, before, after, p_ref, w_ref, gw_ref,
                 momw_ref, smean_ref, sloc_ref, seen_ref, dk_ref, de_ref):
    expand_grad(float(gc_ref.shape[1]), total, p_ref, w_ref, gw_ref, momw_ref, smean_ref, sloc_ref,
                seen_ref, de_ref)
    halves, voxels, _ = gc_ref.shape
    narrow = halves * 128
    parts = 2 if (line // 8) % 2 == 0 else 1
    n = line // 8 // parts
    for h in range(halves):
        for o, field in enumerate((before, mp_ref, after)):

            def row(r, accs):
                accs = list(accs)
                for part in range(parts):
                    where = pl.multiple_of(r * line, line) + part * n * 8
                    g = gc_ref[h, pl.ds(pl.multiple_of(where, 8), n * 8), :].reshape(n, 8, 128)
                    for p in range(3):
                        start = pl.multiple_of((r + p) * line, line)
                        views = line_views(field, h, start, line, part, parts)
                        for q in range(3):
                            accs[3 * p + q] = accs[3 * p + q] + jnp.sum(g * views[q], axis=0)
                return tuple(accs)

            accs = lax.fori_loop(0, voxels // line, row, (jnp.zeros((8, 128), F32),) * 9)
            keep = by_frame(keep_ref, o, frames)
            for i in range(9):
                tap = 9 * o + i
                dk_ref[tap : tap + 1, h * 128 : h * 128 + 128] = total_rows(accs[i] * keep)
    dk_ref[27:128, :] = jnp.zeros((101, narrow), F32)


def mixing_grad(line, a_ref, gm_ref, tv_ref, mom1_ref):
    halves, voxels, _ = a_ref.shape
    narrow = halves * 128
    mom1 = mom1_ref[...]
    scale1 = tv_ref[27:28, :] * mom1[1:2, :]
    chunk = voxels // 2 if (voxels // 2) % line == 0 else voxels

    def mixing(i, acc):
        y = (get(a_ref, i, chunk) - mom1[0:1, :]) * scale1 + tv_ref[28:29, :]
        turned = jnp.maximum(y, 0.0).T
        return acc + dot3(split2(turned), split2(get(gm_ref, i, chunk)))

    return chunk_loop(voxels, chunk, mixing, jnp.zeros((narrow, narrow), F32))


def k_mix_grad(line, a_ref, gm_ref, tv_ref, mom1_ref, dm_ref):
    dm_ref[...] = mixing_grad(line, a_ref, gm_ref, tv_ref, mom1_ref)


def k_pack_grads(line, me_ref, a, gm, tv, mom1, de, dk, mine, theirs):
    narrow = dk.shape[1]
    lower = me_ref[0] % 2 == 1
    pairs = mine.shape[0]
    share = narrow // (2 * pairs)
    groups = de.shape[1] // narrow

    def store(at, piece):
        piece = piece.reshape(pairs, 2, share, narrow)
        mine[:, at : at + share, :] = jnp.where(lower, piece[:, 1], piece[:, 0])
        theirs[:, at : at + share, :] = jnp.where(lower, piece[:, 0], piece[:, 1])

    for g in range(groups):
        store(g * share, de[:, g * narrow : (g + 1) * narrow])
    store(groups * share, mixing_grad(line, a, gm, tv, mom1))
    turned = jnp.concatenate([dk[...].T, jnp.zeros((narrow, narrow - 128), F32)], axis=1)
    store((groups + 1) * share, turned)


def k_update(*refs):
    me_ref, zero, one, reduce_zero, reduce_one = refs[:5]
    vecs = refs[5:11]
    params, momenta = refs[11:21], refs[21:31]
    grads, velocity, updated = refs[31:41], refs[41:51], refs[51:61]
    me = me_ref[0]
    share = params[1].shape[1]
    narrow = params[1].shape[2]
    groups = params[3].shape[2] // narrow

    def apply(i, b, grad, where=slice(None)):
        v = MOMENTUM * momenta[i][b, :, where] + grad
        grads[i][b, :, where] = grad
        velocity[i][b, :, where] = v
        updated[i][b, :, where] = params[i][b, :, where] - LEARN_RATE * (grad + MOMENTUM * v)

    packs = (jnp.sum(zero[...], axis=0), jnp.sum(one[...], axis=0))
    for b, (pack, reduce) in enumerate(zip(packs, (reduce_zero, reduce_one))):
        for g in range(groups):
            apply(3, b, pack[g * share : (g + 1) * share], slice(g * narrow, (g + 1) * narrow))
        at = groups * share
        apply(1, b, pack[at : at + share])
        at += share
        apply(2, b, pack[at : at + share, 0:27])
        apply(0, b, jnp.sum(reduce[...], axis=0))
    for j in range(3):
        for r in range(2):
            i = 4 + 2 * j + r
            pieces = []
            for b in range(2):
                value = vecs[2 * j + b][...]
                width = params[i].shape[1]
                length = value.shape[1]
                turned = pltpu.roll(value, length - me * width, 1)
                pieces.append(turned[r : r + 1, 0:width])
            grad = jnp.concatenate(pieces, axis=0)
            v = MOMENTUM * momenta[i][...] + grad
            grads[i][...] = grad
            velocity[i][...] = v
            updated[i][...] = params[i][...] - LEARN_RATE * (grad + MOMENTUM * v)


def put_by_core(dw, me_ref, out_refs):
    if len(out_refs) == 1:
        out_refs[0][...] = dw
    else:
        mine, theirs = out_refs
        dw = dw.reshape(mine.shape[0], 2, *mine.shape[1:])
        lower = me_ref[0] % 2 == 1
        mine[...] = jnp.where(lower, dw[:, 1], dw[:, 0])
        theirs[...] = jnp.where(lower, dw[:, 0], dw[:, 1])


def reduce_grad(ga, x, f, dwt):
    dw = dot3(split2(ga.T), split2(x))

    @pl.when(f == 0)
    def _():
        dwt[...] = dw

    @pl.when(f > 0)
    def _():
        dwt[...] = dwt[...] + dw


def k_between(total, f, steps, me_ref, n1_ref, a_ref, c_ref, x_ref, gz_in, st_in, tv_ref, mom1_ref,
              wr_ref, mom2_ref, tv2_ref, w_ref, momw_ref, smean_ref, gz_ref, u_ref, p_ref, gn_ref,
              st_ref, *refs):
    *dw_refs, wr_parts, w_parts, dwt, bias_acc = refs
    chunk, wide = x_ref.shape
    norm_sums(f, st_in, gn_ref)

    @pl.when(f == 0)
    def _():
        keep_split(wr_ref[...].T, wr_parts)
        keep_split((w_ref[...] * momw_ref[0:1, :]).T, w_parts)

    x = x_ref[...]
    n, a = get(n1_ref, 0, chunk), get(a_ref, 0, chunk)
    ga = norm_back(n, a, tv_ref[27:28, :], mom1_ref, gn_ref, total)
    gy = dot_split(ga, wr_parts, 2) + gz_in[...]
    gz = jnp.where(x > 0.0, gy, 0.0)
    gz_ref[...] = gz
    reduce_grad(ga, x, f, dwt)
    s = centred_act(c_ref, mom2_ref, tv2_ref, smean_ref)
    wide_step(gz, s, f, u_ref, p_ref, bias_acc, w_parts)

    @pl.when(f == steps - 1)
    def _():
        wide_finish(p_ref, w_ref, momw_ref[2:3, :], bias_acc, st_ref)
        put_by_core(dwt[...].T, me_ref, dw_refs)


def k_last_weight(total, f, steps, me_ref, n1_ref, a_ref, x_ref, st_in, tv_ref, mom1_ref, ga_ref,
                  gn_ref, *refs):
    *dw_refs, dwt = refs
    chunk = n1_ref.shape[1]
    norm_sums(f, st_in, gn_ref)
    n, a = get(n1_ref, 0, chunk), get(a_ref, 0, chunk)
    ga = norm_back(n, a, tv_ref[27:28, :], mom1_ref, gn_ref, total)
    put(ga_ref, 0, ga)
    reduce_grad(ga, x_ref[...].reshape(chunk, -1), f, dwt)

    @pl.when(f == steps - 1)
    def _():
        put_by_core(dwt[...].T, me_ref, dw_refs)


def k_last(f, steps, ga_ref, gz_in, wr_ref, gx_ref, wr_parts):
    @pl.when(f == 0)
    def _():
        keep_split(wr_ref[...].T, wr_parts)

    gy = dot_split(get(ga_ref, 0, ga_ref.shape[1]), wr_parts, 2) + gz_in[...]
    gx_ref[...] = gy.reshape(gx_ref.shape)


def exchange(rows):
    return lax.all_to_all(rows, AX, 0, 0)


def meet(value, bits, devices):
    parts = [value]
    for step in range(1, 1 << len(bits)):
        mask = step << bits[0]
        parts.append(lax.ppermute(value, AX, [(i, i ^ mask) for i in range(devices)]))
    return parts


def perm(step, shape):
    dp, fs = shape
    pairs = []
    for i in range(dp):
        for j in range(fs):
            a, b = i + step[0], j + step[1]
            if 0 <= a < dp and 0 <= b < fs:
                pairs.append((i * fs + j, a * fs + b))
    return pairs


def halo(field, first, last, line, frames, shape, beside=()):
    voxels = field.shape[1]
    width = line // frames
    count = voxels // frames
    move = lambda value, step: lax.ppermute(value, AX, perm(step, shape))
    before, after = move(last, (1, 0)), move(first, (-1, 0))
    low, high = field[:, :line], field[:, voxels - line :]
    tops = jnp.stack([before[:, :width], after[:, :width]])
    ends = jnp.stack([before[:, count - width :], after[:, count - width :]])
    beside = list(beside)
    if beside:
        tops, ends, *beside = lax.optimization_barrier((tops, ends, *beside))
    if shape[1] == 2:
        upper = lax.axis_index("fsdp") == 0
        pairs = [(i, i ^ 1) for i in range(shape[0] * 2)]
        row = lax.ppermute(jnp.where(upper, high, low), AX, pairs)
        corner = lax.ppermute(jnp.where(upper, ends, tops), AX, pairs)
        return [before, after, row, row, corner, corner], *beside
    rows = [move(high, (0, 1)), move(low, (0, -1))]
    return [before, after, *rows, move(ends, (0, 1)), move(tops, (0, -1))], *beside


def tree_gather(part, devices, name):
    for bits in STAGES[:-1]:
        parts = meet(part, bits, devices)
        dims = (part.shape[0] * len(parts),) + part.shape[1:]
        part = call(k_stack, name, [(dims, HB)], [(piece, HB) for piece in parts], limit=4)[0]
    return meet(part, STAGES[-1], devices)


def core_sums(mine, theirs, shape):
    pairs = [(i, i ^ 1) for i in range(shape[0] * 2)]
    return mine + lax.ppermute(theirs, AX, pairs)


def owner_parts(parts, shape):
    return lax.all_to_all(parts, "dp", 0, 0)


HB = pl.BlockSpec(memory_space=pl.ANY)
FILLER = 1 << 31
HIDER = 1 << 32


def pieces(far, near):
    rows = near.shape[0]
    size = 4
    for dim in near.shape:
        size *= dim
    if size < MIB // 2:
        return [(far, near)]
    if len(near.shape) == 3 and rows <= 4:
        return [(far.at[i], near.at[i]) for i in range(rows)]
    if rows % 16 == 0:
        half = rows // 2
        return [(far.at[pl.ds(i * half, half)], near.at[pl.ds(i * half, half)]) for i in range(2)]
    return [(far, near)]


class Stream:
    def __init__(self, axis):
        self.axis = axis

    def part(self, ref, i, steps):
        size = ref.shape[self.axis] // steps
        where = pl.ds(i * size if isinstance(i, int) else pl.multiple_of(i * size, size), size)
        return ref.at[(slice(None),) * self.axis + (where,)]


WIDE, NARROW = Stream(0), Stream(1)
AHEAD = 2


def call(kernel, name, outs, ins, scratch=(), limit=24, steps=None, flushes=False, cost=1000):
    n_i, n_o, n_s = len(ins), len(outs), len(scratch)
    count = steps or 1
    near_i = [i for i in range(n_i) if ins[i][1] is not SM]
    whole_i = [i for i in near_i if ins[i][1] is HB]
    flow_i = [i for i in near_i if ins[i][1] is not HB]
    whole_o = [i for i in range(n_o) if outs[i][1] is HB]
    flow_o = [i for i in range(n_o) if outs[i][1] is not HB]

    def run(*refs):
        far_in, far_out = refs[:n_i], refs[n_i : n_i + n_o]
        own = refs[n_i + n_o : n_i + n_o + n_s]
        near = refs[n_i + n_o + n_s : -2]
        sem, flow_sem = refs[-2:]
        in_refs, out_refs = list(far_in), list(near[len(near_i) :])
        for i, ref in zip(near_i, near):
            in_refs[i] = ref
        used = 0
        loads, stores = [], {}
        for i in whole_i:
            for src, dst in pieces(far_in[i], in_refs[i]):
                loads.append(pltpu.make_async_copy(src, dst, sem.at[used]))
                used += 1
        for i in whole_o:
            stores[i] = []
            for dst, src in pieces(far_out[i], out_refs[i]):
                stores[i].append(pltpu.make_async_copy(src, dst, sem.at[used]))
                used += 1
        started = set()

        def flush(*which):
            for i in which:
                started.add(i)
                for copy in stores[i]:
                    copy.start()

        def flow_in(i):
            return [
                pltpu.make_async_copy(
                    ins[j][1].part(far_in[j], i, count),
                    ins[j][1].part(in_refs[j], i, count),
                    flow_sem.at[k, i],
                )
                for k, j in enumerate(flow_i)
            ]

        def flow_out(i):
            return [
                pltpu.make_async_copy(
                    outs[j][1].part(out_refs[j], i, count),
                    outs[j][1].part(far_out[j], i, count),
                    flow_sem.at[len(flow_i) + k, i],
                )
                for k, j in enumerate(flow_o)
            ]

        for copy in loads:
            copy.start()
        heavy = any(ins[j][1] is WIDE for j in flow_i)
        ahead = min(AHEAD, count) if heavy else count
        for i in range(ahead):
            for copy in flow_in(i):
                copy.start()
        for copy in loads:
            copy.wait()
        if steps is None:
            kernel(*in_refs, *out_refs, *own, **({"flush": flush} if flushes else {}))
        else:

            def step(i, carry):
                for copy in flow_in(i):
                    copy.wait()
                if count > ahead:

                    @pl.when(i + ahead < count)
                    def _():
                        for copy in flow_in(i + ahead):
                            copy.start()

                views = list(in_refs) + list(out_refs)
                for j in flow_i:
                    views[j] = ins[j][1].part(in_refs[j], i, count)
                for j in flow_o:
                    views[n_i + j] = outs[j][1].part(out_refs[j], i, count)
                kernel(i, count, *views, *own)
                for copy in flow_out(i):
                    copy.start()
                return carry

            lax.fori_loop(0, count, step, 0)
        for i in whole_o:
            if i not in started:
                for copy in stores[i]:
                    copy.start()
        for i in range(count):
            for copy in flow_out(i):
                copy.wait()
        for i in whole_o:
            for copy in stores[i]:
                copy.wait()

    values = [
        value if spec is SM else pltpu.with_memory_space_constraint(value, pltpu.HBM)
        for value, spec in ins
    ]
    whole = 2 * (len(whole_i) + len(whole_o))
    flows = len(flow_i) + len(flow_o)
    return pl.pallas_call(
        run,
        in_specs=[spec if spec is SM else HB for _, spec in ins],
        out_specs=(HB,) * n_o,
        out_shape=tuple(pltpu.HBM(shape, F32) for shape, _ in outs),
        scratch_shapes=[pltpu.VMEM(shape, dtype) for shape, dtype in scratch]
        + [pltpu.VMEM(ins[i][0].shape, F32) for i in near_i]
        + [pltpu.VMEM(shape, F32) for shape, _ in outs]
        + [pltpu.SemaphoreType.DMA((max(whole, 1),)), pltpu.SemaphoreType.DMA((max(flows, 1), count))],
        compiler_params=params(limit),
        cost_estimate=pl.CostEstimate(flops=cost, bytes_accessed=1000, transcendentals=0),
        name=name,
    )(*values)


def body(inputs, cotangent, clip_index, *args):
    weights, momenta = args[:10], args[10:]
    frames, rows, width, wide = inputs.shape
    narrow = weights[0].shape[2]
    halves = narrow // 128
    shape = (lax.axis_size("dp"), lax.axis_size("fsdp"))
    devices = shape[0] * shape[1]
    rank = lax.axis_index(AX)
    voxels = frames * rows * width
    line = width * frames
    total = float(voxels * devices)
    many = 7 if voxels % (7 * 8 * frames) == 0 else 1
    x0 = inputs.transpose(1, 2, 0, 3)
    cot = cotangent.transpose(1, 2, 0, 3)

    edge = jnp.full((1,), -1, jnp.int32)
    window = lax.dynamic_slice_in_dim(
        jnp.concatenate([edge, clip_index, edge]), lax.axis_index("dp") * frames, frames + 2
    )
    centre = window[1:-1]
    flags = jnp.concatenate(
        [
            (window[:-2] == centre).astype(F32),
            jnp.ones((frames,), F32),
            (window[2:] == centre).astype(F32),
            (lax.axis_index("fsdp") > 0).astype(F32)[None],
            (lax.axis_index("fsdp") < shape[1] - 1).astype(F32)[None],
        ]
    )
    me = rank.astype(jnp.int32)[None]

    field_n = (halves, voxels, 128)
    grown_n = (halves, voxels + 2 * line, 128)
    face_n = (halves, voxels // frames, 128)
    field_w = (voxels, wide)
    stat_n = (devices, 2 * halves, 128)
    stat_e = (devices, (narrow + wide) // 128, 128)
    stat_w = (devices, 2 * wide // 128, 128)
    mom_n, mom_w = (8, narrow), (8, wide)
    down_r, down_m, down_e = (wide, narrow), (narrow, narrow), (narrow, wide)
    parts = lambda *values: [(value, NARROW) for value in values]

    near = lambda *values: [(value, HB) for value in values]
    fix = near
    owned = devices == 32
    half = (devices // 2, wide // devices, narrow)
    down_halves = (half, half) if owned else (down_r,)

    def first(wr0):
        return call(
            functools.partial(k_first, frames),
            "first",
            [(field_n, NARROW), (face_n, NARROW), (face_n, NARROW)] + near(stat_n, down_r),
            [(me, SM), (x0, WIDE)] + near(*wr0),
            scratch=[((3 * wide, narrow), BF16), (mom_n, F32)],
            limit=48,
            steps=many,
        )

    if owned:
        share_n, share_w = weights[1].shape[1], weights[0].shape[1]
        early, late = call(
            k_pack,
            "pack",
            near(
                (1, share_w + 2 * share_n, narrow),
                (2 * share_w + share_n * (1 + 2 * (wide // narrow)), narrow),
            ),
            near(*weights),
            limit=4,
        )
        wr0 = slots = tree_gather(early, devices, "stack")
        late = lax.all_gather(late, AX, axis=0, tiled=False)
        a0, *faces, st, wr0 = first(wr0)
        wm0, tv = call(
            k_open_early,
            "open_early",
            near(down_m, (2, 32, narrow)),
            [(me, SM)] + near(*slots),
            scratch=[((narrow, 128), F32)],
            limit=8,
            cost=FILLER,
        )
        wr1, wm1, we0, we1, vw = call(
            k_open_later,
            "open_later",
            near(down_r, down_m, down_e, down_e, (2, 8, wide)),
            near(late),
            limit=16,
            cost=FILLER,
        )
    else:
        gather = lambda part: lax.all_gather(part, AX, axis=0, tiled=True)
        wr0, wr1 = [gather(weights[0][0])], gather(weights[0][1])
        wm0, wm1 = gather(weights[1][0]), gather(weights[1][1])
        we0, we1 = gather(weights[3][0]), gather(weights[3][1])
        small = jnp.concatenate([weights[2]] + [weights[i][..., None] for i in (4, 5, 6, 7)], axis=2)
        small = gather(small.transpose(1, 0, 2))
        tv = jnp.pad(small.transpose(1, 2, 0), ((0, 0), (0, 1), (0, 0)))
        large = gather(jnp.stack([weights[8], weights[9]], axis=2).transpose(1, 0, 2))
        vw = jnp.pad(large.transpose(1, 2, 0), ((0, 0), (0, 6), (0, 0)))

    def mix(block, a, halos, st, wm):
        return call(
            functools.partial(k_mix, line, frames, total),
            "mix",
            near(field_n, grown_n, grown_n, grown_n, mom_n, stat_n),
            [(flags, SM)] + near(a, *halos, st, wm, tv[block]),
            scratch=[((halves, 27, 8, 128), F32)],
            limit=20,
            flushes=True,
        )

    def expand(block, c, st, we):
        return call(
            functools.partial(k_expand, line, total),
            "expand",
            near(mom_n, mom_w, mom_n, down_e, stat_e),
            near(c, st, we, tv[block]),
            scratch=[((voxels, narrow), F32)],
            limit=20,
        )

    def widen(block, c, mom2, sloc, we):
        return call(
            k_widen,
            "widen",
            [(field_w, WIDE)],
            [(c, NARROW)] + near(mom2, tv[block], sloc, we),
            scratch=[((3 * narrow, wide), BF16)],
            limit=48,
            steps=many,
            cost=FILLER,
        )[0]

    def join(e, x, st, off, we, wr):
        return call(
            functools.partial(k_join, frames, total, float(voxels)),
            "join",
            [(field_w, WIDE), (field_n, NARROW), (face_n, NARROW), (face_n, NARROW)]
            + near(mom_w, mom_n, stat_n),
            [(e, WIDE), (x, WIDE)] + near(st, off, we, vw[0], wr),
            scratch=[((3 * wide, narrow), BF16), (mom_n, F32)],
            limit=56,
            steps=many,
        )

    def turn(e, x, c, st, off, we, mom2):
        return call(
            functools.partial(k_turn, total, float(voxels)),
            "turn",
            [((rows, width, frames, wide), WIDE), (field_w, WIDE), (field_n, NARROW)]
            + near(down_e, mom_w, mom_n, mom_w, stat_w),
            [(e, WIDE), (x, WIDE), (cot, WIDE), (c, NARROW)]
            + near(st, off, we, vw[1], mom2, tv[1]),
            scratch=[((2 * wide, narrow), BF16), (mom_w, F32)],
            limit=58,
            steps=many,
        )

    def stat_with(more):
        return (devices, 2 * halves + sum(value.shape[-2] for value in more), 128)

    def second(block, u, c, st, we, momw, smean, mom2, *more):
        return call(
            functools.partial(k_second, total),
            "second",
            parts(field_n) + near(mom_w, stat_with(more)),
            parts(u, c) + near(st, we, momw, smean, mom2, tv[block], *more),
            scratch=[((2 * narrow, narrow), BF16), (mom_n, F32)],
            limit=24,
            steps=many,
        )

    def center(block, n, c, st, mom2):
        return call(
            functools.partial(k_center, frames, total),
            "center",
            [(field_n, NARROW), (face_n, NARROW), (face_n, NARROW)]
            + near(mom_n, *([(st.shape[1] - 2 * halves, 128)] if st.shape[1] > 2 * halves else [])),
            parts(n, c) + near(st, tv[block], mom2),
            limit=24,
            steps=many,
        )

    def first_back(block, gc, halos, a, wm, mom1, *more):
        return call(
            functools.partial(k_first_back, line, frames),
            "first_back",
            near(field_n, field_n, stat_with(more)),
            [(flags, SM)] + near(gc, *halos, a, wm, tv[block], mom1, *more),
            scratch=[(grown_n, F32)] * 3 + [((halves, 27, 8, 128), F32)],
            limit=20,
            flushes=True,
        )

    def side_grads(gc, grown, p, we, gw, momw, smean, sloc, seen):
        return call(
            functools.partial(k_side_grads, line, frames, total),
            "side_grads",
            near((128, narrow), down_e),
            [(flags, SM)] + near(gc, *grown, p, we, gw, momw, smean, sloc, seen),
            limit=24,
            cost=HIDER,
        )

    def pack_grads(block, a, gm, mom1, *grads):
        lines = (narrow // devices) * (wide // narrow + 2)
        return call(
            functools.partial(k_pack_grads, line),
            "pack_grads",
            near(*[(devices // 2, lines, narrow)] * 2),
            [(me, SM)] + near(a, gm, tv[block], mom1, *grads),
            limit=20,
            cost=FILLER,
        )

    def mix_grad(block, a, gm, mom1):
        return call(
            functools.partial(k_mix_grad, line),
            "mix_grad",
            near(down_m),
            near(a, gm, tv[block], mom1),
            limit=12,
        )[0]

    def between(n1, a, st, mom1, wr, x, gz, c, mom2, we, momw, smean):
        return call(
            functools.partial(k_between, total),
            "between",
            [(field_w, WIDE), (field_n, NARROW)] + near(down_e, mom_n, stat_w, *down_halves),
            [(me, SM)]
            + parts(n1, a, c)
            + [(x, WIDE), (gz, WIDE)]
            + near(st, tv[1], mom1, wr, mom2, tv[0], we, momw, smean),
            scratch=[((2 * narrow, wide), BF16), ((2 * wide, narrow), BF16), (down_e, F32),
                     (mom_w, F32)],
            limit=58,
            steps=many,
        )

    def last_weight(n1, a, st, mom1):
        return call(
            functools.partial(k_last_weight, total),
            "last_weight",
            [(field_n, NARROW)] + near(mom_n, *down_halves),
            [(me, SM)] + parts(n1, a) + [(x0, WIDE)] + near(st, tv[0], mom1),
            scratch=[(down_e, F32)],
            limit=48,
            steps=many,
        )

    def last(ga, gz, wr):
        return call(
            k_last,
            "last",
            [((rows, width, frames, wide), WIDE)],
            [(ga, NARROW), (gz, WIDE)] + near(wr),
            scratch=[((2 * narrow, wide), BF16)],
            limit=48,
            steps=many,
            cost=FILLER,
        )[0]

    spread = lambda field, face_f, face_l, *beside: halo(
        field, face_f, face_l, line, frames, shape, beside
    )

    if not owned:
        a0, *faces, st, wr0 = first(wr0)
    c0, *grown0, mom10, st = mix(0, a0, spread(a0, *faces)[0], exchange(st), wm0)
    mom20, off0, sloc0, seen0, st = expand(0, c0, exchange(st), we0)
    e0 = widen(0, c0, mom20, sloc0, we0)
    x1, a1, *faces, momw0, smean0, st = join(e0, x0, exchange(st), off0, we0, wr1)
    c1, *grown1, mom11, st = mix(1, a1, spread(a1, *faces)[0], exchange(st), wm1)
    mom21, off1, sloc1, seen1, st = expand(1, c1, exchange(st), we1)
    e1 = widen(1, c1, mom21, sloc1, we1)
    out, gz1, u1, p1, momw1, smean1, pool, st = turn(
        e1, x1, c1, exchange(st), off1, we1, mom21
    )

    clips = clip_index.shape[0] // 6
    labels = jnp.arange(clips, dtype=jnp.int32)
    hot = (centre[None, :] == labels[:, None]).astype(F32)
    pooled = jnp.dot(
        jnp.concatenate([hot] * (8 // frames), axis=1), pool, precision=HIGHEST,
        preferred_element_type=F32,
    )
    if owned:
        room = -(-clips * share_w // 128) * 128
        pooled = pooled.reshape(clips, devices, share_w).transpose(1, 0, 2).reshape(devices, -1)
        pooled = jnp.pad(pooled, ((0, 0), (0, room - clips * share_w)))
        more = (pooled.reshape(devices, room // 128, 128),)
    else:
        more = ()
        pooled = lax.psum(pooled, AX)
    counts = jnp.sum((clip_index[None, :] == labels[:, None]).astype(F32), axis=1)

    n, gw1, st = second(1, u1, c1, exchange(st), we1, momw1, smean1, mom21, *more)
    gc, face_f, face_l, gd1, *more = center(1, n, c1, exchange(st), mom21)
    faces = (face_f, face_l)
    dk1, de1 = side_grads(gc, grown1, p1, we1, gw1, momw1, smean1, sloc1, seen1)
    halos, de1, dk1 = spread(gc, *faces, de1, dk1)
    gm1, n1, st = first_back(1, gc, halos, a1, wm1, mom11, *more)
    st = exchange(st)
    if owned:
        one = core_sums(*pack_grads(1, a1, gm1, mom11, de1, dk1), shape)
        one, st = lax.optimization_barrier((one, st))
        one = owner_parts(one, shape)
        pooled = st[:, 2 * halves :, :].reshape(devices, -1)[:, : clips * share_w]
        pooled = pooled.reshape(devices, clips, share_w).transpose(1, 0, 2).reshape(clips, wide)
    gz0, u0, p0, gn1, st, *dr1 = between(
        n1, a1, st, mom11, wr1, x1, gz1, c0, mom20, we0, momw0, smean0
    )
    if owned:
        st, one = lax.optimization_barrier((st, one))
    st = exchange(st)
    if owned:
        dr1 = core_sums(*dr1, shape)
        dr1, st = lax.optimization_barrier((dr1, st))
        dr1 = owner_parts(dr1, shape)
    n, gw0, st = second(0, u0, c0, st, we0, momw0, smean0, mom20)
    gc, *faces, gd0 = center(0, n, c0, exchange(st), mom20)
    dk0, de0 = side_grads(gc, grown0, p0, we0, gw0, momw0, smean0, sloc0, seen0)
    halos, de0, dk0 = spread(gc, *faces, de0, dk0)
    gm0, n1, st = first_back(0, gc, halos, a0, wm0, mom10)
    st = exchange(st)
    home = lambda field: field.transpose(2, 0, 1, 3)
    if owned:
        zero = core_sums(*pack_grads(0, a0, gm0, mom10, de0, dk0), shape)
        zero, n1, dr1 = lax.optimization_barrier((zero, n1, dr1))
        zero = owner_parts(zero, shape)
        ga0, gn0, mine, theirs = last_weight(n1, a0, st, mom10)
        tail = owner_parts(core_sums(mine, theirs, shape), shape)
        gx = last(ga0, gz0, wr0)
        pooled = pooled / (counts * float(rows * shape[1] * width))[:, None]
        values = call(
            k_update,
            "update",
            near(*[weights[i].shape for i in range(10)] * 3),
            [(me, SM)]
            + near(zero, one, tail, dr1, gn0, gn1, gd0, gd1, gw0, gw1, *weights, *momenta),
            limit=12,
        )
        return (home(out), pooled, home(gx), *values)

    ga0, gn0, dr0 = last_weight(n1, a0, st, mom10)
    gx = last(ga0, gz0, wr0)
    dm0, dm1 = mix_grad(0, a0, gm0, mom10), mix_grad(1, a1, gm1, mom11)
    pooled = pooled / (counts * float(rows * shape[1] * width))[:, None]

    def own(full):
        parts = full.reshape((devices, full.shape[0] // devices) + full.shape[1:])
        return jnp.sum(lax.all_to_all(parts, AX, 0, 0), axis=0)

    deltas = [
        jnp.stack([own(dr0), own(dr1[0])]),
        jnp.stack([own(dm0), own(dm1)]),
        jnp.stack([own(dk0[:27].T), own(dk1[:27].T)]),
        jnp.stack([own(de0), own(de1)]),
    ]

    def mine(vec0, vec1, row):
        share = vec0.shape[1] // devices
        both = jnp.stack([vec0[row], vec1[row]])
        return lax.dynamic_slice_in_dim(both, rank * share, share, axis=1)

    for first_part, second_part in ((gn0, gn1), (gd0, gd1), (gw0, gw1)):
        deltas.append(mine(first_part, second_part, 0))
        deltas.append(mine(first_part, second_part, 1))
    velocity = [MOMENTUM * momenta[i] + deltas[i] for i in range(10)]
    updated = [
        weights[i] - LEARN_RATE * (deltas[i] + MOMENTUM * velocity[i]) for i in range(10)
    ]
    return (home(out), pooled, home(gx), *deltas, *velocity, *updated)


def solution(mesh):
    field = P("dp", "fsdp", None, None)
    mat = P(None, AX, None)
    vec = P(None, AX)
    group = (mat,) * 4 + (vec,) * 6
    return jax.shard_map(
        body,
        mesh=mesh,
        in_specs=(field, field, P()) + group * 2,
        out_specs=(field, P(), field) + group * 3,
        check_vma=False,
    )
```

time: 2210 us -> 510 us (0.23)
  blocking collectives: 844 us -> 34.4 us
  waiting for transfers between devices: 847 us -> 111 us
  Pallas kernels: 0 us -> 229 us
  matrix products: 159 us -> 0.98 us
  local copies, waits for them, and re-layouts: 161 us -> 13.3 us
  other arithmetic: 134 us -> 13.1 us
  starting transfers between devices: 35.9 us -> 82.8 us
    reduce_scatter x4 -> x0, waiting for transfers between devices: 492 us -> none  [the longest x2 265 us: scatter_gradients(): lax.psum_scatter(expand_delta, ('dp', 'fsdp'), scatter_dimension=0, tiled...]
    psum x11 -> x0, blocking collectives: 433 us -> none  [the longest x6 231 us: batch_moments(): totals = lax.psum(jnp.sum(values, axis=0), ('dp', 'fsdp'))]
    unnamed x13 -> x1, waiting for transfers between devices: 265 us -> 0.02 us
    unnamed x6 -> x0, blocking collectives: 250 us -> none
    pallas_call x0 -> x28, Pallas kernels: none -> 229 us  [call(): pl.pallas_call(run, in_specs=[spec if spec is SM else HB for _, spec in i...]
    all_gather x4 -> x0, blocking collectives: 161 us -> none  [the longest x2 82.5 us: gather_forward(): lax.all_gather(mixing_part, ('dp', 'fsdp'), axis=0, tiled=True)]
    dot_general x18 -> x1, matrix products: 145 us -> 0.98 us  [body(): jnp.dot(jnp.concatenate([hot] * (8 // frames), axis=1), pool, precision=H...]
    reduce_sum x18 -> x1, other arithmetic: 89 us -> 0.11 us  [body(): jnp.sum((clip_index[None, :] == labels[:, None]).astype(F32), axis=1)]
  transfers between devices with their start and end apart: 27 -> 41, of which waited for: 12 -> 26; matrix products, arithmetic and copies ran while one was open for 14% -> 4% of each run, Pallas kernels for 0% -> 27%
where the time goes in v2:
time: 510 us; the launch traced here: 500 us
  Pallas kernels  229 us (45%)
  waiting for transfers between devices  111 us (22%)
  starting transfers between devices  82.8 us (16%)
  blocking collectives  34.4 us (7%)
  between operations  15.4 us (3%)
  local copies, waits for them, and re-layouts  13.3 us (3%)
  other arithmetic  13.1 us (3%)
    pallas_call x28, Pallas kernels, call(): pl.pallas_call(run, in_specs=[spec if spec is SM else HB for _, spec in i...  229 us
    ppermute x8, waiting for transfers between devices, halo(): move = lambda value, step: lax.ppermute(value, AX, perm(step, shape))  43.9 us
    all_to_all x9, starting transfers between devices, exchange(): return lax.all_to_all(rows, AX, 0, 0)  39 us
    all_to_all x3, blocking collectives, exchange(): return lax.all_to_all(rows, AX, 0, 0)  34.4 us
    all_to_all x9, waiting for transfers between devices, exchange(): return lax.all_to_all(rows, AX, 0, 0)  33.1 us
    ppermute x8, starting transfers between devices, halo(): move = lambda value, step: lax.ppermute(value, AX, perm(step, shape))  16.8 us
    ppermute x7, waiting for transfers between devices, meet(): lax.ppermute(value, AX, [(i, i ^ mask) for i in range(devices)])  16.3 us
    all_to_all x4, starting transfers between devices, owner_parts(): return lax.all_to_all(parts, 'dp', 0, 0)  16.2 us
  transfers between devices with their start and end apart: 41, of which 26 were waited for; matrix products, arithmetic and copies ran while one was open for 4% of the time, Pallas kernels for 27%

profile of v2, /device:TPU:0, one launch (start us, length us, event | category | flops | bytes accessed | tf_op | source)
XLA Modules:
  0.0 500.1 jit_solution(10680445539354701869)
XLA Ops:
  26.9 4.6 collective-permute-done.3.refs_1_
  42.0 10.9 %first.1 = (f32[2,1568,128]{2,1,0:T(8,128)}, f32[2,392,128]{2,1,0:T(8,128)}, f32[2,392,128]{2,1,0:T(8,128)}, f32[32,4,128]{2,1,0:T(4,128)}, f32[1024,256]{1,0:T(8,128)}) custom-call(s32[1]{0:T(128)} %bitcast.2.refs_0_, f32[14,28,4,1024]{3,2,1,0:T(4,128)} %bitcast.58, f32[16,48,256]{2,1,0:T(8,128)} %stack.99.refs_2_.refs_1_, f32[16,48,256]{2,1,0:T(8,128)} %copy-done.10), custom_call_target="tpu_custom_call" | custom-call | flops 1000 | bytes 1000 | tf_op jit(solution)/shard_map/first/pallas_call | solution.py:1070
  57.4 5.7 %all-to-all-start = ((f32[32,4,128]{2,1,0:T(4,128)}), f32[32,4,128]{2,1,0:T(4,128)S(1)}, u32[]{:S(2)}, u32[]{:S(2)}) async-start(f32[32,4,128]{2,1,0:T(4,128)} %get-tuple-element.175), calls=%async_computation | async-start | bytes 131072 | tf_op jit(solution)/shard_map/all_to_all | solution.py:868
  65.3 14.6 %collective-permute-done.7.refs_2_ = f32[2,392,128]{2,1,0:T(8,128)S(1)} collective-permute-done((f32[2,392,128]{2,1,0:T(8,128)}, f32[2,392,128]{2,1,0:T(8,128)S(1)}, u32[]{:S(2)}, u32[]{:S(2)}) %collective-permute-start.7) | collective-permute-done | bytes 401440 | tf_op jit(solution)/shard_map/ppermute | solution.py:894
  80.0 4.0 collective-permute-done.8.refs_3_
  86.2 12.4 %mix.2 = (f32[2,1568,128]{2,1,0:T(8,128)}, f32[2,1792,128]{2,1,0:T(8,128)}, f32[2,1792,128]{2,1,0:T(8,128)}, f32[2,1792,128]{2,1,0:T(8,128)}, f32[8,256]{1,0:T(8,128)}, /*index=5*/f32[32,4,128]{2,1,0:T(4,128)}) custom-call(f32[14]{0:T(128)S(1)} %concatenate.13.refs_0_, f32[2,1568,128]{2,1,0:T(8,128)} %get-tuple-element.172.refs_1_.refs_8_.refs_2_, ...), custom_call_target="tpu_custom_call" | custom-call | flops 1000 | bytes 1000 | tf_op jit(solution)/shard_map/mix/pallas_call | solution.py:1070
  101.2 4.3 open_later.1
  109.2 7.5 %expand.2 = (f32[8,256]{1,0:T(8,128)}, f32[8,1024]{1,0:T(8,128)}, f32[8,256]{1,0:T(8,128)}, f32[256,1024]{1,0:T(8,128)}, f32[32,10,128]{2,1,0:T(8,128)}) custom-call(f32[2,1568,128]{2,1,0:T(8,128)} %get-tuple-element.178.refs_0_.refs_3_.refs_1_, f32[32,4,128]{2,1,0:T(4,128)} %copy-done.26, ...), custom_call_target="tpu_custom_call" | custom-call | flops 1000 | bytes 1000 | tf_op jit(solution)/shard_map/expand/pallas_call | solution.py:1070
  119.7 9.5 %widen.2.refs_0_ = f32[1568,1024]{1,0:T(8,128)} custom-call(f32[2,1568,128]{2,1,0:T(8,128)} %get-tuple-element.178.refs_0_.refs_3_.refs_1_, f32[8,256]{1,0:T(8,128)} %get-tuple-element.182.refs_1_.refs_10_.refs_6_.refs_4_, f32[32,256]{1,0:T(8,128)} %get-tuple-element.328.refs_10_.refs_3_.refs_2_.refs_11_.refs_7_.refs_5_, ...), custom_call_target="tpu_custom_call" | custom-call | flops 2147483648 | bytes 1000 | tf_op jit(solution)/shard_map/widen/pallas_call | solution.py:1070
  131.0 13.0 %join.1 = (f32[1568,1024]{1,0:T(8,128)}, f32[2,1568,128]{2,1,0:T(8,128)}, f32[2,392,128]{2,1,0:T(8,128)}, f32[2,392,128]{2,1,0:T(8,128)}, f32[8,1024]{1,0:T(8,12...) custom-call(f32[1568,1024]{1,0:T(8,128)} %widen.2.refs_0_, f32[14,28,4,1024]{3,2,1,0:T(4,128)} %bitcast.59, ...), custom_call_target="tpu_custom_call" | custom-call | flops 1000 | bytes 1000 | tf_op jit(solution)/shard_map/join/pallas_call | solution.py:1070
  149.7 6.8 %all-to-all-start.3 = ((f32[32,4,128]{2,1,0:T(4,128)}), f32[32,4,128]{2,1,0:T(4,128)S(1)}, u32[]{:S(2)}, u32[]{:S(2)}) async-start(f32[32,4,128]{2,1,0:T(4,128)} %get-tuple-element.191), calls=%async_computation.3 | async-start | bytes 131072 | tf_op jit(solution)/shard_map/all_to_all | solution.py:868
  156.6 9.1 %collective-permute-done.11.refs_2_ = f32[2,392,128]{2,1,0:T(8,128)S(1)} collective-permute-done((f32[2,392,128]{2,1,0:T(8,128)}, f32[2,392,128]{2,1,0:T(8,128)S(1)}, u32[]{:S(2)}, u32[]{:S(2)}) %collective-permute-start.11) | collective-permute-done | bytes 401440 | tf_op jit(solution)/shard_map/ppermute | solution.py:894
  169.5 12.3 %mix.3 = (f32[2,1568,128]{2,1,0:T(8,128)}, f32[2,1792,128]{2,1,0:T(8,128)}, f32[2,1792,128]{2,1,0:T(8,128)}, f32[2,1792,128]{2,1,0:T(8,128)}, f32[8,256]{1,0:T(8,128)}, /*index=5*/f32[32,4,128]{2,1,0:T(4,128)}) custom-call(f32[14]{0:T(128)S(1)} %concatenate.13.refs_0_, f32[2,1568,128]{2,1,0:T(8,128)} %get-tuple-element.188.refs_1_.refs_8_.refs_2_, ...), custom_call_target="tpu_custom_call" | custom-call | flops 1000 | bytes 1000 | tf_op jit(solution)/shard_map/mix/pallas_call | solution.py:1070
  181.8 12.2 %all_to_all.80.refs_1_ = f32[32,4,128]{2,1,0:T(4,128)} all-to-all(f32[32,4,128]{2,1,0:T(4,128)} %get-tuple-element.194), channel_id=1, replica_groups=mesh['dp'=16,'fsdp'=2] {'dp','fsdp'}, dimensions={0} | all-to-all | bytes 131072 | tf_op jit(solution)/shard_map/all_to_all | solution.py:868
  194.0 7.4 %expand.3 = (f32[8,256]{1,0:T(8,128)}, f32[8,1024]{1,0:T(8,128)}, f32[8,256]{1,0:T(8,128)}, f32[256,1024]{1,0:T(8,128)}, f32[32,10,128]{2,1,0:T(8,128)}) custom-call(f32[2,1568,128]{2,1,0:T(8,128)} %get-tuple-element.193.refs_0_.refs_3_.refs_1_, f32[32,4,128]{2,1,0:T(4,128)} %all_to_all.80.refs_1_, ...), custom_call_target="tpu_custom_call" | custom-call | flops 1000 | bytes 1000 | tf_op jit(solution)/shard_map/expand/pallas_call | solution.py:1070
  204.3 9.5 %widen.3.refs_0_ = f32[1568,1024]{1,0:T(8,128)} custom-call(f32[2,1568,128]{2,1,0:T(8,128)} %get-tuple-element.193.refs_0_.refs_3_.refs_1_, f32[8,256]{1,0:T(8,128)} %get-tuple-element.196.refs_1_.refs_8_.refs_6_.refs_4_, f32[32,256]{1,0:T(8,128)} %get-tuple-element.327.refs_10_.refs_3_.refs_2_.refs_9_.refs_7_, ...), custom_call_target="tpu_custom_call" | custom-call | flops 2147483648 | bytes 1000 | tf_op jit(solution)/shard_map/widen/pallas_call | solution.py:1070
  215.6 17.3 %turn.1 = (f32[14,28,4,1024]{3,2,1,0:T(4,128)}, f32[1568,1024]{1,0:T(8,128)}, f32[2,1568,128]{2,1,0:T(8,128)}, f32[256,1024]{1,0:T(8,128)}, f32[8,1024]{1,0:T(8,...) custom-call(f32[1568,1024]{1,0:T(8,128)} %widen.3.refs_0_, ...), custom_call_target="tpu_custom_call" | custom-call | flops 1000 | bytes 1000 | tf_op jit(solution)/shard_map/turn/pallas_call | solution.py:1070
  232.8 4.9 all-to-all-start.6
  239.8 8.5 %all-to-all-done.6.refs_2_ = f32[32,16,128]{2,1,0:T(8,128)S(1)} async-done(((f32[32,16,128]{2,1,0:T(8,128)}), f32[32,16,128]{2,1,0:T(8,128)S(1)}, u32[]{:S(2)}, u32[]{:S(2)}) %all-to-all-start.6) | async-done | bytes 262176 | tf_op jit(solution)/shard_map/all_to_all | solution.py:868
  249.0 6.8 %second.2 = (f32[2,1568,128]{2,1,0:T(8,128)}, f32[8,1024]{1,0:T(8,128)}, f32[32,7,128]{2,1,0:T(8,128)}) custom-call(f32[2,1568,128]{2,1,0:T(8,128)} %get-tuple-element.202.refs_0_, f32[2,1568,128]{2,1,0:T(8,128)} %get-tuple-element.193.refs_0_.refs_3_.refs_1_, f32[32,16,128]{2,1,0:T(8,128)} %copy-done.5, ...), custom_call_target="tpu_custom_call" | custom-call | flops 1000 | bytes 1000 | tf_op jit(solution)/shard_map/second/pallas_call | solution.py:1070
  255.8 11.5 %all_to_all.81.refs_2_ = f32[32,7,128]{2,1,0:T(8,128)} all-to-all(f32[32,7,128]{2,1,0:T(8,128)} %get-tuple-element.208), channel_id=1, replica_groups=mesh['dp'=16,'fsdp'=2] {'dp','fsdp'}, dimensions={0} | all-to-all | bytes 229376 | tf_op jit(solution)/shard_map/all_to_all | solution.py:868
  267.3 3.8 center.2
  275.8 11.0 %side_grads.2 = (f32[128,256]{1,0:T(8,128)}, f32[256,1024]{1,0:T(8,128)}) custom-call(f32[14]{0:T(128)S(1)} %concatenate.13.refs_0_, f32[2,1568,128]{2,1,0:T(8,128)} %get-tuple-element.209.refs_1_, f32[2,1792,128]{2,1,0:T(8,128)} %get-tuple-element.212.refs_2_, f32[2,1792,128]{2,1,0:T(8,128)} %get-tuple-element.213.refs_3_, ...), custom_call_target="tpu_custom_call" | custom-call | flops 4294967296 | bytes 1000 | tf_op jit(solution)/shard_map/side_grads/pallas_call | solution.py:1070
  286.9 4.3 collective-permute-done.15.refs_2_
  295.0 10.2 %first_back.2 = (f32[2,1568,128]{2,1,0:T(8,128)}, f32[2,1568,128]{2,1,0:T(8,128)}, f32[32,7,128]{2,1,0:T(8,128)}) custom-call(f32[14]{0:T(128)S(1)} %concatenate.13.refs_0_, f32[2,1568,128]{2,1,0:T(8,128)} %get-tuple-element.209.refs_1_, f32[2,392,128]{2,1,0:T(8,128)} %copy-done.11, f32[2,392,128]{2,1,0:T(8,128)} %copy-done.13, f32[2,112,128]{2,1,0:T(8,128)} %copy-done.19, ...), custom_call_target="tpu_custom_call" | custom-call | flops 1000 | bytes 1000 | tf_op jit(solution)/shard_map/first_back/pallas_call | solution.py:1070
  305.2 5.1 %pack_grads.2 = (f32[16,48,256]{2,1,0:T(8,128)}, f32[16,48,256]{2,1,0:T(8,128)}) custom-call(s32[1]{0:T(128)} %bitcast.2.refs_0_, f32[2,1568,128]{2,1,0:T(8,128)} %get-tuple-element.188.refs_1_.refs_8_.refs_2_, f32[2,1568,128]{2,1,0:T(8,128)} %get-tuple-element.224.refs_2_, f32[32,256]{1,0:T(8,128)} %get-tuple-element.327.refs_10_.refs_3_.refs_2_.refs_9_.refs_7_, ...), custom_call_target="tpu_custom_call" | custom-call | flops 2147483648 | bytes 1000 | tf_op jit(solution)/shard_map/pack_grads/pallas_call | solution.py:1070
  315.5 6.1 %all-to-all-done.8.refs_6_ = f32[32,7,128]{2,1,0:T(8,128)S(1)} async-done(((f32[32,7,128]{2,1,0:T(8,128)}), f32[32,7,128]{2,1,0:T(8,128)S(1)}, u32[]{:S(2)}, u32[]{:S(2)}) %all-to-all-start.8) | async-done | bytes 114720 | tf_op jit(solution)/shard_map/all_to_all | solution.py:868
  321.6 3.9 all-to-all-start.9
  325.5 22.7 %between.1 = (f32[1568,1024]{1,0:T(8,128)}, f32[2,1568,128]{2,1,0:T(8,128)}, f32[256,1024]{1,0:T(8,128)}, f32[8,256]{1,0:T(8,128)}, f32[32,16,128]{2,1,0:T(8,128...) custom-call(s32[1]{0:T(128)} %bitcast.2.refs_0_, f32[2,1568,128]{2,1,0:T(8,128)} %get-tuple-element.231.refs_1_, ...), custom_call_target="tpu_custom_call" | custom-call | flops 1000 | bytes 1000 | tf_op jit(solution)/shard_map/between/pallas_call | solution.py:1070
  348.5 5.9 %all-to-all-start.10 = ((f32[32,16,128]{2,1,0:T(8,128)}), f32[32,16,128]{2,1,0:T(8,128)S(1)}, u32[]{:S(2)}, u32[]{:S(2)}) async-start(f32[32,16,128]{2,1,0:T(8,128)} %get-tuple-element.240), calls=%async_computation.10 | async-start | bytes 524288 | tf_op jit(solution)/shard_map/all_to_all | solution.py:868
  356.3 8.7 %all-to-all-done.10.refs_2_ = f32[32,16,128]{2,1,0:T(8,128)S(1)} async-done(((f32[32,16,128]{2,1,0:T(8,128)}), f32[32,16,128]{2,1,0:T(8,128)S(1)}, u32[]{:S(2)}, u32[]{:S(2)}) %all-to-all-start.10) | async-done | bytes 262176 | tf_op jit(solution)/shard_map/all_to_all | solution.py:868
  365.6 6.7 %second.3 = (f32[2,1568,128]{2,1,0:T(8,128)}, f32[8,1024]{1,0:T(8,128)}, f32[32,4,128]{2,1,0:T(4,128)}) custom-call(f32[2,1568,128]{2,1,0:T(8,128)} %get-tuple-element.235.refs_0_, f32[2,1568,128]{2,1,0:T(8,128)} %get-tuple-element.178.refs_0_.refs_3_.refs_1_, f32[32,16,128]{2,1,0:T(8,128)} %copy-done.6, ...), custom_call_target="tpu_custom_call" | custom-call | flops 1000 | bytes 1000 | tf_op jit(solution)/shard_map/second/pallas_call | solution.py:1070
  372.4 10.7 %all_to_all.82.refs_2_ = f32[32,4,128]{2,1,0:T(4,128)} all-to-all(f32[32,4,128]{2,1,0:T(4,128)} %get-tuple-element.243), channel_id=1, replica_groups=mesh['dp'=16,'fsdp'=2] {'dp','fsdp'}, dimensions={0} | all-to-all | bytes 131072 | tf_op jit(solution)/shard_map/all_to_all | solution.py:868
  386.6 3.7 center.3
  390.3 3.7 collective-permute-start.21
  396.4 11.2 %side_grads.3 = (f32[128,256]{1,0:T(8,128)}, f32[256,1024]{1,0:T(8,128)}) custom-call(f32[14]{0:T(128)S(1)} %concatenate.13.refs_0_, f32[2,1568,128]{2,1,0:T(8,128)} %get-tuple-element.244.refs_1_, f32[2,1792,128]{2,1,0:T(8,128)} %get-tuple-element.247.refs_2_, f32[2,1792,128]{2,1,0:T(8,128)} %get-tuple-element.248.refs_3_, ...), custom_call_target="tpu_custom_call" | custom-call | flops 4294967296 | bytes 1000 | tf_op jit(solution)/shard_map/side_grads/pallas_call | solution.py:1070
  407.6 6.4 %collective-permute-done.21.refs_2_ = f32[2,392,128]{2,1,0:T(8,128)S(1)} collective-permute-done((f32[2,392,128]{2,1,0:T(8,128)}, f32[2,392,128]{2,1,0:T(8,128)S(1)}, u32[]{:S(2)}, u32[]{:S(2)}) %collective-permute-start.21) | collective-permute-done | bytes 401440 | tf_op jit(solution)/shard_map/ppermute | solution.py:894
  417.8 10.1 %first_back.3 = (f32[2,1568,128]{2,1,0:T(8,128)}, f32[2,1568,128]{2,1,0:T(8,128)}, f32[32,4,128]{2,1,0:T(4,128)}) custom-call(f32[14]{0:T(128)S(1)} %concatenate.13.refs_0_, f32[2,1568,128]{2,1,0:T(8,128)} %get-tuple-element.244.refs_1_, f32[2,392,128]{2,1,0:T(8,128)} %copy-done.12, f32[2,392,128]{2,1,0:T(8,128)} %copy-done.14, f32[2,112,128]{2,1,0:T(8,128)} %copy-done.20, ...), custom_call_target="tpu_custom_call" | custom-call | flops 1000 | bytes 1000 | tf_op jit(solution)/shard_map/first_back/pallas_call | solution.py:1070
  427.9 5.1 %pack_grads.3 = (f32[16,48,256]{2,1,0:T(8,128)}, f32[16,48,256]{2,1,0:T(8,128)}) custom-call(s32[1]{0:T(128)} %bitcast.2.refs_0_, f32[2,1568,128]{2,1,0:T(8,128)} %get-tuple-element.172.refs_1_.refs_8_.refs_2_, f32[2,1568,128]{2,1,0:T(8,128)} %get-tuple-element.258.refs_2_, f32[32,256]{1,0:T(8,128)} %get-tuple-element.328.refs_10_.refs_3_.refs_2_.refs_11_.refs_7_.refs_5_, ...), custom_call_target="tpu_custom_call" | custom-call | flops 2147483648 | bytes 1000 | tf_op jit(solution)/shard_map/pack_grads/pallas_call | solution.py:1070
  433.3 4.4 all-to-all-start.13
  439.8 5.3 %all-to-all-done.13.refs_4_ = f32[32,4,128]{2,1,0:T(4,128)S(1)} async-done(((f32[32,4,128]{2,1,0:T(4,128)}), f32[32,4,128]{2,1,0:T(4,128)S(1)}, u32[]{:S(2)}, u32[]{:S(2)}) %all-to-all-start.13) | async-done | bytes 65568 | tf_op jit(solution)/shard_map/all_to_all | solution.py:868
  445.1 3.6 all-to-all-start.14
  448.8 8.5 %last_weight.1 = (f32[2,1568,128]{2,1,0:T(8,128)}, f32[8,256]{1,0:T(8,128)}, f32[16,32,256]{2,1,0:T(8,128)}, f32[16,32,256]{2,1,0:T(8,128)}) custom-call(s32[1]{0:T(128)} %bitcast.2.refs_0_, f32[2,1568,128]{2,1,0:T(8,128)} %get-tuple-element.265.refs_1_, f32[2,1568,128]{2,1,0:T(8,128)} %get-tuple-element.172.refs_1_.refs_8_.refs_2_, ...), custom_call_target="tpu_custom_call" | custom-call | flops 1000 | bytes 1000 | tf_op jit(solution)/shard_map/last_weight/pallas_call | solution.py:1070
  461.4 7.4 %all-to-all-done.14.refs_1_ = f32[16,48,256]{2,1,0:T(8,128)S(1)} async-done(((f32[16,48,256]{2,1,0:T(8,128)}), f32[16,48,256]{2,1,0:T(8,128)S(1)}, u32[]{:S(2)}, u32[]{:S(2)}) %all-to-all-start.14) | async-done | bytes 786464 | tf_op jit(solution)/shard_map/all_to_all | solution.py:926
  468.8 5.1 %all-to-all-start.15 = ((f32[16,32,256]{2,1,0:T(8,128)}), f32[16,32,256]{2,1,0:T(8,128)S(1)}, u32[]{:S(2)}, u32[]{:S(2)}) async-start(f32[16,32,256]{2,1,0:T(8,128)} %add.25), calls=%async_computation.15 | async-start | bytes 1048576 | tf_op jit(solution)/shard_map/all_to_all | solution.py:926
  475.1 8.5 %last.1 = f32[14,28,4,1024]{3,2,1,0:T(4,128)} custom-call(f32[2,1568,128]{2,1,0:T(8,128)} %get-tuple-element.267.refs_0_, f32[1568,1024]{1,0:T(8,128)} %get-tuple-element.268.refs_1_, f32[1024,256]{1,0:T(8,128)} %get-tuple-element.269.refs_2_), custom_call_target="tpu_custom_call" | custom-call | flops 2147483648 | bytes 1000 | tf_op jit(solution)/shard_map/last/pallas_call | solution.py:1070
  483.6 4.6 all-to-all-done.15.refs_3_
  489.0 3.8 update.1
  (190 shorter events, 101.5 us)
Async XLA Ops:
  7.2 31.5 %copy-start.38 = (s32[64]{0:T(128)S(1)}, s32[64]{0:T(128)}, u32[]{:S(2)}) copy-start(s32[64]{0:T(128)} %param.25) | copy-start | bytes 772
  7.2 94.0 %all-gather.3.cloned.1.call-start = ((), (), s32[]{:S(2)}) async-start(), calls=%async_computation.16 | async-start | bytes 4595712 | tf_op jit(solution)/shard_map/all_gather | solution.py:1157
  9.3 5.7 %collective-permute-start = (f32[1,48,256]{2,1,0:T(8,128)}, f32[1,48,256]{2,1,0:T(8,128)S(1)}, u32[]{:S(2)}, u32[]{:S(2)}) collective-permute-start(f32[1,48,256]{2,1,0:T(8,128)} %get-tuple-element.171.refs_0_), channel_id=1, source_target_pairs={{0,8},{1,9},{2,10},{3,11},{4,12},{5,13},{6,14},{7,15},{8,0},{9,1},... | collective-permute-start | bytes 147464 | tf_op jit(solution)/shard_map/ppermute | solution.py:875
  12.4 6.1 %collective-permute-start.1 = (f32[1,48,256]{2,1,0:T(8,128)}, f32[1,48,256]{2,1,0:T(8,128)S(1)}, u32[]{:S(2)}, u32[]{:S(2)}) collective-permute-start(f32[1,48,256]{2,1,0:T(8,128)} %get-tuple-element.171.refs_0_), channel_id=1, source_target_pairs={{0,16},{1,17},{2,18},{3,19},{4,20},{5,21},{6,22},{7,23},{8,24},{9,... | collective-permute-start | bytes 147464 | tf_op jit(solution)/shard_map/ppermute | solution.py:875
  15.0 6.1 %collective-permute-start.2 = (f32[1,48,256]{2,1,0:T(8,128)}, f32[1,48,256]{2,1,0:T(8,128)S(1)}, u32[]{:S(2)}, u32[]{:S(2)}) collective-permute-start(f32[1,48,256]{2,1,0:T(8,128)} %get-tuple-element.171.refs_0_), channel_id=1, source_target_pairs={{0,24},{1,25},{2,26},{3,27},{4,28},{5,29},{6,30},{7,31},{8,16},{9,... | collective-permute-start | bytes 147464 | tf_op jit(solution)/shard_map/ppermute | solution.py:875
  15.0 6.1 %copy-start.35 = (f32[1,48,256]{2,1,0:T(8,128)}, f32[1,48,256]{2,1,0:T(8,128)S(1)}, u32[]{:S(2)}) copy-start(f32[1,48,256]{2,1,0:T(8,128)S(1)} %collective-permute-done.refs_1_) | copy-start | bytes 147460
  23.3 8.1 %collective-permute-start.3 = (f32[4,48,256]{2,1,0:T(8,128)}, f32[4,48,256]{2,1,0:T(8,128)S(1)}, u32[]{:S(2)}, u32[]{:S(2)}) collective-permute-start(f32[4,48,256]{2,1,0:T(8,128)} %stack.98.refs_0_), channel_id=1, source_target_pairs={{0,2},{1,3},{2,0},{3,1},{4,6},{5,7},{6,4},{7,5},{8,10},{9,11},{10,... | collective-permute-start | bytes 589832 | tf_op jit(solution)/shard_map/ppermute | solution.py:875
  24.9 10.1 %collective-permute-start.4 = (f32[4,48,256]{2,1,0:T(8,128)}, f32[4,48,256]{2,1,0:T(8,128)S(1)}, u32[]{:S(2)}, u32[]{:S(2)}) collective-permute-start(f32[4,48,256]{2,1,0:T(8,128)} %stack.98.refs_0_), channel_id=1, source_target_pairs={{0,4},{1,5},{2,6},{3,7},{4,0},{5,1},{6,2},{7,3},{8,12},{9,13},{10,... | collective-permute-start | bytes 589832 | tf_op jit(solution)/shard_map/ppermute | solution.py:875
  26.4 8.6 %collective-permute-start.5 = (f32[4,48,256]{2,1,0:T(8,128)}, f32[4,48,256]{2,1,0:T(8,128)S(1)}, u32[]{:S(2)}, u32[]{:S(2)}) collective-permute-start(f32[4,48,256]{2,1,0:T(8,128)} %stack.98.refs_0_), channel_id=1, source_target_pairs={{0,6},{1,7},{2,4},{3,5},{4,2},{5,3},{6,0},{7,1},{8,14},{9,15},{10,... | collective-permute-start | bytes 589832 | tf_op jit(solution)/shard_map/ppermute | solution.py:875
  38.6 2.6 collective-permute-start.6
  52.9 27.1 %collective-permute-start.7 = (f32[2,392,128]{2,1,0:T(8,128)}, f32[2,392,128]{2,1,0:T(8,128)S(1)}, u32[]{:S(2)}, u32[]{:S(2)}) collective-permute-start(f32[2,392,128]{2,1,0:T(8,128)} %get-tuple-element.173), channel_id=1, source_target_pairs={{0,2},{1,3},{2,4},{3,5},{4,6},{5,7},{6,8},{7,9},{8,10},{9,11},{10,... | collective-permute-start | bytes 1204232 | tf_op jit(solution)/shard_map/ppermute | solution.py:894
  55.0 28.9 %collective-permute-start.8 = (f32[2,392,128]{2,1,0:T(8,128)}, f32[2,392,128]{2,1,0:T(8,128)S(1)}, u32[]{:S(2)}, u32[]{:S(2)}) collective-permute-start(f32[2,392,128]{2,1,0:T(8,128)} %get-tuple-element.174), channel_id=1, source_target_pairs={{2,0},{3,1},{4,2},{5,3},{6,4},{7,5},{8,6},{9,7},{10,8},{11,9},{12,... | collective-permute-start | bytes 1204232 | tf_op jit(solution)/shard_map/ppermute | solution.py:894
  57.3 28.2 %collective-permute-start.9 = (f32[2,112,128]{2,1,0:T(8,128)S(1)}, f32[2,112,128]{2,1,0:T(8,128)S(1)}, u32[]{:S(2)}, u32[]{:S(2)}) collective-permute-start(f32[2,112,128]{2,1,0:T(8,128)S(1)} %slice_select_fusion.3), channel_id=1, source_target_pairs={{0,1},{1,0},{2,3},{3,2},{4,5},{5,4},{6,7},{7,6},{8,9},{9,8},{10,11... | collective-permute-start | bytes 344072 | tf_op jit(solution)/shard_map/ppermute | solution.py:905
  57.4 28.2 %all-to-all-start = ((f32[32,4,128]{2,1,0:T(4,128)}), f32[32,4,128]{2,1,0:T(4,128)S(1)}, u32[]{:S(2)}, u32[]{:S(2)}) async-start(f32[32,4,128]{2,1,0:T(4,128)} %get-tuple-element.175), calls=%async_computation | async-start | bytes 131072 | tf_op jit(solution)/shard_map/all_to_all | solution.py:868
  84.0 1.6 collective-permute-start.10
  98.6 10.0 %all-to-all-start.1 = ((f32[32,4,128]{2,1,0:T(4,128)}), f32[32,4,128]{2,1,0:T(4,128)S(1)}, u32[]{:S(2)}, u32[]{:S(2)}) async-start(f32[32,4,128]{2,1,0:T(4,128)} %get-tuple-element.179), calls=%async_computation.1 | async-start | bytes 131072 | tf_op jit(solution)/shard_map/all_to_all | solution.py:868
  116.7 13.6 %all-to-all-start.2 = ((f32[32,10,128]{2,1,0:T(8,128)}), f32[32,10,128]{2,1,0:T(8,128)S(1)}, u32[]{:S(2)}, u32[]{:S(2)}) async-start(f32[32,10,128]{2,1,0:T(8,128)} %get-tuple-element.184), calls=%async_computation.2 | async-start | bytes 524288 | tf_op jit(solution)/shard_map/all_to_all | solution.py:868
  119.7 9.6 %copy-start.34 = (f32[2,8,1024]{2,1,0:T(8,128)S(1)}, f32[2,8,1024]{2,1,0:T(8,128)}, u32[]{:S(2)}) copy-start(f32[2,8,1024]{2,1,0:T(8,128)} %get-tuple-element.186) | copy-start | bytes 196612
  143.9 21.8 %collective-permute-start.11 = (f32[2,392,128]{2,1,0:T(8,128)}, f32[2,392,128]{2,1,0:T(8,128)S(1)}, u32[]{:S(2)}, u32[]{:S(2)}) collective-permute-start(f32[2,392,128]{2,1,0:T(8,128)} %get-tuple-element.189), channel_id=1, source_target_pairs={{0,2},{1,3},{2,4},{3,5},{4,6},{5,7},{6,8},{7,9},{8,10},{9,11},{10,... | collective-permute-start | bytes 1204232 | tf_op jit(solution)/shard_map/ppermute | solution.py:894
  147.4 20.2 %collective-permute-start.12 = (f32[2,392,128]{2,1,0:T(8,128)}, f32[2,392,128]{2,1,0:T(8,128)S(1)}, u32[]{:S(2)}, u32[]{:S(2)}) collective-permute-start(f32[2,392,128]{2,1,0:T(8,128)} %get-tuple-element.190), channel_id=1, source_target_pairs={{2,0},{3,1},{4,2},{5,3},{6,4},{7,5},{8,6},{9,7},{10,8},{11,9},{12,... | collective-permute-start | bytes 1204232 | tf_op jit(solution)/shard_map/ppermute | solution.py:894
  149.6 18.0 %collective-permute-start.13 = (f32[2,112,128]{2,1,0:T(8,128)S(1)}, f32[2,112,128]{2,1,0:T(8,128)S(1)}, u32[]{:S(2)}, u32[]{:S(2)}) collective-permute-start(f32[2,112,128]{2,1,0:T(8,128)S(1)} %slice_select_fusion.2), channel_id=1, source_target_pairs={{0,1},{1,0},{2,3},{3,2},{4,5},{5,4},{6,7},{7,6},{8,9},{9,8},{10,11... | collective-permute-start | bytes 344072 | tf_op jit(solution)/shard_map/ppermute | solution.py:905
  149.7 17.9 %all-to-all-start.3 = ((f32[32,4,128]{2,1,0:T(4,128)}), f32[32,4,128]{2,1,0:T(4,128)S(1)}, u32[]{:S(2)}, u32[]{:S(2)}) async-start(f32[32,4,128]{2,1,0:T(4,128)} %get-tuple-element.191), calls=%async_computation.3 | async-start | bytes 131072 | tf_op jit(solution)/shard_map/all_to_all | solution.py:868
  167.6 1.3 collective-permute-start.14
  201.4 13.4 %all-to-all-start.5 = ((f32[32,10,128]{2,1,0:T(8,128)}), f32[32,10,128]{2,1,0:T(8,128)S(1)}, u32[]{:S(2)}, u32[]{:S(2)}) async-start(f32[32,10,128]{2,1,0:T(8,128)} %get-tuple-element.199), calls=%async_computation.5 | async-start | bytes 524288 | tf_op jit(solution)/shard_map/all_to_all | solution.py:868
  232.8 15.5 %all-to-all-start.6 = ((f32[32,16,128]{2,1,0:T(8,128)}), f32[32,16,128]{2,1,0:T(8,128)S(1)}, u32[]{:S(2)}, u32[]{:S(2)}) async-start(f32[32,16,128]{2,1,0:T(8,128)} %get-tuple-element.203), calls=%async_computation.6 | async-start | bytes 524288 | tf_op jit(solution)/shard_map/all_to_all | solution.py:868
  271.1 20.1 %collective-permute-start.15 = (f32[2,392,128]{2,1,0:T(8,128)}, f32[2,392,128]{2,1,0:T(8,128)S(1)}, u32[]{:S(2)}, u32[]{:S(2)}) collective-permute-start(f32[2,392,128]{2,1,0:T(8,128)} %get-tuple-element.210), channel_id=1, source_target_pairs={{0,2},{1,3},{2,4},{3,5},{4,6},{5,7},{6,8},{7,9},{8,10},{9,11},{10,... | collective-permute-start | bytes 1204232 | tf_op jit(solution)/shard_map/ppermute | solution.py:894
  273.5 19.5 %collective-permute-start.16 = (f32[2,392,128]{2,1,0:T(8,128)}, f32[2,392,128]{2,1,0:T(8,128)S(1)}, u32[]{:S(2)}, u32[]{:S(2)}) collective-permute-start(f32[2,392,128]{2,1,0:T(8,128)} %get-tuple-element.211), channel_id=1, source_target_pairs={{2,0},{3,1},{4,2},{5,3},{6,4},{7,5},{8,6},{9,7},{10,8},{11,9},{12,... | collective-permute-start | bytes 1204232 | tf_op jit(solution)/shard_map/ppermute | solution.py:894
  275.8 17.4 %collective-permute-start.17 = (f32[2,112,128]{2,1,0:T(8,128)S(1)}, f32[2,112,128]{2,1,0:T(8,128)S(1)}, u32[]{:S(2)}, u32[]{:S(2)}) collective-permute-start(f32[2,112,128]{2,1,0:T(8,128)S(1)} %slice_select_fusion.1), channel_id=1, source_target_pairs={{0,1},{1,0},{2,3},{3,2},{4,5},{5,4},{6,7},{7,6},{8,9},{9,8},{10,11... | collective-permute-start | bytes 344072 | tf_op jit(solution)/shard_map/ppermute | solution.py:905
  293.0 1.3 collective-permute-start.18
  310.3 3.1 collective-permute-start.19
  310.5 11.1 %all-to-all-start.8 = ((f32[32,7,128]{2,1,0:T(8,128)}), f32[32,7,128]{2,1,0:T(8,128)S(1)}, u32[]{:S(2)}, u32[]{:S(2)}) async-start(f32[32,7,128]{2,1,0:T(8,128)} %get-tuple-element.229), calls=%async_computation.8 | async-start | bytes 262144 | tf_op jit(solution)/shard_map/all_to_all | solution.py:868
  321.6 26.8 %all-to-all-start.9 = ((f32[16,48,256]{2,1,0:T(8,128)}), f32[16,48,256]{2,1,0:T(8,128)S(1)}, u32[]{:S(2)}, u32[]{:S(2)}) async-start(f32[16,48,256]{2,1,0:T(8,128)} %add.22), calls=%async_computation.9 | async-start | bytes 1572864 | tf_op jit(solution)/shard_map/all_to_all | solution.py:926
  348.2 6.1 %collective-permute-start.20 = (f32[16,32,256]{2,1,0:T(8,128)}, f32[16,32,256]{2,1,0:T(8,128)S(1)}, u32[]{:S(2)}, u32[]{:S(2)}) collective-permute-start(f32[16,32,256]{2,1,0:T(8,128)} %get-tuple-element.237), channel_id=1, source_target_pairs={{0,1},{1,0},{2,3},{3,2},{4,5},{5,4},{6,7},{7,6},{8,9},{9,8},{10,11... | collective-permute-start | bytes 1572872 | tf_op jit(solution)/shard_map/ppermute | solution.py:922
  348.5 23.9 %copy-start = (f32[16,48,256]{2,1,0:T(8,128)}, f32[16,48,256]{2,1,0:T(8,128)S(1)}, u32[]{:S(2)}) copy-start(f32[16,48,256]{2,1,0:T(8,128)S(1)} %all-to-all-done.9.refs_2_) | copy-start | bytes 2359300
  348.5 16.5 %all-to-all-start.10 = ((f32[32,16,128]{2,1,0:T(8,128)}), f32[32,16,128]{2,1,0:T(8,128)S(1)}, u32[]{:S(2)}, u32[]{:S(2)}) async-start(f32[32,16,128]{2,1,0:T(8,128)} %get-tuple-element.240), calls=%async_computation.10 | async-start | bytes 524288 | tf_op jit(solution)/shard_map/all_to_all | solution.py:868
  383.1 50.2 %all-to-all-start.12 = ((f32[16,32,256]{2,1,0:T(8,128)}), f32[16,32,256]{2,1,0:T(8,128)S(1)}, u32[]{:S(2)}, u32[]{:S(2)}) async-start(f32[16,32,256]{2,1,0:T(8,128)} %add.23), calls=%async_computation.12 | async-start | bytes 1048576 | tf_op jit(solution)/shard_map/all_to_all | solution.py:926
  390.3 23.7 %collective-permute-start.21 = (f32[2,392,128]{2,1,0:T(8,128)}, f32[2,392,128]{2,1,0:T(8,128)S(1)}, u32[]{:S(2)}, u32[]{:S(2)}) collective-permute-start(f32[2,392,128]{2,1,0:T(8,128)} %get-tuple-element.245), channel_id=1, source_target_pairs={{0,2},{1,3},{2,4},{3,5},{4,6},{5,7},{6,8},{7,9},{8,10},{9,11},{10,... | collective-permute-start | bytes 1204232 | tf_op jit(solution)/shard_map/ppermute | solution.py:894
  394.0 21.8 %collective-permute-start.22 = (f32[2,392,128]{2,1,0:T(8,128)}, f32[2,392,128]{2,1,0:T(8,128)S(1)}, u32[]{:S(2)}, u32[]{:S(2)}) collective-permute-start(f32[2,392,128]{2,1,0:T(8,128)} %get-tuple-element.246), channel_id=1, source_target_pairs={{2,0},{3,1},{4,2},{5,3},{6,4},{7,5},{8,6},{9,7},{10,8},{11,9},{12,... | collective-permute-start | bytes 1204232 | tf_op jit(solution)/shard_map/ppermute | solution.py:894
  396.3 19.6 %collective-permute-start.23 = (f32[2,112,128]{2,1,0:T(8,128)S(1)}, f32[2,112,128]{2,1,0:T(8,128)S(1)}, u32[]{:S(2)}, u32[]{:S(2)}) collective-permute-start(f32[2,112,128]{2,1,0:T(8,128)S(1)} %slice_select_fusion), channel_id=1, source_target_pairs={{0,1},{1,0},{2,3},{3,2},{4,5},{5,4},{6,7},{7,6},{8,9},{9,8},{10,11... | collective-permute-start | bytes 344072 | tf_op jit(solution)/shard_map/ppermute | solution.py:905
  415.9 1.3 collective-permute-start.24
  433.0 4.7 collective-permute-start.25
  433.3 11.9 %copy-start.2 = (f32[16,32,256]{2,1,0:T(8,128)}, f32[16,32,256]{2,1,0:T(8,128)S(1)}, u32[]{:S(2)}) copy-start(f32[16,32,256]{2,1,0:T(8,128)S(1)} %all-to-all-done.12.refs_4_) | copy-start | bytes 1572868
  433.3 11.9 %all-to-all-start.13 = ((f32[32,4,128]{2,1,0:T(4,128)}), f32[32,4,128]{2,1,0:T(4,128)S(1)}, u32[]{:S(2)}, u32[]{:S(2)}) async-start(f32[32,4,128]{2,1,0:T(4,128)} %get-tuple-element.266), calls=%async_computation.13 | async-start | bytes 131072 | tf_op jit(solution)/shard_map/all_to_all | solution.py:868
  445.1 23.6 %all-to-all-start.14 = ((f32[16,48,256]{2,1,0:T(8,128)}), f32[16,48,256]{2,1,0:T(8,128)S(1)}, u32[]{:S(2)}, u32[]{:S(2)}) async-start(f32[16,48,256]{2,1,0:T(8,128)} %add.24), calls=%async_computation.14 | async-start | bytes 1572864 | tf_op jit(solution)/shard_map/all_to_all | solution.py:926
  457.3 16.7 %copy-start.9 = (f32[32,7,128]{2,1,0:T(8,128)S(1)}, f32[32,7,128]{2,1,0:T(8,128)}, u32[]{:S(2)}) copy-start(f32[32,7,128]{2,1,0:T(8,128)} %copy-done.8) | copy-start | bytes 344068
  457.3 2.2 collective-permute-start.26
  468.8 14.8 %copy-start.1 = (f32[16,48,256]{2,1,0:T(8,128)}, f32[16,48,256]{2,1,0:T(8,128)S(1)}, u32[]{:S(2)}) copy-start(f32[16,48,256]{2,1,0:T(8,128)S(1)} %all-to-all-done.14.refs_1_) | copy-start | bytes 2359300
  468.8 19.5 %all-to-all-start.15 = ((f32[16,32,256]{2,1,0:T(8,128)}), f32[16,32,256]{2,1,0:T(8,128)S(1)}, u32[]{:S(2)}, u32[]{:S(2)}) async-start(f32[16,32,256]{2,1,0:T(8,128)} %add.25), calls=%async_computation.15 | async-start | bytes 1048576 | tf_op jit(solution)/shard_map/all_to_all | solution.py:926
  (32 other events, 50.4 us)
Sparse Core Ops, SparseCore 0:
  10.9 74.9 all-gather.2
